TPU v7x, 256 devices: a whole 4x4x8 slice. The times are simulated.
256 devices in a mesh: seq: 16 (over z, core), tensor: 16 (over y, x).
Axes of the slice: x: 4, y: 4, z: 8, core: 2. Of those that a mesh axis runs over, the one named last changes fastest.
Arguments:
- tokens: bfloat16 [2, 2048, 3072], P(None, ('seq', 'tensor')), may hold values from -6 to 6
- qkv_weight: bfloat16 [48, 192, 3072], P('tensor'), may hold values from -0.109375 to 0.109375
- rate_weight: bfloat16 [48, 3072], P('tensor'), may hold values from -0.109375 to 0.109375
- base_rate: float32 [48], P('tensor'), may hold values from 0.003 to 0.03
- first_w: float32 [48, 64, 256], P('tensor'), may hold values from -0.75 to 0.75
- first_b: float32 [48, 256], P('tensor'), may hold values from -3 to 3
- second_w: float32 [48, 256, 64], P('tensor'), may hold values from -0.375 to 0.375
- second_b: float32 [48, 64], P('tensor'), may hold values from -3 to 3
- norm_gain: float32 [48, 64], P('tensor'), may hold values from 0.5 to 1.5
- norm_shift: float32 [48, 64], P('tensor'), may hold values from -3 to 3
- out_weight: bfloat16 [3072, 3072], P('tensor'), may hold values from -0.109375 to 0.109375
Outputs:
- mixed: bfloat16 [2, 2048, 3072], P(None, ('seq', 'tensor'))
All inputs are finite; a program needn't handle non-finite values.
Results may differ from a plain program's by a relative error of at most 0.019.
Values may be sent and summed in bfloat16 or wider, within the bound.
No kernel may reach another device: no remote copies, remote signals or barrier semaphores. Data moves between devices by JAX's collectives and lax.ppermute only.
A program may use at most 64 MiB of HBM per device.

v0:
```python
import jax
import jax.numpy as jnp
import numpy as np
from jax import lax
from jax.experimental import pallas as pl
from jax.experimental.pallas import tpu as pltpu
from jax.sharding import PartitionSpec as P


HEAD = 64
MB = 64
INNER = 256
F32 = jnp.float32
BF16 = jnp.bfloat16
C0 = 0.7978845608028654
C1 = 0.044715
NT = (((1,), (1,)), ((), ()))
TN = (((0,), (0,)), ((), ()))


def mm(a, b):
    return jnp.dot(a, b, preferred_element_type=F32)


def mm_nt(a, b):
    return lax.dot_general(a, b, NT, preferred_element_type=F32)


def mm_tn(a, b):
    return lax.dot_general(a, b, TN, preferred_element_type=F32)


def mean_last(value):
    return jnp.mean(value, axis=-1, keepdims=True)


def gelu_parts(u):
    square = u * u
    t = jnp.tanh(u * (C0 + (C0 * C1) * square))
    half = 0.5 * u
    return square, t, half


HOMES = ((0, 1, 2), (3, 2, 1))
GROUP = 4
SIDE = 4
ROWS = 2 * GROUP
PHASE, OWN, CORE, Y, SEAT = 0, 1, 2, 3, 4
GROUPS = [list(range(ROWS)), list(range(ROWS, 2 * ROWS))]


def seat(group, u, core):
    return 2 * (u if group == 0 else GROUP - 1 - u) + core


def routes():
    table = np.zeros((2 * ROWS, SIDE * SIDE, SEAT + 6), np.int32)
    table[:, :, Y] = np.arange(SIDE * SIDE)[None] // SIDE
    for group in range(2):
        for u in range(GROUP):
            for core in range(2):
                line = table[group * ROWS + seat(group, u, core)]
                line[:, PHASE], line[:, CORE] = group, core
                for seq in range(2):
                    for head, home in enumerate(HOMES[seq]):
                        line[:, SEAT + 3 * seq + head] = seat(group, home, seq)
                        if (home, seq) == (u, core):
                            line[:, OWN] = head
    return table.reshape(2 * ROWS * SIDE * SIDE, -1)


def from_side(value, turn, ahead):
    pairs = []
    for row in range(2 * ROWS):
        unit = 1 if (row + turn) % 2 == 0 else SIDE
        for place in range(SIDE * SIDE):
            at = place // unit % SIDE
            source = place + ((at + ahead) % SIDE - at) * unit
            pairs.append((row * SIDE * SIDE + source, row * SIDE * SIDE + place))
    return lax.ppermute(value, ("seq", "tensor"), pairs)


RELAY = [
    (seat(0, home, core), ROWS + seat(1, home, core))
    for core in range(2)
    for home in HOMES[core]
]


def in_vmem(count):
    return [pl.BlockSpec(memory_space=pltpu.VMEM)] * count


SCALARS = pl.BlockSpec(memory_space=pltpu.SMEM)


def fetch_kernel(after, weight_in, rate_weight_in, base_rate_in, *refs):
    arrived = refs[3]
    copies = [
        pltpu.make_async_copy(source, target, arrived.at[k])
        for k, (source, target) in enumerate(
            zip((weight_in, rate_weight_in, base_rate_in), refs[:3], strict=True)
        )
    ]
    for copy in copies:
        copy.start()
    for copy in copies:
        copy.wait()


def project_kernel(place, *refs):
    pieces = refs[: 2 * SIDE]
    weight, rate_weight, base_rate, pairs, queries, by_place = refs[2 * SIDE :]
    rows = jnp.concatenate([piece[...].reshape(32, piece.shape[2]) for piece in pieces], axis=0)
    logit = mm_nt(rows, rate_weight[...])
    rates = base_rate[...] * jax.nn.sigmoid(logit)
    lane = lax.broadcasted_iota(jnp.int32, (256, HEAD), 1)
    for head in range(3):
        parts = [weight[head, spot * HEAD : (spot + 1) * HEAD, :] for spot in (1, 2, 0)]
        value = mm_nt(rows, jnp.concatenate(parts, axis=0))
        rate = rates[:, head : head + 1]
        high = rate.astype(BF16).astype(F32)
        tail = jnp.where(lane == 0, high, jnp.where(lane == 1, rate - high, 0.0))
        value = jnp.concatenate([value, tail], axis=1).reshape(SIDE, SIDE, 2, 8, 256)
        for k in range(SIDE):
            y = lax.rem(place[Y] + k, SIDE)
            for seq in range(2):
                by_place[seq, y] = jnp.where(
                    place[CORE] == 0, value[k, :, seq], value[:, k, seq]
                )
        for seq in range(2):
            target = place[SEAT + 3 * seq + head]
            block = by_place[seq].reshape(2 * MB, 256)
            pairs[target, 0 : 2 * MB] = block[:, 0 : 2 * HEAD].astype(BF16)
            flipped = block[:, 2 * HEAD :].T
            pairs[target, 2 * MB :] = flipped[HEAD : HEAD + 16].astype(BF16)
            for part in range(2):
                queries[target, :, part * HEAD : (part + 1) * HEAD] = block[
                    part * MB : (part + 1) * MB, 2 * HEAD : 3 * HEAD
                ].astype(BF16)


def answer(q, w1b, c1, w2tb, c2, gain, shift):
    _, t, half = gelu_parts(mm(q, w1b) + c1)
    hidden = (half + half * t).astype(BF16)
    outer = mm_nt(hidden, w2tb) + c2
    m = mean_last(outer)
    s = lax.rsqrt(mean_last(outer * outer) - m * m + 1e-6)
    return (q.astype(F32) + (gain * ((outer - m) * s) + shift)).astype(BF16)


def advance(pairs, w1, c1, w2t, c2, gain, shift, visit):
    gain2 = gain * gain
    g_mean = mean_last(gain2)
    line = lax.broadcasted_iota(jnp.int32, (16, HEAD), 0)
    rate_sum = jnp.where(line < 2, 1.0, 0.0).astype(BF16)

    def step(state, here, part, kn, row, last):
        w1, c1, w2t, c2, pre = state
        spot = slice(part * MB, (part + 1) * MB)
        k, v = here[spot, 0:HEAD], here[spot, HEAD : 2 * HEAD]
        w1b = w1.astype(BF16)
        w2tb = w2t.astype(BF16)
        r = mm_tn(here[2 * MB :, spot], rate_sum)
        gram = (mm_nt(kn, k) + 1.0).astype(BF16)
        n_pre = mm(kn, w1b) + c1
        visit(row, last, w1b, c1, w2tb, c2)
        target = gain * (shift - (v.astype(F32) - k.astype(F32)))
        t_mean = mean_last(target)

        square, t, half = gelu_parts(pre)
        hidden = (half + half * t).astype(BF16)
        slope = 0.5 + 0.5 * t + half * (1.0 - t * t) * (C0 + (3.0 * C0 * C1) * square)
        outer = mm_nt(hidden, w2tb) + c2
        sq = outer * outer
        m = mean_last(outer)
        s2 = mean_last(sq)
        s3 = mean_last(gain2 * outer)
        s4 = mean_last(gain2 * sq)
        s5 = mean_last(target * outer)
        s = lax.rsqrt(s2 - m * m + 1e-6)
        mu = s * (s3 - m * g_mean) + t_mean
        mn = s * s * (s4 - 2.0 * m * s3 + m * m * g_mean) + s * (s5 - m * t_mean)
        normed = (outer - m) * s
        w_outer = (r * s) * ((gain2 - mn) * normed + (target - mu))
        scaled = w_outer.astype(BF16)
        w_inner = mm(scaled, w2tb) * slope
        inner = w_inner.astype(BF16)
        return (
            w1 - mm_tn(k, inner),
            c1 - jnp.sum(w_inner, axis=0, keepdims=True),
            w2t - mm_tn(scaled, hidden),
            c2 - jnp.sum(w_outer, axis=0, keepdims=True),
            n_pre - mm(gram, inner),
        )

    def two_steps(row, state):
        before, after = jnp.maximum(row - 1, 0), jnp.minimum(row + 1, ROWS - 1)
        here = pairs.at[row]
        state = step(state, here, 0, here[MB : 2 * MB, 0:HEAD], before, 1)
        return step(state, here, 1, pairs[after, 0:MB, 0:HEAD], row, 0)

    pre = mm(pairs[0, 0:MB, 0:HEAD], w1.astype(BF16)) + c1
    w1, c1, w2t, c2, pre = lax.fori_loop(0, ROWS, two_steps, (w1, c1, w2t, c2, pre))
    visit(ROWS - 1, 1, w1.astype(BF16), c1, w2t.astype(BF16), c2)
    return w1, c1, w2t, c2


def first_kernel(
    place, pairs, w1_in, c1_in, w2t_in, c2_in, gain_in, shift_in, state, weights, biases
):
    @pl.when(place[PHASE] == 0)
    def _():
        own = pl.ds(place[OWN], 1)
        w2t, c2 = w2t_in[place[OWN]], c2_in[own]
        w2t = w2t - jnp.mean(w2t, axis=0, keepdims=True)
        c2 = c2 - mean_last(c2)

        def keep(row, part, w1b, c1, w2tb, c2):
            weights[row, part, 0:HEAD] = w1b
            weights[row, part, HEAD : 2 * HEAD] = w2tb
            biases[row, part, 0:1] = c1
            biases[row, part, 1:2, 0:HEAD] = c2

        w1, c1, w2t, c2 = advance(
            pairs, w1_in[place[OWN]], c1_in[own], w2t, c2, gain_in[own], shift_in[own], keep
        )
        state[0:64] = w1.astype(BF16)
        state[64:128] = w2t.astype(BF16)
        line = lax.broadcasted_iota(jnp.int32, (16, INNER), 0)
        c1_high = c1.astype(BF16).astype(F32)
        c2 = jnp.concatenate([c2] * 4, axis=1)
        c2_high = c2.astype(BF16).astype(F32)
        low = jnp.where(line == 2, c2_high, c2 - c2_high)
        low = jnp.where(line == 1, c1 - c1_high, low)
        state[128:144] = jnp.where(line == 0, c1_high, low).astype(BF16)


def second_kernel(place, pairs, queries, state, gain_in, shift_in, weights, biases, out):
    own = pl.ds(place[OWN], 1)
    gain, shift = gain_in[own], shift_in[own]

    def put(row, part, w1b, c1, w2tb, c2):
        span = slice(part * HEAD, (part + 1) * HEAD)
        out[row, :, span] = answer(queries[row, :, span], w1b, c1, w2tb, c2, gain, shift)

    @pl.when(place[PHASE] == 0)
    def _():
        def both(row, unused):
            for part in range(2):
                kept = weights.at[row, part]
                bias = biases.at[row, part]
                put(row, part, kept[0:HEAD], bias[0:1], kept[HEAD:], bias[1:2, 0:HEAD])
            return unused

        lax.fori_loop(0, ROWS, both, 0)

    @pl.when(place[PHASE] == 1)
    def _():
        bias = state[128:144].astype(F32)
        advance(
            pairs,
            state[0:64].astype(F32),
            bias[0:1] + bias[1:2],
            state[64:128].astype(F32),
            (bias[2:3] + bias[3:4])[:, 0:HEAD],
            gain,
            shift,
            put,
        )


def mix_kernel(place, answers, weight, *refs):
    outs, by_place = refs[: 2 * SIDE], refs[2 * SIDE]
    width = weight.shape[1]
    for seq in range(2):
        heads = [answers[place[SEAT + 3 * seq + head]].astype(F32) for head in range(3)]
        for half in range(2):
            rows = [both[:, half * HEAD : (half + 1) * HEAD] for both in heads]
            rows = jnp.concatenate(rows, axis=1).reshape(2, SIDE, 8, 3 * HEAD)
            by_place[seq, 2 * half : 2 * half + 2] = rows
    turns = [
        [by_place[seq, lax.rem(place[Y] + k, SIDE)] for seq in range(2)] for k in range(SIDE)
    ]
    for k in range(SIDE):
        first = jnp.stack(turns[k], axis=1)
        second = jnp.stack(
            [jnp.stack([turn[seq][k] for seq in range(2)]) for turn in turns]
        )
        rows = jnp.where(place[CORE] == 0, first, second).reshape(64, 3 * HEAD)
        total = mm(rows.astype(BF16), weight[...]).astype(BF16)
        outs[2 * k][...] = total[0:32].reshape(2, 16, width)
        outs[2 * k + 1][...] = total[32:64].reshape(2, 16, width)


def pair_kernel(left, right, out):
    out[...] = (left[...].astype(F32) + right[...].astype(F32)).astype(BF16)


def line_kernel(*refs):
    for half in range(2):
        parts = refs[half : 6 : 2]
        total = sum(part[...].astype(F32) for part in parts).astype(BF16)
        refs[6 + 2 * half][...] = total[0]
        refs[7 + 2 * half][...] = total[1]


def last_kernel(*refs):
    total = sum(part[...].astype(F32) for part in refs[:SIDE])
    refs[SIDE][...] = total.astype(BF16)


def kernel_call(kernel, out_shape, count, scalars=1, scratch=()):
    many = isinstance(out_shape, tuple)
    return pl.pallas_call(
        kernel,
        out_shape=out_shape,
        in_specs=[SCALARS] * scalars + in_vmem(count),
        out_specs=in_vmem(len(out_shape)) if many else in_vmem(1)[0],
        scratch_shapes=scratch,
        compiler_params=pltpu.CompilerParams(vmem_limit_bytes=24 << 20),
    )


def exchange(value):
    return lax.all_to_all(value, "seq", 0, 0, axis_index_groups=GROUPS, tiled=True)


def shards(
    tokens,
    qkv_weight,
    rate_weight,
    base_rate,
    first_w,
    first_b,
    second_w,
    second_b,
    norm_gain,
    norm_shift,
    out_weight,
):
    seqs, own_rows, width = tokens.shape
    place = jnp.asarray(routes())[lax.axis_index(("seq", "tensor"))]
    tokens, place = lax.optimization_barrier((tokens, place))
    own = tokens.reshape(seqs * own_rows, width)
    one, three, two = (from_side(own, 0, ahead) for ahead in (1, 3, 2))
    low, high = jnp.stack([own, one]), jnp.stack([two, three])
    low_one, low_three = from_side(low, 1, 1), from_side(low, 1, 3)
    high_three, high_one = from_side(high, 1, 3), from_side(high, 1, 1)
    low_two, high_two = from_side(low_one, 1, 1), from_side(high_three, 1, 3)
    in_hbm = pl.BlockSpec(memory_space=pltpu.HBM)
    sources = tuple(
        pltpu.with_memory_space_constraint(value, pltpu.HBM)
        for value in (qkv_weight, rate_weight, base_rate[None])
    )
    fetched = pl.pallas_call(
        fetch_kernel,
        out_shape=tuple(jax.ShapeDtypeStruct(value.shape, value.dtype) for value in sources),
        in_specs=[pl.BlockSpec(memory_space=pl.ANY)] + [in_hbm] * 3,
        out_specs=in_vmem(3),
        scratch_shapes=[pltpu.SemaphoreType.DMA((3,))],
        compiler_params=pltpu.CompilerParams(vmem_limit_bytes=24 << 20),
        cost_estimate=pl.CostEstimate(flops=0, bytes_accessed=4 << 20, transcendentals=0),
        name="fetch",
    )(high, *sources)
    pieces = (low, high, low_one, high_one, low_two, high_two, low_three, high_three)
    answer_shape = jax.ShapeDtypeStruct((ROWS, MB, 2 * HEAD), BF16)
    pairs, queries = kernel_call(
        project_kernel,
        (jax.ShapeDtypeStruct((ROWS, 2 * MB + 16, 2 * HEAD), BF16), answer_shape),
        2 * SIDE + 3,
        scratch=[pltpu.VMEM((2, SIDE, SIDE, 8, 256), F32)],
    )(place, *pieces, *fetched)
    pairs = exchange(pairs)
    state, weights, biases = kernel_call(
        first_kernel,
        (
            jax.ShapeDtypeStruct((144, INNER), BF16),
            jax.ShapeDtypeStruct((ROWS, 2, 2 * HEAD, INNER), BF16),
            jax.ShapeDtypeStruct((ROWS, 2, 8, INNER), F32),
        ),
        7,
    )(
        place,
        pairs,
        first_w,
        first_b,
        jnp.swapaxes(second_w, 1, 2),
        second_b,
        norm_gain,
        norm_shift,
    )
    state = lax.ppermute(state, "seq", RELAY)
    queries, biases = lax.optimization_barrier((queries, biases))
    queries = exchange(queries)
    answers = kernel_call(second_kernel, answer_shape, 7)(
        place, pairs, queries, state, norm_gain, norm_shift, weights, biases
    )
    pair = jax.ShapeDtypeStruct((2, 16, width), BF16)
    single = jax.ShapeDtypeStruct((16, width), BF16)
    parts = kernel_call(
        mix_kernel,
        (pair,) * (2 * SIDE),
        2,
        scratch=[pltpu.VMEM((2, SIDE, SIDE, 8, 3 * HEAD), F32)],
    )(place, exchange(answers), out_weight)
    low, high, low_one, high_one, low_two, high_two, low_three, high_three = parts
    add = kernel_call(pair_kernel, pair, 2, 0)
    passing_one, passing_three = from_side(low_two, 1, 3), from_side(high_two, 1, 1)
    high_one, low_three = from_side(high_one, 1, 3), from_side(low_three, 1, 1)
    low_one = from_side(add(low_one, passing_one), 1, 3)
    high_three = from_side(add(high_three, passing_three), 1, 1)
    line = kernel_call(line_kernel, (single,) * SIDE, 6, 0)(
        low, high, low_one, high_one, low_three, high_three
    )
    far = [from_side(line[k], 0, SIDE - k) for k in (1, 3, 2)]
    mixed = kernel_call(last_kernel, single, SIDE, 0)(line[0], *far)
    return mixed.reshape(seqs, own_rows, width)


def solution(mesh):
    in_specs = (
        P(None, ("seq", "tensor"), None),
        P("tensor", None, None),
        P("tensor", None),
        P("tensor"),
        P("tensor", None, None),
        P("tensor", None),
        P("tensor", None, None),
        P("tensor", None),
        P("tensor", None),
        P("tensor", None),
        P("tensor", None),
    )
    out_specs = P(None, ("seq", "tensor"), None)
    return jax.shard_map(
        shards, mesh=mesh, in_specs=in_specs, out_specs=out_specs, check_vma=False
    )
```

profile of v0, /device:TPU:152, one launch (start us, length us, event | category | flops | bytes accessed | tf_op | source)
XLA Modules:
  0.0 108.4 jit_solution(13432595816348791737)
XLA Ops:
  0.0 0.7 dynamic-slice_bitcast_fusion.place
  0.7 2.8 %collective-permute-start = (bf16[16,3072]{1,0:T(8,128)(2,1)}, bf16[16,3072]{1,0:T(8,128)(2,1)S(1)}, u32[]{:S(2)}, u32[]{:S(2)}) collective-permute-start(bf16[16,3072]{1,0:T(8,128)(2,1)} %bitcast.11), channel_id=1, source_target_pairs={{1,0},{2,1},{3,2},{0,3},{5,4},{6,5},{7,6},{4,7},{9,8},{10,9},{11,1... | collective-permute-start | bytes 294920 | tf_op jit(solution)/shard_map/ppermute | solution.py:80
  3.5 2.3 %collective-permute-start.1 = (bf16[16,3072]{1,0:T(8,128)(2,1)}, bf16[16,3072]{1,0:T(8,128)(2,1)S(1)}, u32[]{:S(2)}, u32[]{:S(2)}) collective-permute-start(bf16[16,3072]{1,0:T(8,128)(2,1)} %bitcast.13), channel_id=1, source_target_pairs={{2,0},{3,1},{0,2},{1,3},{6,4},{7,5},{4,6},{5,7},{10,8},{11,9},{8,1... | collective-permute-start | bytes 294920 | tf_op jit(solution)/shard_map/ppermute | solution.py:80
  6.0 0.9 pad_maximum_fusion.refs_0_
  6.9 0.8 collective-permute-start.3
  7.7 2.8 %collective-permute-done.2 = bf16[16,3072]{1,0:T(8,128)(2,1)S(1)} collective-permute-done((bf16[16,3072]{1,0:T(8,128)(2,1)}, bf16[16,3072]{1,0:T(8,128)(2,1)S(1)}, u32[]{:S(2)}, u32[]{:S(2)}) %collective-permute-start.2) | collective-permute-done | bytes 98336 | tf_op jit(solution)/shard_map/ppermute | solution.py:80
  10.9 1.6 %collective-permute-start.8 = (bf16[2,16,3072]{2,1,0:T(8,128)(2,1)S(1)}, bf16[2,16,3072]{2,1,0:T(8,128)(2,1)S(1)}, u32[]{:S(2)}, u32[]{:S(2)}) collective-permute-start(bf16[2,16,3072]{2,1,0:T(8,128)(2,1)S(1)} %pad_maximum_fusion.refs_0_), channel_id=1, source_target_pairs={{12,0},{13,1},{14,2},{15,3},{0,4},{1,5},{2,6},{3,7},{4,8},{5,9},{6... | collective-permute-start | bytes 589832 | tf_op jit(solution)/shard_map/ppermute | solution.py:80
  12.9 1.0 collective-permute-done.3.refs_2_
  13.9 0.9 collective-permute-start.5
  14.7 1.6 %collective-permute-done.6.refs_7_ = bf16[2,16,3072]{2,1,0:T(8,128)(2,1)S(1)} collective-permute-done((bf16[2,16,3072]{2,1,0:T(8,128)(2,1)S(1)}, bf16[2,16,3072]{2,1,0:T(8,128)(2,1)S(1)}, u32[]{:S(2)}, u32[]{:S(2)}) %collective-permute-start.6) | collective-permute-done | bytes 196640 | tf_op jit(solution)/shard_map/ppermute | solution.py:80
  16.3 1.4 %collective-permute-start.7 = (bf16[2,16,3072]{2,1,0:T(8,128)(2,1)S(1)}, bf16[2,16,3072]{2,1,0:T(8,128)(2,1)S(1)}, u32[]{:S(2)}, u32[]{:S(2)}) collective-permute-start(bf16[2,16,3072]{2,1,0:T(8,128)(2,1)S(1)} %collective-permute-done.6.refs_7_), channel_id=1, source_target_pairs={{12,0},{13,1},{14,2},{15,3},{0,4},{1,5},{2,6},{3,7},{4,8},{5,9},{6... | collective-permute-start | bytes 589832 | tf_op jit(solution)/shard_map/ppermute | solution.py:80
  17.8 2.0 %fetch.1 = (bf16[3,192,3072]{2,1,0:T(8,128)(2,1)S(1)}, bf16[3,3072]{1,0:T(4,128)(2,1)S(1)}, f32[1,3]{1,0:T(1,128)S(1)}) custom-call(bf16[2,16,3072]{2,1,0:T(8,128)(2,1)S(1)} %pad_maximum_fusion.1.after.refs_1_, bf16[3,192,3072]{2,1,0:T(8,128)(2,1)} %weight_in.1, bf16[3,3072]{1,0:T(4,128)(2,1)} %rate_weight_in.1, f32[1,3]{1,0:T(1,128)} %bitcast.18), custom_call_target="tpu_custom_call" | custom-call | bytes 4194304 | tf_op jit(solution)/shard_map/fetch/pallas_call | solution.py:356
  19.9 1.6 %collective-permute-done.5.refs_4_ = bf16[2,16,3072]{2,1,0:T(8,128)(2,1)S(1)} collective-permute-done((bf16[2,16,3072]{2,1,0:T(8,128)(2,1)S(1)}, bf16[2,16,3072]{2,1,0:T(8,128)(2,1)S(1)}, u32[]{:S(2)}, u32[]{:S(2)}) %collective-permute-start.5) | collective-permute-done | bytes 196640 | tf_op jit(solution)/shard_map/ppermute | solution.py:80
  22.0 3.1 %shard_map.118 = (bf16[8,144,128]{2,1,0:T(8,128)(2,1)S(1)}, bf16[8,64,128]{2,1,0:T(8,128)(2,1)}) custom-call(s32[10]{0:T(128)S(1)} %dynamic-slice_bitcast_fusion.place, bf16[2,16,3072]{2,1,0:T(8,128)(2,1)S(1)} %pad_maximum_fusion.refs_0_, bf16[2,16,3072]{2,1,0:T(8,128)(2,1)S(1)} %pad_maximum_fusion.1.after.refs_1_, ...), custom_call_target="tpu_custom_call" | custom-call | tf_op jit(solution)/shard_map/pallas_call | solution.py:368
  25.1 13.4 %all_to_all.15.pairs = bf16[8,144,128]{2,1,0:T(8,128)(2,1)S(1)} all-to-all(bf16[8,144,128]{2,1,0:T(8,128)(2,1)S(1)} %get-tuple-element.34), channel_id=1, replica_groups={{0,16,32,48,64,80,96,112},{128,144,160,176,192,208,224,240},{1,17,33,49..., dimensions={0} | all-to-all | bytes 589824 | tf_op jit(solution)/shard_map/all_to_all | solution.py:326
  39.1 3.4 %all-to-all-start.1 = ((bf16[8,64,128]{2,1,0:T(8,128)(2,1)}), bf16[8,64,128]{2,1,0:T(8,128)(2,1)S(1)}, u32[]{:S(2)}, u32[]{:S(2)}) async-start(bf16[8,64,128]{2,1,0:T(8,128)(2,1)} %get-tuple-element.37), calls=%async_computation.1 | async-start | bytes 262144 | tf_op jit(solution)/shard_map/all_to_all | solution.py:326
  42.5 0.7 collective-permute-start.9
  43.2 6.0 %all-to-all-done.1.queries = bf16[8,64,128]{2,1,0:T(8,128)(2,1)S(1)} async-done(((bf16[8,64,128]{2,1,0:T(8,128)(2,1)}), bf16[8,64,128]{2,1,0:T(8,128)(2,1)S(1)}, u32[]{:S(2)}, u32[]{:S(2)}) %all-to-all-start.1) | async-done | bytes 131104 | tf_op jit(solution)/shard_map/all_to_all | solution.py:326
  49.2 11.3 %shard_map.120 = bf16[8,64,128]{2,1,0:T(8,128)(2,1)S(1)} custom-call(s32[10]{0:T(128)S(1)} %dynamic-slice_bitcast_fusion.place, bf16[8,144,128]{2,1,0:T(8,128)(2,1)S(1)} %all_to_all.15.pairs, bf16[8,64,128]{2,1,0:T(8,128)(2,1)S(1)} %all-to-all-done.1.queries, bf16[144,256]{1,0:T(8,128)(2,1)S(1)} %collective-permute-done.9.state, f32[3,64]{1,0:T(4,128)S(1)} %copy-done.3, ...), custom_call_target="tpu_custom_call" | custom-call | tf_op jit(solution)/shard_map/pallas_call | solution.py:396
  60.5 18.7 %all_to_all.16.answers = bf16[8,64,128]{2,1,0:T(8,128)(2,1)S(1)} all-to-all(bf16[8,64,128]{2,1,0:T(8,128)(2,1)S(1)} %shard_map.120), channel_id=1, replica_groups={{0,16,32,48,64,80,96,112},{128,144,160,176,192,208,224,240},{1,17,33,49..., dimensions={0} | all-to-all | bytes 262144 | tf_op jit(solution)/shard_map/all_to_all | solution.py:326
  79.2 1.6 %shard_map.121 = (bf16[2,16,3072]{2,1,0:T(8,128)(2,1)S(1)}, bf16[2,16,3072]{2,1,0:T(8,128)(2,1)S(1)}, bf16[2,16,3072]{2,1,0:T(8,128)(2,1)S(1)}, bf16[2,16,3072]{...) custom-call(s32[10]{0:T(128)S(1)} %dynamic-slice_bitcast_fusion.plac, ...), custom_call_target="tpu_custom_call" | custom-call | tf_op jit(solution)/shard_map/pallas_call | solution.py:401
  80.8 2.9 %collective-permute-start.10 = (bf16[2,16,3072]{2,1,0:T(8,128)(2,1)S(1)}, bf16[2,16,3072]{2,1,0:T(8,128)(2,1)S(1)}, u32[]{:S(2)}, u32[]{:S(2)}) collective-permute-start(bf16[2,16,3072]{2,1,0:T(8,128)(2,1)S(1)} %get-tuple-element.44), channel_id=1, source_target_pairs={{12,0},{13,1},{14,2},{15,3},{0,4},{1,5},{2,6},{3,7},{4,8},{5,9},{6... | collective-permute-start | bytes 589832 | tf_op jit(solution)/shard_map/ppermute | solution.py:80
  83.7 3.2 %collective-permute-start.12 = (bf16[2,16,3072]{2,1,0:T(8,128)(2,1)S(1)}, bf16[2,16,3072]{2,1,0:T(8,128)(2,1)S(1)}, u32[]{:S(2)}, u32[]{:S(2)}) collective-permute-start(bf16[2,16,3072]{2,1,0:T(8,128)(2,1)S(1)} %get-tuple-element.45), channel_id=1, source_target_pairs={{12,0},{13,1},{14,2},{15,3},{0,4},{1,5},{2,6},{3,7},{4,8},{5,9},{6... | collective-permute-start | bytes 589832 | tf_op jit(solution)/shard_map/ppermute | solution.py:80
  87.0 3.7 %collective-permute-start.11 = (bf16[2,16,3072]{2,1,0:T(8,128)(2,1)S(1)}, bf16[2,16,3072]{2,1,0:T(8,128)(2,1)S(1)}, u32[]{:S(2)}, u32[]{:S(2)}) collective-permute-start(bf16[2,16,3072]{2,1,0:T(8,128)(2,1)S(1)} %shard_map.122), channel_id=1, source_target_pairs={{12,0},{13,1},{14,2},{15,3},{0,4},{1,5},{2,6},{3,7},{4,8},{5,9},{6... | collective-permute-start | bytes 589832 | tf_op jit(solution)/shard_map/ppermute | solution.py:80
  90.9 3.0 %collective-permute-done.13.refs_4_ = bf16[2,16,3072]{2,1,0:T(8,128)(2,1)S(1)} collective-permute-done((bf16[2,16,3072]{2,1,0:T(8,128)(2,1)S(1)}, bf16[2,16,3072]{2,1,0:T(8,128)(2,1)S(1)}, u32[]{:S(2)}, u32[]{:S(2)}) %collective-permute-start.13) | collective-permute-done | bytes 196640 | tf_op jit(solution)/shard_map/ppermute | solution.py:80
  93.9 3.8 %collective-permute-done.15.refs_5_ = bf16[2,16,3072]{2,1,0:T(8,128)(2,1)S(1)} collective-permute-done((bf16[2,16,3072]{2,1,0:T(8,128)(2,1)S(1)}, bf16[2,16,3072]{2,1,0:T(8,128)(2,1)S(1)}, u32[]{:S(2)}, u32[]{:S(2)}) %collective-permute-start.15) | collective-permute-done | bytes 196640 | tf_op jit(solution)/shard_map/ppermute | solution.py:80
  97.9 1.1 %collective-permute-start.16 = (bf16[16,3072]{1,0:T(8,128)(2,1)S(1)}, bf16[16,3072]{1,0:T(8,128)(2,1)S(1)}, u32[]{:S(2)}, u32[]{:S(2)}) collective-permute-start(bf16[16,3072]{1,0:T(8,128)(2,1)S(1)} %get-tuple-element.50), channel_id=1, source_target_pairs={{3,0},{0,1},{1,2},{2,3},{7,4},{4,5},{5,6},{6,7},{11,8},{8,9},{9,10... | collective-permute-start | bytes 294920 | tf_op jit(solution)/shard_map/ppermute | solution.py:80
  99.0 2.6 %collective-permute-start.17 = (bf16[16,3072]{1,0:T(8,128)(2,1)S(1)}, bf16[16,3072]{1,0:T(8,128)(2,1)S(1)}, u32[]{:S(2)}, u32[]{:S(2)}) collective-permute-start(bf16[16,3072]{1,0:T(8,128)(2,1)S(1)} %get-tuple-element.51), channel_id=1, source_target_pairs={{1,0},{2,1},{3,2},{0,3},{5,4},{6,5},{7,6},{4,7},{9,8},{10,9},{11,1... | collective-permute-start | bytes 294920 | tf_op jit(solution)/shard_map/ppermute | solution.py:80
  101.6 1.4 %collective-permute-start.18 = (bf16[16,3072]{1,0:T(8,128)(2,1)S(1)}, bf16[16,3072]{1,0:T(8,128)(2,1)S(1)}, u32[]{:S(2)}, u32[]{:S(2)}) collective-permute-start(bf16[16,3072]{1,0:T(8,128)(2,1)S(1)} %get-tuple-element.52), channel_id=1, source_target_pairs={{2,0},{3,1},{0,2},{1,3},{6,4},{7,5},{4,6},{5,7},{10,8},{11,9},{8,1... | collective-permute-start | bytes 294920 | tf_op jit(solution)/shard_map/ppermute | solution.py:80
  103.0 1.1 %collective-permute-done.16.refs_1_ = bf16[16,3072]{1,0:T(8,128)(2,1)S(1)} collective-permute-done((bf16[16,3072]{1,0:T(8,128)(2,1)S(1)}, bf16[16,3072]{1,0:T(8,128)(2,1)S(1)}, u32[]{:S(2)}, u32[]{:S(2)}) %collective-permute-start.16) | collective-permute-done | bytes 98336 | tf_op jit(solution)/shard_map/ppermute | solution.py:80
  104.1 3.6 %collective-permute-done.18.refs_3_ = bf16[16,3072]{1,0:T(8,128)(2,1)S(1)} collective-permute-done((bf16[16,3072]{1,0:T(8,128)(2,1)S(1)}, bf16[16,3072]{1,0:T(8,128)(2,1)S(1)}, u32[]{:S(2)}, u32[]{:S(2)}) %collective-permute-start.18) | collective-permute-done | bytes 98336 | tf_op jit(solution)/shard_map/ppermute | solution.py:80
  107.7 0.7 shard_map.125
  (36 shorter events, 2.6 us)
Async XLA Ops:
  0.7 5.3 %collective-permute-start = (bf16[16,3072]{1,0:T(8,128)(2,1)}, bf16[16,3072]{1,0:T(8,128)(2,1)S(1)}, u32[]{:S(2)}, u32[]{:S(2)}) collective-permute-start(bf16[16,3072]{1,0:T(8,128)(2,1)} %bitcast.11), channel_id=1, source_target_pairs={{1,0},{2,1},{3,2},{0,3},{5,4},{6,5},{7,6},{4,7},{9,8},{10,9},{11,1... | collective-permute-start | bytes 294920 | tf_op jit(solution)/shard_map/ppermute | solution.py:80
  3.5 7.1 %collective-permute-start.2 = (bf16[16,3072]{1,0:T(8,128)(2,1)}, bf16[16,3072]{1,0:T(8,128)(2,1)S(1)}, u32[]{:S(2)}, u32[]{:S(2)}) collective-permute-start(bf16[16,3072]{1,0:T(8,128)(2,1)} %bitcast.12), channel_id=1, source_target_pairs={{3,0},{0,1},{1,2},{2,3},{7,4},{4,5},{5,6},{6,7},{11,8},{8,9},{9,10... | collective-permute-start | bytes 294920 | tf_op jit(solution)/shard_map/ppermute | solution.py:80
  3.5 7.1 %collective-permute-start.1 = (bf16[16,3072]{1,0:T(8,128)(2,1)}, bf16[16,3072]{1,0:T(8,128)(2,1)S(1)}, u32[]{:S(2)}, u32[]{:S(2)}) collective-permute-start(bf16[16,3072]{1,0:T(8,128)(2,1)} %bitcast.13), channel_id=1, source_target_pairs={{2,0},{3,1},{0,2},{1,3},{6,4},{7,5},{4,6},{5,7},{10,8},{11,9},{8,1... | collective-permute-start | bytes 294920 | tf_op jit(solution)/shard_map/ppermute | solution.py:80
  6.9 7.0 %collective-permute-start.3 = (bf16[2,16,3072]{2,1,0:T(8,128)(2,1)S(1)}, bf16[2,16,3072]{2,1,0:T(8,128)(2,1)S(1)}, u32[]{:S(2)}, u32[]{:S(2)}) collective-permute-start(bf16[2,16,3072]{2,1,0:T(8,128)(2,1)S(1)} %pad_maximum_fusion.refs_0_), channel_id=1, source_target_pairs={{4,0},{5,1},{6,2},{7,3},{8,4},{9,5},{10,6},{11,7},{12,8},{13,9},{1... | collective-permute-start | bytes 589832 | tf_op jit(solution)/shard_map/ppermute | solution.py:80
  10.6 5.7 %collective-permute-start.6 = (bf16[2,16,3072]{2,1,0:T(8,128)(2,1)S(1)}, bf16[2,16,3072]{2,1,0:T(8,128)(2,1)S(1)}, u32[]{:S(2)}, u32[]{:S(2)}) collective-permute-start(bf16[2,16,3072]{2,1,0:T(8,128)(2,1)S(1)} %pad_maximum_fusion.1.after.refs_1_), channel_id=1, source_target_pairs={{12,0},{13,1},{14,2},{15,3},{0,4},{1,5},{2,6},{3,7},{4,8},{5,9},{6... | collective-permute-start | bytes 589832 | tf_op jit(solution)/shard_map/ppermute | solution.py:80
  10.9 9.0 %collective-permute-start.8 = (bf16[2,16,3072]{2,1,0:T(8,128)(2,1)S(1)}, bf16[2,16,3072]{2,1,0:T(8,128)(2,1)S(1)}, u32[]{:S(2)}, u32[]{:S(2)}) collective-permute-start(bf16[2,16,3072]{2,1,0:T(8,128)(2,1)S(1)} %pad_maximum_fusion.refs_0_), channel_id=1, source_target_pairs={{12,0},{13,1},{14,2},{15,3},{0,4},{1,5},{2,6},{3,7},{4,8},{5,9},{6... | collective-permute-start | bytes 589832 | tf_op jit(solution)/shard_map/ppermute | solution.py:80
  12.4 7.4 %collective-permute-start.4 = (bf16[2,16,3072]{2,1,0:T(8,128)(2,1)S(1)}, bf16[2,16,3072]{2,1,0:T(8,128)(2,1)S(1)}, u32[]{:S(2)}, u32[]{:S(2)}) collective-permute-start(bf16[2,16,3072]{2,1,0:T(8,128)(2,1)S(1)} %pad_maximum_fusion.1.after.refs_1_), channel_id=1, source_target_pairs={{4,0},{5,1},{6,2},{7,3},{8,4},{9,5},{10,6},{11,7},{12,8},{13,9},{1... | collective-permute-start | bytes 589832 | tf_op jit(solution)/shard_map/ppermute | solution.py:80
  13.9 7.6 %collective-permute-start.5 = (bf16[2,16,3072]{2,1,0:T(8,128)(2,1)S(1)}, bf16[2,16,3072]{2,1,0:T(8,128)(2,1)S(1)}, u32[]{:S(2)}, u32[]{:S(2)}) collective-permute-start(bf16[2,16,3072]{2,1,0:T(8,128)(2,1)S(1)} %collective-permute-done.3.refs_2_), channel_id=1, source_target_pairs={{4,0},{5,1},{6,2},{7,3},{8,4},{9,5},{10,6},{11,7},{12,8},{13,9},{1... | collective-permute-start | bytes 589832 | tf_op jit(solution)/shard_map/ppermute | solution.py:80
  16.3 5.7 %collective-permute-start.7 = (bf16[2,16,3072]{2,1,0:T(8,128)(2,1)S(1)}, bf16[2,16,3072]{2,1,0:T(8,128)(2,1)S(1)}, u32[]{:S(2)}, u32[]{:S(2)}) collective-permute-start(bf16[2,16,3072]{2,1,0:T(8,128)(2,1)S(1)} %collective-permute-done.6.refs_7_), channel_id=1, source_target_pairs={{12,0},{13,1},{14,2},{15,3},{0,4},{1,5},{2,6},{3,7},{4,8},{5,9},{6... | collective-permute-start | bytes 589832 | tf_op jit(solution)/shard_map/ppermute | solution.py:80
  19.8 18.8 %copy-start.1 = (f32[3,64,256]{2,1,0:T(8,128)S(1)}, f32[3,64,256]{2,1,0:T(8,128)}, u32[]{:S(2)}) copy-start(f32[3,64,256]{2,1,0:T(8,128)} %w1_in.1) | copy-start | bytes 589828
  19.8 18.7 %copy-start.2 = (f32[3,256,64]{1,2,0:T(8,128)S(1)}, f32[3,256,64]{1,2,0:T(8,128)}, u32[]{:S(2)}) copy-start(f32[3,256,64]{1,2,0:T(8,128)} %param.18) | copy-start | bytes 589828
  19.8 18.7 %copy-start.3 = (f32[3,64]{1,0:T(4,128)S(1)}, f32[3,64]{1,0:T(4,128)}, u32[]{:S(2)}) copy-start(f32[3,64]{1,0:T(4,128)} %gain_in.3) | copy-start | bytes 2308
  19.8 18.7 %copy-start.4 = (f32[3,64]{1,0:T(4,128)S(1)}, f32[3,64]{1,0:T(4,128)}, u32[]{:S(2)}) copy-start(f32[3,64]{1,0:T(4,128)} %shift_in.3) | copy-start | bytes 2308
  19.8 18.7 %copy-start.5 = (f32[3,256]{1,0:T(4,128)S(1)}, f32[3,256]{1,0:T(4,128)}, u32[]{:S(2)}) copy-start(f32[3,256]{1,0:T(4,128)} %c1_in.1) | copy-start | bytes 9220
  19.9 18.7 %copy-start.6 = (f32[3,64]{1,0:T(4,128)S(1)}, f32[3,64]{1,0:T(4,128)}, u32[]{:S(2)}) copy-start(f32[3,64]{1,0:T(4,128)} %c2_in.1) | copy-start | bytes 2308
  22.0 57.2 %copy-start = (bf16[192,3072]{1,0:T(8,128)(2,1)S(1)}, bf16[192,3072]{1,0:T(8,128)(2,1)}, u32[]{:S(2)}) copy-start(bf16[192,3072]{1,0:T(8,128)(2,1)} %weight.1) | copy-start | bytes 3538948
  39.1 10.1 %all-to-all-start.1 = ((bf16[8,64,128]{2,1,0:T(8,128)(2,1)}), bf16[8,64,128]{2,1,0:T(8,128)(2,1)S(1)}, u32[]{:S(2)}, u32[]{:S(2)}) async-start(bf16[8,64,128]{2,1,0:T(8,128)(2,1)} %get-tuple-element.37), calls=%async_computation.1 | async-start | bytes 262144 | tf_op jit(solution)/shard_map/all_to_all | solution.py:326
  42.5 0.7 collective-permute-start.9
  80.8 6.1 %collective-permute-start.10 = (bf16[2,16,3072]{2,1,0:T(8,128)(2,1)S(1)}, bf16[2,16,3072]{2,1,0:T(8,128)(2,1)S(1)}, u32[]{:S(2)}, u32[]{:S(2)}) collective-permute-start(bf16[2,16,3072]{2,1,0:T(8,128)(2,1)S(1)} %get-tuple-element.44), channel_id=1, source_target_pairs={{12,0},{13,1},{14,2},{15,3},{0,4},{1,5},{2,6},{3,7},{4,8},{5,9},{6... | collective-permute-start | bytes 589832 | tf_op jit(solution)/shard_map/ppermute | solution.py:80
  83.7 7.0 %collective-permute-start.14 = (bf16[2,16,3072]{2,1,0:T(8,128)(2,1)S(1)}, bf16[2,16,3072]{2,1,0:T(8,128)(2,1)S(1)}, u32[]{:S(2)}, u32[]{:S(2)}) collective-permute-start(bf16[2,16,3072]{2,1,0:T(8,128)(2,1)S(1)} %get-tuple-element.48), channel_id=1, source_target_pairs={{4,0},{5,1},{6,2},{7,3},{8,4},{9,5},{10,6},{11,7},{12,8},{13,9},{1... | collective-permute-start | bytes 589832 | tf_op jit(solution)/shard_map/ppermute | solution.py:80
  83.7 7.2 %collective-permute-start.12 = (bf16[2,16,3072]{2,1,0:T(8,128)(2,1)S(1)}, bf16[2,16,3072]{2,1,0:T(8,128)(2,1)S(1)}, u32[]{:S(2)}, u32[]{:S(2)}) collective-permute-start(bf16[2,16,3072]{2,1,0:T(8,128)(2,1)S(1)} %get-tuple-element.45), channel_id=1, source_target_pairs={{12,0},{13,1},{14,2},{15,3},{0,4},{1,5},{2,6},{3,7},{4,8},{5,9},{6... | collective-permute-start | bytes 589832 | tf_op jit(solution)/shard_map/ppermute | solution.py:80
  87.0 6.9 %collective-permute-start.13 = (bf16[2,16,3072]{2,1,0:T(8,128)(2,1)S(1)}, bf16[2,16,3072]{2,1,0:T(8,128)(2,1)S(1)}, u32[]{:S(2)}, u32[]{:S(2)}) collective-permute-start(bf16[2,16,3072]{2,1,0:T(8,128)(2,1)S(1)} %get-tuple-element.46), channel_id=1, source_target_pairs={{4,0},{5,1},{6,2},{7,3},{8,4},{9,5},{10,6},{11,7},{12,8},{13,9},{1... | collective-permute-start | bytes 589832 | tf_op jit(solution)/shard_map/ppermute | solution.py:80
  87.0 6.9 %collective-permute-start.11 = (bf16[2,16,3072]{2,1,0:T(8,128)(2,1)S(1)}, bf16[2,16,3072]{2,1,0:T(8,128)(2,1)S(1)}, u32[]{:S(2)}, u32[]{:S(2)}) collective-permute-start(bf16[2,16,3072]{2,1,0:T(8,128)(2,1)S(1)} %shard_map.122), channel_id=1, source_target_pairs={{12,0},{13,1},{14,2},{15,3},{0,4},{1,5},{2,6},{3,7},{4,8},{5,9},{6... | collective-permute-start | bytes 589832 | tf_op jit(solution)/shard_map/ppermute | solution.py:80
  90.8 7.0 %collective-permute-start.15 = (bf16[2,16,3072]{2,1,0:T(8,128)(2,1)S(1)}, bf16[2,16,3072]{2,1,0:T(8,128)(2,1)S(1)}, u32[]{:S(2)}, u32[]{:S(2)}) collective-permute-start(bf16[2,16,3072]{2,1,0:T(8,128)(2,1)S(1)} %shard_map.123), channel_id=1, source_target_pairs={{4,0},{5,1},{6,2},{7,3},{8,4},{9,5},{10,6},{11,7},{12,8},{13,9},{1... | collective-permute-start | bytes 589832 | tf_op jit(solution)/shard_map/ppermute | solution.py:80
  97.9 6.2 %collective-permute-start.16 = (bf16[16,3072]{1,0:T(8,128)(2,1)S(1)}, bf16[16,3072]{1,0:T(8,128)(2,1)S(1)}, u32[]{:S(2)}, u32[]{:S(2)}) collective-permute-start(bf16[16,3072]{1,0:T(8,128)(2,1)S(1)} %get-tuple-element.50), channel_id=1, source_target_pairs={{3,0},{0,1},{1,2},{2,3},{7,4},{4,5},{5,6},{6,7},{11,8},{8,9},{9,10... | collective-permute-start | bytes 294920 | tf_op jit(solution)/shard_map/ppermute | solution.py:80
  99.0 5.1 %collective-permute-start.17 = (bf16[16,3072]{1,0:T(8,128)(2,1)S(1)}, bf16[16,3072]{1,0:T(8,128)(2,1)S(1)}, u32[]{:S(2)}, u32[]{:S(2)}) collective-permute-start(bf16[16,3072]{1,0:T(8,128)(2,1)S(1)} %get-tuple-element.51), channel_id=1, source_target_pairs={{1,0},{2,1},{3,2},{0,3},{5,4},{6,5},{7,6},{4,7},{9,8},{10,9},{11,1... | collective-permute-start | bytes 294920 | tf_op jit(solution)/shard_map/ppermute | solution.py:80
  101.6 6.1 %collective-permute-start.18 = (bf16[16,3072]{1,0:T(8,128)(2,1)S(1)}, bf16[16,3072]{1,0:T(8,128)(2,1)S(1)}, u32[]{:S(2)}, u32[]{:S(2)}) collective-permute-start(bf16[16,3072]{1,0:T(8,128)(2,1)S(1)} %get-tuple-element.52), channel_id=1, source_target_pairs={{2,0},{3,1},{0,2},{1,3},{6,4},{7,5},{4,6},{5,7},{10,8},{11,9},{8,1... | collective-permute-start | bytes 294920 | tf_op jit(solution)/shard_map/ppermute | solution.py:80
where the time goes:
time: 109 us; the launch traced here: 108 us
  blocking collectives  32.1 us (29%)
  starting transfers between devices  29.5 us (27%)
  waiting for transfers between devices  25.4 us (23%)
  Pallas kernels  19.5 us (18%)
    all_to_all x2, blocking collectives, exchange(): lax.all_to_all(value, 'seq', 0, 0, axis_index_groups=GROUPS, tiled=True)  32.1 us
    ppermute x18, starting transfers between devices, from_side(): return lax.ppermute(value, ('seq', 'tensor'), pairs)  25.5 us
    ppermute x18, waiting for transfers between devices, from_side(): return lax.ppermute(value, ('seq', 'tensor'), pairs)  19.4 us
    pallas_call x1, Pallas kernels, shards(): kernel_call(second_kernel, answer_shape, 7)  11.3 us
    all_to_all x1, waiting for transfers between devices, exchange(): lax.all_to_all(value, 'seq', 0, 0, axis_index_groups=GROUPS, tiled=True)  6 us
    all_to_all x1, starting transfers between devices, exchange(): lax.all_to_all(value, 'seq', 0, 0, axis_index_groups=GROUPS, tiled=True)  3.38 us
    pallas_call x1, Pallas kernels, shards(): kernel_call(project_kernel, (jax.ShapeDtypeStruct((ROWS, 2 * MB + 16, 2 *...  3.15 us
  transfers between devices with their start and end apart: 20, of which 12 were waited for; matrix products, arithmetic and copies ran while one was open for 1% of the time, Pallas kernels for 2%

commit v1 on v0

--- a/solution.py
+++ b/solution.py
@@ -115,6 +115,8 @@
     logit = mm_nt(rows, rate_weight[...])
     rates = base_rate[...] * jax.nn.sigmoid(logit)
     lane = lax.broadcasted_iota(jnp.int32, (256, HEAD), 1)
+    spots = (lax.broadcasted_iota(jnp.int32, (16, 2 * HEAD), axis) for axis in range(2))
+    pick = jnp.where(next(spots) + HEAD == next(spots), 1.0, 0.0).astype(BF16)
     for head in range(3):
         parts = [weight[head, spot * HEAD : (spot + 1) * HEAD, :] for spot in (1, 2, 0)]
         value = mm_nt(rows, jnp.concatenate(parts, axis=0))
@@ -132,8 +134,7 @@
             target = place[SEAT + 3 * seq + head]
             block = by_place[seq].reshape(2 * MB, 256)
             pairs[target, 0 : 2 * MB] = block[:, 0 : 2 * HEAD].astype(BF16)
-            flipped = block[:, 2 * HEAD :].T
-            pairs[target, 2 * MB :] = flipped[HEAD : HEAD + 16].astype(BF16)
+            pairs[target, 2 * MB :] = mm_nt(pick, block[:, 2 * HEAD :].astype(BF16)).astype(BF16)
             for part in range(2):
                 queries[target, :, part * HEAD : (part + 1) * HEAD] = block[
                     part * MB : (part + 1) * MB, 2 * HEAD : 3 * HEAD
@@ -149,19 +150,21 @@
     return (q.astype(F32) + (gain * ((outer - m) * s) + shift)).astype(BF16)
 
 
-def advance(pairs, w1, c1, w2t, c2, gain, shift, visit):
+def advance(pairs, w1, c1, w2t, c2, gain, shift, rates, visit):
     gain2 = gain * gain
     g_mean = mean_last(gain2)
     line = lax.broadcasted_iota(jnp.int32, (16, HEAD), 0)
     rate_sum = jnp.where(line < 2, 1.0, 0.0).astype(BF16)
-
-    def step(state, here, part, kn, row, last):
+    for row in range(ROWS):
+        rates[row] = mm_tn(pairs[row, 2 * MB :, :], rate_sum)
+
+    def step(state, here, rate, part, kn, row, last):
         w1, c1, w2t, c2, pre = state
         spot = slice(part * MB, (part + 1) * MB)
         k, v = here[spot, 0:HEAD], here[spot, HEAD : 2 * HEAD]
         w1b = w1.astype(BF16)
         w2tb = w2t.astype(BF16)
-        r = mm_tn(here[2 * MB :, spot], rate_sum)
+        r = rate[spot]
         gram = (mm_nt(kn, k) + 1.0).astype(BF16)
         n_pre = mm(kn, w1b) + c1
         visit(row, last, w1b, c1, w2tb, c2)
@@ -197,8 +200,9 @@
     def two_steps(row, state):
         before, after = jnp.maximum(row - 1, 0), jnp.minimum(row + 1, ROWS - 1)
         here = pairs.at[row]
-        state = step(state, here, 0, here[MB : 2 * MB, 0:HEAD], before, 1)
-        return step(state, here, 1, pairs[after, 0:MB, 0:HEAD], row, 0)
+        rate = rates.at[row]
+        state = step(state, here, rate, 0, here[MB : 2 * MB, 0:HEAD], before, 1)
+        return step(state, here, rate, 1, pairs[after, 0:MB, 0:HEAD], row, 0)
 
     pre = mm(pairs[0, 0:MB, 0:HEAD], w1.astype(BF16)) + c1
     w1, c1, w2t, c2, pre = lax.fori_loop(0, ROWS, two_steps, (w1, c1, w2t, c2, pre))
@@ -207,7 +211,7 @@
 
 
 def first_kernel(
-    place, pairs, w1_in, c1_in, w2t_in, c2_in, gain_in, shift_in, state, weights, biases
+    place, pairs, w1_in, c1_in, w2t_in, c2_in, gain_in, shift_in, state, weights, biases, rates
 ):
     @pl.when(place[PHASE] == 0)
     def _():
@@ -223,7 +227,15 @@
             biases[row, part, 1:2, 0:HEAD] = c2
 
         w1, c1, w2t, c2 = advance(
-            pairs, w1_in[place[OWN]], c1_in[own], w2t, c2, gain_in[own], shift_in[own], keep
+            pairs,
+            w1_in[place[OWN]],
+            c1_in[own],
+            w2t,
+            c2,
+            gain_in[own],
+            shift_in[own],
+            rates,
+            keep,
         )
         state[0:64] = w1.astype(BF16)
         state[64:128] = w2t.astype(BF16)
@@ -236,7 +248,9 @@
         state[128:144] = jnp.where(line == 0, c1_high, low).astype(BF16)
 
 
-def second_kernel(place, pairs, queries, state, gain_in, shift_in, weights, biases, out):
+def second_kernel(
+    place, pairs, queries, state, gain_in, shift_in, weights, biases, out, rates
+):
     own = pl.ds(place[OWN], 1)
     gain, shift = gain_in[own], shift_in[own]
 
@@ -246,14 +260,15 @@
 
     @pl.when(place[PHASE] == 0)
     def _():
-        def both(row, unused):
-            for part in range(2):
+        def four(turn, unused):
+            for k in range(4):
+                row, part = 2 * turn + k // 2, k % 2
                 kept = weights.at[row, part]
                 bias = biases.at[row, part]
                 put(row, part, kept[0:HEAD], bias[0:1], kept[HEAD:], bias[1:2, 0:HEAD])
             return unused
 
-        lax.fori_loop(0, ROWS, both, 0)
+        lax.fori_loop(0, ROWS // 2, four, 0)
 
     @pl.when(place[PHASE] == 1)
     def _():
@@ -266,6 +281,7 @@
             (bias[2:3] + bias[3:4])[:, 0:HEAD],
             gain,
             shift,
+            rates,
             put,
         )
 
@@ -372,6 +388,7 @@
         scratch=[pltpu.VMEM((2, SIDE, SIDE, 8, 256), F32)],
     )(place, *pieces, *fetched)
     pairs = exchange(pairs)
+    rates = pltpu.VMEM((ROWS, 2 * MB, HEAD), F32)
     state, weights, biases = kernel_call(
         first_kernel,
         (
@@ -380,6 +397,7 @@
             jax.ShapeDtypeStruct((ROWS, 2, 8, INNER), F32),
         ),
         7,
+        scratch=[rates],
     )(
         place,
         pairs,
@@ -393,7 +411,7 @@
     state = lax.ppermute(state, "seq", RELAY)
     queries, biases = lax.optimization_barrier((queries, biases))
     queries = exchange(queries)
-    answers = kernel_call(second_kernel, answer_shape, 7)(
+    answers = kernel_call(second_kernel, answer_shape, 7, scratch=[rates])(
         place, pairs, queries, state, norm_gain, norm_shift, weights, biases
     )
     pair = jax.ShapeDtypeStruct((2, 16, width), BF16)

time: 109 us -> 109 us (level)
  no operation moved by 1% of the time
where the time goes in v1:
time: 109 us; the launch traced here: 108 us
  blocking collectives  31.8 us (29%)
  starting transfers between devices  29.5 us (27%)
  waiting for transfers between devices  25.4 us (23%)
  Pallas kernels  19.9 us (18%)
    all_to_all x2, blocking collectives, exchange(): lax.all_to_all(value, 'seq', 0, 0, axis_index_groups=GROUPS, tiled=True)  31.8 us
    ppermute x18, starting transfers between devices, from_side(): return lax.ppermute(value, ('seq', 'tensor'), pairs)  25.5 us
    ppermute x18, waiting for transfers between devices, from_side(): return lax.ppermute(value, ('seq', 'tensor'), pairs)  19.4 us
    pallas_call x1, Pallas kernels, shards(): kernel_call(second_kernel, answer_shape, 7, scratch=[rates])  10.6 us
    all_to_all x1, waiting for transfers between devices, exchange(): lax.all_to_all(value, 'seq', 0, 0, axis_index_groups=GROUPS, tiled=True)  6 us
    pallas_call x1, Pallas kernels, shards(): kernel_call(project_kernel, (jax.ShapeDtypeStruct((ROWS, 2 * MB + 16, 2 *...  4.2 us
    all_to_all x1, starting transfers between devices, exchange(): lax.all_to_all(value, 'seq', 0, 0, axis_index_groups=GROUPS, tiled=True)  3.38 us
  transfers between devices with their start and end apart: 20, of which 12 were waited for; matrix products, arithmetic and copies ran while one was open for 1% of the time, Pallas kernels for 2%

profile of v1, /device:TPU:152, one launch (start us, length us, event | category | flops | bytes accessed | tf_op | source)
XLA Modules:
  0.0 108.5 jit_solution(2153414017720947967)
XLA Ops:
  0.0 0.7 dynamic-slice_bitcast_fusion.place
  0.7 2.8 %collective-permute-start = (bf16[16,3072]{1,0:T(8,128)(2,1)}, bf16[16,3072]{1,0:T(8,128)(2,1)S(1)}, u32[]{:S(2)}, u32[]{:S(2)}) collective-permute-start(bf16[16,3072]{1,0:T(8,128)(2,1)} %bitcast.11), channel_id=1, source_target_pairs={{1,0},{2,1},{3,2},{0,3},{5,4},{6,5},{7,6},{4,7},{9,8},{10,9},{11,1... | collective-permute-start | bytes 294920 | tf_op jit(solution)/shard_map/ppermute | solution.py:80
  3.5 2.3 %collective-permute-start.1 = (bf16[16,3072]{1,0:T(8,128)(2,1)}, bf16[16,3072]{1,0:T(8,128)(2,1)S(1)}, u32[]{:S(2)}, u32[]{:S(2)}) collective-permute-start(bf16[16,3072]{1,0:T(8,128)(2,1)} %bitcast.13), channel_id=1, source_target_pairs={{2,0},{3,1},{0,2},{1,3},{6,4},{7,5},{4,6},{5,7},{10,8},{11,9},{8,1... | collective-permute-start | bytes 294920 | tf_op jit(solution)/shard_map/ppermute | solution.py:80
  6.0 0.9 pad_maximum_fusion.refs_0_
  6.9 0.8 collective-permute-start.3
  7.7 2.8 %collective-permute-done.2 = bf16[16,3072]{1,0:T(8,128)(2,1)S(1)} collective-permute-done((bf16[16,3072]{1,0:T(8,128)(2,1)}, bf16[16,3072]{1,0:T(8,128)(2,1)S(1)}, u32[]{:S(2)}, u32[]{:S(2)}) %collective-permute-start.2) | collective-permute-done | bytes 98336 | tf_op jit(solution)/shard_map/ppermute | solution.py:80
  10.9 1.6 %collective-permute-start.8 = (bf16[2,16,3072]{2,1,0:T(8,128)(2,1)S(1)}, bf16[2,16,3072]{2,1,0:T(8,128)(2,1)S(1)}, u32[]{:S(2)}, u32[]{:S(2)}) collective-permute-start(bf16[2,16,3072]{2,1,0:T(8,128)(2,1)S(1)} %pad_maximum_fusion.refs_0_), channel_id=1, source_target_pairs={{12,0},{13,1},{14,2},{15,3},{0,4},{1,5},{2,6},{3,7},{4,8},{5,9},{6... | collective-permute-start | bytes 589832 | tf_op jit(solution)/shard_map/ppermute | solution.py:80
  12.9 1.0 collective-permute-done.3.refs_2_
  13.9 0.9 collective-permute-start.5
  14.7 1.6 %collective-permute-done.6.refs_7_ = bf16[2,16,3072]{2,1,0:T(8,128)(2,1)S(1)} collective-permute-done((bf16[2,16,3072]{2,1,0:T(8,128)(2,1)S(1)}, bf16[2,16,3072]{2,1,0:T(8,128)(2,1)S(1)}, u32[]{:S(2)}, u32[]{:S(2)}) %collective-permute-start.6) | collective-permute-done | bytes 196640 | tf_op jit(solution)/shard_map/ppermute | solution.py:80
  16.3 1.4 %collective-permute-start.7 = (bf16[2,16,3072]{2,1,0:T(8,128)(2,1)S(1)}, bf16[2,16,3072]{2,1,0:T(8,128)(2,1)S(1)}, u32[]{:S(2)}, u32[]{:S(2)}) collective-permute-start(bf16[2,16,3072]{2,1,0:T(8,128)(2,1)S(1)} %collective-permute-done.6.refs_7_), channel_id=1, source_target_pairs={{12,0},{13,1},{14,2},{15,3},{0,4},{1,5},{2,6},{3,7},{4,8},{5,9},{6... | collective-permute-start | bytes 589832 | tf_op jit(solution)/shard_map/ppermute | solution.py:80
  17.8 2.0 %fetch.1 = (bf16[3,192,3072]{2,1,0:T(8,128)(2,1)S(1)}, bf16[3,3072]{1,0:T(4,128)(2,1)S(1)}, f32[1,3]{1,0:T(1,128)S(1)}) custom-call(bf16[2,16,3072]{2,1,0:T(8,128)(2,1)S(1)} %pad_maximum_fusion.1.after.refs_1_, bf16[3,192,3072]{2,1,0:T(8,128)(2,1)} %weight_in.1, bf16[3,3072]{1,0:T(4,128)(2,1)} %rate_weight_in.1, f32[1,3]{1,0:T(1,128)} %bitcast.18), custom_call_target="tpu_custom_call" | custom-call | bytes 4194304 | tf_op jit(solution)/shard_map/fetch/pallas_call | solution.py:372
  19.9 1.6 %collective-permute-done.5.refs_4_ = bf16[2,16,3072]{2,1,0:T(8,128)(2,1)S(1)} collective-permute-done((bf16[2,16,3072]{2,1,0:T(8,128)(2,1)S(1)}, bf16[2,16,3072]{2,1,0:T(8,128)(2,1)S(1)}, u32[]{:S(2)}, u32[]{:S(2)}) %collective-permute-start.5) | collective-permute-done | bytes 196640 | tf_op jit(solution)/shard_map/ppermute | solution.py:80
  22.0 4.2 %shard_map.118 = (bf16[8,144,128]{2,1,0:T(8,128)(2,1)S(1)}, bf16[8,64,128]{2,1,0:T(8,128)(2,1)}) custom-call(s32[10]{0:T(128)S(1)} %dynamic-slice_bitcast_fusion.place, bf16[2,16,3072]{2,1,0:T(8,128)(2,1)S(1)} %pad_maximum_fusion.refs_0_, bf16[2,16,3072]{2,1,0:T(8,128)(2,1)S(1)} %pad_maximum_fusion.1.after.refs_1_, ...), custom_call_target="tpu_custom_call" | custom-call | tf_op jit(solution)/shard_map/pallas_call | solution.py:384
  26.2 13.4 %all_to_all.15.pairs = bf16[8,144,128]{2,1,0:T(8,128)(2,1)S(1)} all-to-all(bf16[8,144,128]{2,1,0:T(8,128)(2,1)S(1)} %get-tuple-element.34), channel_id=1, replica_groups={{0,16,32,48,64,80,96,112},{128,144,160,176,192,208,224,240},{1,17,33,49..., dimensions={0} | all-to-all | bytes 589824 | tf_op jit(solution)/shard_map/all_to_all | solution.py:342
  40.2 3.4 %all-to-all-start.1 = ((bf16[8,64,128]{2,1,0:T(8,128)(2,1)}), bf16[8,64,128]{2,1,0:T(8,128)(2,1)S(1)}, u32[]{:S(2)}, u32[]{:S(2)}) async-start(bf16[8,64,128]{2,1,0:T(8,128)(2,1)} %get-tuple-element.37), calls=%async_computation.1 | async-start | bytes 262144 | tf_op jit(solution)/shard_map/all_to_all | solution.py:342
  43.6 0.7 collective-permute-start.9
  44.3 6.0 %all-to-all-done.1.queries = bf16[8,64,128]{2,1,0:T(8,128)(2,1)S(1)} async-done(((bf16[8,64,128]{2,1,0:T(8,128)(2,1)}), bf16[8,64,128]{2,1,0:T(8,128)(2,1)S(1)}, u32[]{:S(2)}, u32[]{:S(2)}) %all-to-all-start.1) | async-done | bytes 131104 | tf_op jit(solution)/shard_map/all_to_all | solution.py:342
  50.3 10.6 %shard_map.120 = bf16[8,64,128]{2,1,0:T(8,128)(2,1)S(1)} custom-call(s32[10]{0:T(128)S(1)} %dynamic-slice_bitcast_fusion.place, bf16[8,144,128]{2,1,0:T(8,128)(2,1)S(1)} %all_to_all.15.pairs, bf16[8,64,128]{2,1,0:T(8,128)(2,1)S(1)} %all-to-all-done.1.queries, bf16[144,256]{1,0:T(8,128)(2,1)S(1)} %collective-permute-done.9.state, f32[3,64]{1,0:T(4,128)S(1)} %copy-done.3, ...), custom_call_target="tpu_custom_call" | custom-call | tf_op jit(solution)/shard_map/pallas_call | solution.py:414
  60.8 18.4 %all_to_all.16.answers = bf16[8,64,128]{2,1,0:T(8,128)(2,1)S(1)} all-to-all(bf16[8,64,128]{2,1,0:T(8,128)(2,1)S(1)} %shard_map.120), channel_id=1, replica_groups={{0,16,32,48,64,80,96,112},{128,144,160,176,192,208,224,240},{1,17,33,49..., dimensions={0} | all-to-all | bytes 262144 | tf_op jit(solution)/shard_map/all_to_all | solution.py:342
  79.3 1.6 %shard_map.121 = (bf16[2,16,3072]{2,1,0:T(8,128)(2,1)S(1)}, bf16[2,16,3072]{2,1,0:T(8,128)(2,1)S(1)}, bf16[2,16,3072]{2,1,0:T(8,128)(2,1)S(1)}, bf16[2,16,3072]{...) custom-call(s32[10]{0:T(128)S(1)} %dynamic-slice_bitcast_fusion.plac, ...), custom_call_target="tpu_custom_call" | custom-call | tf_op jit(solution)/shard_map/pallas_call | solution.py:419
  80.9 2.9 %collective-permute-start.10 = (bf16[2,16,3072]{2,1,0:T(8,128)(2,1)S(1)}, bf16[2,16,3072]{2,1,0:T(8,128)(2,1)S(1)}, u32[]{:S(2)}, u32[]{:S(2)}) collective-permute-start(bf16[2,16,3072]{2,1,0:T(8,128)(2,1)S(1)} %get-tuple-element.44), channel_id=1, source_target_pairs={{12,0},{13,1},{14,2},{15,3},{0,4},{1,5},{2,6},{3,7},{4,8},{5,9},{6... | collective-permute-start | bytes 589832 | tf_op jit(solution)/shard_map/ppermute | solution.py:80
  83.8 3.2 %collective-permute-start.12 = (bf16[2,16,3072]{2,1,0:T(8,128)(2,1)S(1)}, bf16[2,16,3072]{2,1,0:T(8,128)(2,1)S(1)}, u32[]{:S(2)}, u32[]{:S(2)}) collective-permute-start(bf16[2,16,3072]{2,1,0:T(8,128)(2,1)S(1)} %get-tuple-element.45), channel_id=1, source_target_pairs={{12,0},{13,1},{14,2},{15,3},{0,4},{1,5},{2,6},{3,7},{4,8},{5,9},{6... | collective-permute-start | bytes 589832 | tf_op jit(solution)/shard_map/ppermute | solution.py:80
  87.1 3.7 %collective-permute-start.11 = (bf16[2,16,3072]{2,1,0:T(8,128)(2,1)S(1)}, bf16[2,16,3072]{2,1,0:T(8,128)(2,1)S(1)}, u32[]{:S(2)}, u32[]{:S(2)}) collective-permute-start(bf16[2,16,3072]{2,1,0:T(8,128)(2,1)S(1)} %shard_map.122), channel_id=1, source_target_pairs={{12,0},{13,1},{14,2},{15,3},{0,4},{1,5},{2,6},{3,7},{4,8},{5,9},{6... | collective-permute-start | bytes 589832 | tf_op jit(solution)/shard_map/ppermute | solution.py:80
  91.0 3.0 %collective-permute-done.13.refs_4_ = bf16[2,16,3072]{2,1,0:T(8,128)(2,1)S(1)} collective-permute-done((bf16[2,16,3072]{2,1,0:T(8,128)(2,1)S(1)}, bf16[2,16,3072]{2,1,0:T(8,128)(2,1)S(1)}, u32[]{:S(2)}, u32[]{:S(2)}) %collective-permute-start.13) | collective-permute-done | bytes 196640 | tf_op jit(solution)/shard_map/ppermute | solution.py:80
  94.0 3.8 %collective-permute-done.15.refs_5_ = bf16[2,16,3072]{2,1,0:T(8,128)(2,1)S(1)} collective-permute-done((bf16[2,16,3072]{2,1,0:T(8,128)(2,1)S(1)}, bf16[2,16,3072]{2,1,0:T(8,128)(2,1)S(1)}, u32[]{:S(2)}, u32[]{:S(2)}) %collective-permute-start.15) | collective-permute-done | bytes 196640 | tf_op jit(solution)/shard_map/ppermute | solution.py:80
  98.0 1.1 %collective-permute-start.16 = (bf16[16,3072]{1,0:T(8,128)(2,1)S(1)}, bf16[16,3072]{1,0:T(8,128)(2,1)S(1)}, u32[]{:S(2)}, u32[]{:S(2)}) collective-permute-start(bf16[16,3072]{1,0:T(8,128)(2,1)S(1)} %get-tuple-element.50), channel_id=1, source_target_pairs={{3,0},{0,1},{1,2},{2,3},{7,4},{4,5},{5,6},{6,7},{11,8},{8,9},{9,10... | collective-permute-start | bytes 294920 | tf_op jit(solution)/shard_map/ppermute | solution.py:80
  99.1 2.6 %collective-permute-start.17 = (bf16[16,3072]{1,0:T(8,128)(2,1)S(1)}, bf16[16,3072]{1,0:T(8,128)(2,1)S(1)}, u32[]{:S(2)}, u32[]{:S(2)}) collective-permute-start(bf16[16,3072]{1,0:T(8,128)(2,1)S(1)} %get-tuple-element.51), channel_id=1, source_target_pairs={{1,0},{2,1},{3,2},{0,3},{5,4},{6,5},{7,6},{4,7},{9,8},{10,9},{11,1... | collective-permute-start | bytes 294920 | tf_op jit(solution)/shard_map/ppermute | solution.py:80
  101.7 1.4 %collective-permute-start.18 = (bf16[16,3072]{1,0:T(8,128)(2,1)S(1)}, bf16[16,3072]{1,0:T(8,128)(2,1)S(1)}, u32[]{:S(2)}, u32[]{:S(2)}) collective-permute-start(bf16[16,3072]{1,0:T(8,128)(2,1)S(1)} %get-tuple-element.52), channel_id=1, source_target_pairs={{2,0},{3,1},{0,2},{1,3},{6,4},{7,5},{4,6},{5,7},{10,8},{11,9},{8,1... | collective-permute-start | bytes 294920 | tf_op jit(solution)/shard_map/ppermute | solution.py:80
  103.1 1.1 %collective-permute-done.16.refs_1_ = bf16[16,3072]{1,0:T(8,128)(2,1)S(1)} collective-permute-done((bf16[16,3072]{1,0:T(8,128)(2,1)S(1)}, bf16[16,3072]{1,0:T(8,128)(2,1)S(1)}, u32[]{:S(2)}, u32[]{:S(2)}) %collective-permute-start.16) | collective-permute-done | bytes 98336 | tf_op jit(solution)/shard_map/ppermute | solution.py:80
  104.2 3.6 %collective-permute-done.18.refs_3_ = bf16[16,3072]{1,0:T(8,128)(2,1)S(1)} collective-permute-done((bf16[16,3072]{1,0:T(8,128)(2,1)S(1)}, bf16[16,3072]{1,0:T(8,128)(2,1)S(1)}, u32[]{:S(2)}, u32[]{:S(2)}) %collective-permute-start.18) | collective-permute-done | bytes 98336 | tf_op jit(solution)/shard_map/ppermute | solution.py:80
  107.8 0.7 shard_map.125
  (36 shorter events, 2.6 us)
Async XLA Ops:
  0.7 5.3 %collective-permute-start = (bf16[16,3072]{1,0:T(8,128)(2,1)}, bf16[16,3072]{1,0:T(8,128)(2,1)S(1)}, u32[]{:S(2)}, u32[]{:S(2)}) collective-permute-start(bf16[16,3072]{1,0:T(8,128)(2,1)} %bitcast.11), channel_id=1, source_target_pairs={{1,0},{2,1},{3,2},{0,3},{5,4},{6,5},{7,6},{4,7},{9,8},{10,9},{11,1... | collective-permute-start | bytes 294920 | tf_op jit(solution)/shard_map/ppermute | solution.py:80
  3.5 7.1 %collective-permute-start.2 = (bf16[16,3072]{1,0:T(8,128)(2,1)}, bf16[16,3072]{1,0:T(8,128)(2,1)S(1)}, u32[]{:S(2)}, u32[]{:S(2)}) collective-permute-start(bf16[16,3072]{1,0:T(8,128)(2,1)} %bitcast.12), channel_id=1, source_target_pairs={{3,0},{0,1},{1,2},{2,3},{7,4},{4,5},{5,6},{6,7},{11,8},{8,9},{9,10... | collective-permute-start | bytes 294920 | tf_op jit(solution)/shard_map/ppermute | solution.py:80
  3.5 7.1 %collective-permute-start.1 = (bf16[16,3072]{1,0:T(8,128)(2,1)}, bf16[16,3072]{1,0:T(8,128)(2,1)S(1)}, u32[]{:S(2)}, u32[]{:S(2)}) collective-permute-start(bf16[16,3072]{1,0:T(8,128)(2,1)} %bitcast.13), channel_id=1, source_target_pairs={{2,0},{3,1},{0,2},{1,3},{6,4},{7,5},{4,6},{5,7},{10,8},{11,9},{8,1... | collective-permute-start | bytes 294920 | tf_op jit(solution)/shard_map/ppermute | solution.py:80
  6.9 7.0 %collective-permute-start.3 = (bf16[2,16,3072]{2,1,0:T(8,128)(2,1)S(1)}, bf16[2,16,3072]{2,1,0:T(8,128)(2,1)S(1)}, u32[]{:S(2)}, u32[]{:S(2)}) collective-permute-start(bf16[2,16,3072]{2,1,0:T(8,128)(2,1)S(1)} %pad_maximum_fusion.refs_0_), channel_id=1, source_target_pairs={{4,0},{5,1},{6,2},{7,3},{8,4},{9,5},{10,6},{11,7},{12,8},{13,9},{1... | collective-permute-start | bytes 589832 | tf_op jit(solution)/shard_map/ppermute | solution.py:80
  10.6 5.7 %collective-permute-start.6 = (bf16[2,16,3072]{2,1,0:T(8,128)(2,1)S(1)}, bf16[2,16,3072]{2,1,0:T(8,128)(2,1)S(1)}, u32[]{:S(2)}, u32[]{:S(2)}) collective-permute-start(bf16[2,16,3072]{2,1,0:T(8,128)(2,1)S(1)} %pad_maximum_fusion.1.after.refs_1_), channel_id=1, source_target_pairs={{12,0},{13,1},{14,2},{15,3},{0,4},{1,5},{2,6},{3,7},{4,8},{5,9},{6... | collective-permute-start | bytes 589832 | tf_op jit(solution)/shard_map/ppermute | solution.py:80
  10.9 9.0 %collective-permute-start.8 = (bf16[2,16,3072]{2,1,0:T(8,128)(2,1)S(1)}, bf16[2,16,3072]{2,1,0:T(8,128)(2,1)S(1)}, u32[]{:S(2)}, u32[]{:S(2)}) collective-permute-start(bf16[2,16,3072]{2,1,0:T(8,128)(2,1)S(1)} %pad_maximum_fusion.refs_0_), channel_id=1, source_target_pairs={{12,0},{13,1},{14,2},{15,3},{0,4},{1,5},{2,6},{3,7},{4,8},{5,9},{6... | collective-permute-start | bytes 589832 | tf_op jit(solution)/shard_map/ppermute | solution.py:80
  12.4 7.4 %collective-permute-start.4 = (bf16[2,16,3072]{2,1,0:T(8,128)(2,1)S(1)}, bf16[2,16,3072]{2,1,0:T(8,128)(2,1)S(1)}, u32[]{:S(2)}, u32[]{:S(2)}) collective-permute-start(bf16[2,16,3072]{2,1,0:T(8,128)(2,1)S(1)} %pad_maximum_fusion.1.after.refs_1_), channel_id=1, source_target_pairs={{4,0},{5,1},{6,2},{7,3},{8,4},{9,5},{10,6},{11,7},{12,8},{13,9},{1... | collective-permute-start | bytes 589832 | tf_op jit(solution)/shard_map/ppermute | solution.py:80
  13.9 7.6 %collective-permute-start.5 = (bf16[2,16,3072]{2,1,0:T(8,128)(2,1)S(1)}, bf16[2,16,3072]{2,1,0:T(8,128)(2,1)S(1)}, u32[]{:S(2)}, u32[]{:S(2)}) collective-permute-start(bf16[2,16,3072]{2,1,0:T(8,128)(2,1)S(1)} %collective-permute-done.3.refs_2_), channel_id=1, source_target_pairs={{4,0},{5,1},{6,2},{7,3},{8,4},{9,5},{10,6},{11,7},{12,8},{13,9},{1... | collective-permute-start | bytes 589832 | tf_op jit(solution)/shard_map/ppermute | solution.py:80
  16.3 5.7 %collective-permute-start.7 = (bf16[2,16,3072]{2,1,0:T(8,128)(2,1)S(1)}, bf16[2,16,3072]{2,1,0:T(8,128)(2,1)S(1)}, u32[]{:S(2)}, u32[]{:S(2)}) collective-permute-start(bf16[2,16,3072]{2,1,0:T(8,128)(2,1)S(1)} %collective-permute-done.6.refs_7_), channel_id=1, source_target_pairs={{12,0},{13,1},{14,2},{15,3},{0,4},{1,5},{2,6},{3,7},{4,8},{5,9},{6... | collective-permute-start | bytes 589832 | tf_op jit(solution)/shard_map/ppermute | solution.py:80
  19.8 19.8 %copy-start.1 = (f32[3,64,256]{2,1,0:T(8,128)S(1)}, f32[3,64,256]{2,1,0:T(8,128)}, u32[]{:S(2)}) copy-start(f32[3,64,256]{2,1,0:T(8,128)} %w1_in.1) | copy-start | bytes 589828
  19.8 19.8 %copy-start.2 = (f32[3,256,64]{1,2,0:T(8,128)S(1)}, f32[3,256,64]{1,2,0:T(8,128)}, u32[]{:S(2)}) copy-start(f32[3,256,64]{1,2,0:T(8,128)} %param.18) | copy-start | bytes 589828
  19.8 19.8 %copy-start.3 = (f32[3,64]{1,0:T(4,128)S(1)}, f32[3,64]{1,0:T(4,128)}, u32[]{:S(2)}) copy-start(f32[3,64]{1,0:T(4,128)} %gain_in.3) | copy-start | bytes 2308
  19.8 19.8 %copy-start.4 = (f32[3,64]{1,0:T(4,128)S(1)}, f32[3,64]{1,0:T(4,128)}, u32[]{:S(2)}) copy-start(f32[3,64]{1,0:T(4,128)} %shift_in.3) | copy-start | bytes 2308
  19.8 19.8 %copy-start.5 = (f32[3,256]{1,0:T(4,128)S(1)}, f32[3,256]{1,0:T(4,128)}, u32[]{:S(2)}) copy-start(f32[3,256]{1,0:T(4,128)} %c1_in.1) | copy-start | bytes 9220
  19.9 19.8 %copy-start.6 = (f32[3,64]{1,0:T(4,128)S(1)}, f32[3,64]{1,0:T(4,128)}, u32[]{:S(2)}) copy-start(f32[3,64]{1,0:T(4,128)} %c2_in.1) | copy-start | bytes 2308
  22.0 57.3 %copy-start = (bf16[192,3072]{1,0:T(8,128)(2,1)S(1)}, bf16[192,3072]{1,0:T(8,128)(2,1)}, u32[]{:S(2)}) copy-start(bf16[192,3072]{1,0:T(8,128)(2,1)} %weight.1) | copy-start | bytes 3538948
  40.2 10.1 %all-to-all-start.1 = ((bf16[8,64,128]{2,1,0:T(8,128)(2,1)}), bf16[8,64,128]{2,1,0:T(8,128)(2,1)S(1)}, u32[]{:S(2)}, u32[]{:S(2)}) async-start(bf16[8,64,128]{2,1,0:T(8,128)(2,1)} %get-tuple-element.37), calls=%async_computation.1 | async-start | bytes 262144 | tf_op jit(solution)/shard_map/all_to_all | solution.py:342
  43.6 0.7 collective-permute-start.9
  80.9 6.1 %collective-permute-start.10 = (bf16[2,16,3072]{2,1,0:T(8,128)(2,1)S(1)}, bf16[2,16,3072]{2,1,0:T(8,128)(2,1)S(1)}, u32[]{:S(2)}, u32[]{:S(2)}) collective-permute-start(bf16[2,16,3072]{2,1,0:T(8,128)(2,1)S(1)} %get-tuple-element.44), channel_id=1, source_target_pairs={{12,0},{13,1},{14,2},{15,3},{0,4},{1,5},{2,6},{3,7},{4,8},{5,9},{6... | collective-permute-start | bytes 589832 | tf_op jit(solution)/shard_map/ppermute | solution.py:80
  83.8 7.0 %collective-permute-start.14 = (bf16[2,16,3072]{2,1,0:T(8,128)(2,1)S(1)}, bf16[2,16,3072]{2,1,0:T(8,128)(2,1)S(1)}, u32[]{:S(2)}, u32[]{:S(2)}) collective-permute-start(bf16[2,16,3072]{2,1,0:T(8,128)(2,1)S(1)} %get-tuple-element.48), channel_id=1, source_target_pairs={{4,0},{5,1},{6,2},{7,3},{8,4},{9,5},{10,6},{11,7},{12,8},{13,9},{1... | collective-permute-start | bytes 589832 | tf_op jit(solution)/shard_map/ppermute | solution.py:80
  83.8 7.2 %collective-permute-start.12 = (bf16[2,16,3072]{2,1,0:T(8,128)(2,1)S(1)}, bf16[2,16,3072]{2,1,0:T(8,128)(2,1)S(1)}, u32[]{:S(2)}, u32[]{:S(2)}) collective-permute-start(bf16[2,16,3072]{2,1,0:T(8,128)(2,1)S(1)} %get-tuple-element.45), channel_id=1, source_target_pairs={{12,0},{13,1},{14,2},{15,3},{0,4},{1,5},{2,6},{3,7},{4,8},{5,9},{6... | collective-permute-start | bytes 589832 | tf_op jit(solution)/shard_map/ppermute | solution.py:80
  87.1 6.9 %collective-permute-start.13 = (bf16[2,16,3072]{2,1,0:T(8,128)(2,1)S(1)}, bf16[2,16,3072]{2,1,0:T(8,128)(2,1)S(1)}, u32[]{:S(2)}, u32[]{:S(2)}) collective-permute-start(bf16[2,16,3072]{2,1,0:T(8,128)(2,1)S(1)} %get-tuple-element.46), channel_id=1, source_target_pairs={{4,0},{5,1},{6,2},{7,3},{8,4},{9,5},{10,6},{11,7},{12,8},{13,9},{1... | collective-permute-start | bytes 589832 | tf_op jit(solution)/shard_map/ppermute | solution.py:80
  87.1 6.9 %collective-permute-start.11 = (bf16[2,16,3072]{2,1,0:T(8,128)(2,1)S(1)}, bf16[2,16,3072]{2,1,0:T(8,128)(2,1)S(1)}, u32[]{:S(2)}, u32[]{:S(2)}) collective-permute-start(bf16[2,16,3072]{2,1,0:T(8,128)(2,1)S(1)} %shard_map.122), channel_id=1, source_target_pairs={{12,0},{13,1},{14,2},{15,3},{0,4},{1,5},{2,6},{3,7},{4,8},{5,9},{6... | collective-permute-start | bytes 589832 | tf_op jit(solution)/shard_map/ppermute | solution.py:80
  90.9 7.0 %collective-permute-start.15 = (bf16[2,16,3072]{2,1,0:T(8,128)(2,1)S(1)}, bf16[2,16,3072]{2,1,0:T(8,128)(2,1)S(1)}, u32[]{:S(2)}, u32[]{:S(2)}) collective-permute-start(bf16[2,16,3072]{2,1,0:T(8,128)(2,1)S(1)} %shard_map.123), channel_id=1, source_target_pairs={{4,0},{5,1},{6,2},{7,3},{8,4},{9,5},{10,6},{11,7},{12,8},{13,9},{1... | collective-permute-start | bytes 589832 | tf_op jit(solution)/shard_map/ppermute | solution.py:80
  98.0 6.2 %collective-permute-start.16 = (bf16[16,3072]{1,0:T(8,128)(2,1)S(1)}, bf16[16,3072]{1,0:T(8,128)(2,1)S(1)}, u32[]{:S(2)}, u32[]{:S(2)}) collective-permute-start(bf16[16,3072]{1,0:T(8,128)(2,1)S(1)} %get-tuple-element.50), channel_id=1, source_target_pairs={{3,0},{0,1},{1,2},{2,3},{7,4},{4,5},{5,6},{6,7},{11,8},{8,9},{9,10... | collective-permute-start | bytes 294920 | tf_op jit(solution)/shard_map/ppermute | solution.py:80
  99.1 5.1 %collective-permute-start.17 = (bf16[16,3072]{1,0:T(8,128)(2,1)S(1)}, bf16[16,3072]{1,0:T(8,128)(2,1)S(1)}, u32[]{:S(2)}, u32[]{:S(2)}) collective-permute-start(bf16[16,3072]{1,0:T(8,128)(2,1)S(1)} %get-tuple-element.51), channel_id=1, source_target_pairs={{1,0},{2,1},{3,2},{0,3},{5,4},{6,5},{7,6},{4,7},{9,8},{10,9},{11,1... | collective-permute-start | bytes 294920 | tf_op jit(solution)/shard_map/ppermute | solution.py:80
  101.7 6.1 %collective-permute-start.18 = (bf16[16,3072]{1,0:T(8,128)(2,1)S(1)}, bf16[16,3072]{1,0:T(8,128)(2,1)S(1)}, u32[]{:S(2)}, u32[]{:S(2)}) collective-permute-start(bf16[16,3072]{1,0:T(8,128)(2,1)S(1)} %get-tuple-element.52), channel_id=1, source_target_pairs={{2,0},{3,1},{0,2},{1,3},{6,4},{7,5},{4,6},{5,7},{10,8},{11,9},{8,1... | collective-permute-start | bytes 294920 | tf_op jit(solution)/shard_map/ppermute | solution.py:80

commit v2 on v1

--- a/solution.py
+++ b/solution.py
@@ -69,15 +69,20 @@
     return table.reshape(2 * ROWS * SIDE * SIDE, -1)
 
 
-def from_side(value, turn, ahead):
+def from_side(value, turn, step):
     pairs = []
     for row in range(2 * ROWS):
         unit = 1 if (row + turn) % 2 == 0 else SIDE
         for place in range(SIDE * SIDE):
             at = place // unit % SIDE
-            source = place + ((at + ahead) % SIDE - at) * unit
-            pairs.append((row * SIDE * SIDE + source, row * SIDE * SIDE + place))
+            far = (at + (step if at % 2 == 0 else -step)) % SIDE
+            pairs.append((row * SIDE * SIDE + place + (far - at) * unit, row * SIDE * SIDE + place))
     return lax.ppermute(value, ("seq", "tensor"), pairs)
+
+
+def line_y(place, step):
+    up, down = place[Y] + step, place[Y] + SIDE - step
+    return lax.rem(jnp.where(lax.rem(place[Y], 2) == 0, up, down), SIDE)
 
 
 RELAY = [
@@ -94,50 +99,55 @@
 SCALARS = pl.BlockSpec(memory_space=pltpu.SMEM)
 
 
-def fetch_kernel(after, weight_in, rate_weight_in, base_rate_in, *refs):
-    arrived = refs[3]
+def fetch_kernel(after, weight_in, rate_weight_in, *refs):
+    weight, rate_weight, rate_weight_here, arrived = refs
     copies = [
         pltpu.make_async_copy(source, target, arrived.at[k])
         for k, (source, target) in enumerate(
-            zip((weight_in, rate_weight_in, base_rate_in), refs[:3], strict=True)
+            ((weight_in, weight), (rate_weight_in, rate_weight_here))
         )
     ]
     for copy in copies:
         copy.start()
-    for copy in copies:
-        copy.wait()
+    rate_weight[...] = jnp.zeros_like(rate_weight)
+    copies[1].wait()
+    for head in range(3):
+        for part in range(2):
+            rate_weight[2 * head + part : 2 * head + part + 1] = rate_weight_here[head : head + 1]
+    copies[0].wait()
 
 
 def project_kernel(place, *refs):
     pieces = refs[: 2 * SIDE]
-    weight, rate_weight, base_rate, pairs, queries, by_place = refs[2 * SIDE :]
+    weight, rate_weight, base_rate, pairs, queries, by_place, rate_place = refs[2 * SIDE :]
     rows = jnp.concatenate([piece[...].reshape(32, piece.shape[2]) for piece in pieces], axis=0)
-    logit = mm_nt(rows, rate_weight[...])
-    rates = base_rate[...] * jax.nn.sigmoid(logit)
-    lane = lax.broadcasted_iota(jnp.int32, (256, HEAD), 1)
-    spots = (lax.broadcasted_iota(jnp.int32, (16, 2 * HEAD), axis) for axis in range(2))
-    pick = jnp.where(next(spots) + HEAD == next(spots), 1.0, 0.0).astype(BF16)
+
+    def settle(value, target):
+        value = value.reshape(SIDE, SIDE, 2, 8, value.shape[1])
+        for k in range(SIDE):
+            y = line_y(place, k)
+            for seq in range(2):
+                target[seq, y] = jnp.where(place[CORE] == 0, value[k, :, seq], value[:, k, seq])
+
+    lane = lax.broadcasted_iota(jnp.int32, (1, 16), 1)
+    base = jnp.zeros((1, 16), F32)
+    for head in range(3):
+        base = jnp.where(lane // 2 == head, base_rate[:, head : head + 1], base)
+    rate = base * jax.nn.sigmoid(mm_nt(rows, rate_weight[...]))
+    high = rate.astype(BF16).astype(F32)
+    settle(jnp.where(lane % 2 == 0, high, rate - high), rate_place)
+    rates = [rate_place[seq].reshape(2 * MB, 16).T.astype(BF16) for seq in range(2)]
     for head in range(3):
         parts = [weight[head, spot * HEAD : (spot + 1) * HEAD, :] for spot in (1, 2, 0)]
-        value = mm_nt(rows, jnp.concatenate(parts, axis=0))
-        rate = rates[:, head : head + 1]
-        high = rate.astype(BF16).astype(F32)
-        tail = jnp.where(lane == 0, high, jnp.where(lane == 1, rate - high, 0.0))
-        value = jnp.concatenate([value, tail], axis=1).reshape(SIDE, SIDE, 2, 8, 256)
-        for k in range(SIDE):
-            y = lax.rem(place[Y] + k, SIDE)
-            for seq in range(2):
-                by_place[seq, y] = jnp.where(
-                    place[CORE] == 0, value[k, :, seq], value[:, k, seq]
-                )
+        settle(mm_nt(rows, jnp.concatenate(parts, axis=0)), by_place)
         for seq in range(2):
             target = place[SEAT + 3 * seq + head]
-            block = by_place[seq].reshape(2 * MB, 256)
+            block = by_place[seq].reshape(2 * MB, 3 * HEAD)
             pairs[target, 0 : 2 * MB] = block[:, 0 : 2 * HEAD].astype(BF16)
-            pairs[target, 2 * MB :] = mm_nt(pick, block[:, 2 * HEAD :].astype(BF16)).astype(BF16)
+            pairs[target, 2 * MB :] = rates[seq]
             for part in range(2):
                 queries[target, :, part * HEAD : (part + 1) * HEAD] = block[
-                    part * MB : (part + 1) * MB, 2 * HEAD : 3 * HEAD
+                    part * MB : (part + 1) * MB, 2 * HEAD :
                 ].astype(BF16)
 
 
@@ -150,11 +160,11 @@
     return (q.astype(F32) + (gain * ((outer - m) * s) + shift)).astype(BF16)
 
 
-def advance(pairs, w1, c1, w2t, c2, gain, shift, rates, visit):
+def advance(pairs, own, w1, c1, w2t, c2, gain, shift, rates, visit):
     gain2 = gain * gain
     g_mean = mean_last(gain2)
     line = lax.broadcasted_iota(jnp.int32, (16, HEAD), 0)
-    rate_sum = jnp.where(line < 2, 1.0, 0.0).astype(BF16)
+    rate_sum = jnp.where(line // 2 == own, 1.0, 0.0).astype(BF16)
     for row in range(ROWS):
         rates[row] = mm_tn(pairs[row, 2 * MB :, :], rate_sum)
 
@@ -228,6 +238,7 @@
 
         w1, c1, w2t, c2 = advance(
             pairs,
+            place[OWN],
             w1_in[place[OWN]],
             c1_in[own],
             w2t,
@@ -275,6 +286,7 @@
         bias = state[128:144].astype(F32)
         advance(
             pairs,
+            place[OWN],
             state[0:64].astype(F32),
             bias[0:1] + bias[1:2],
             state[64:128].astype(F32),
@@ -296,7 +308,7 @@
             rows = jnp.concatenate(rows, axis=1).reshape(2, SIDE, 8, 3 * HEAD)
             by_place[seq, 2 * half : 2 * half + 2] = rows
     turns = [
-        [by_place[seq, lax.rem(place[Y] + k, SIDE)] for seq in range(2)] for k in range(SIDE)
+        [by_place[seq, line_y(place, k)] for seq in range(2)] for k in range(SIDE)
     ]
     for k in range(SIDE):
         first = jnp.stack(turns[k], axis=1)
@@ -362,19 +374,21 @@
     one, three, two = (from_side(own, 0, ahead) for ahead in (1, 3, 2))
     low, high = jnp.stack([own, one]), jnp.stack([two, three])
     low_one, low_three = from_side(low, 1, 1), from_side(low, 1, 3)
-    high_three, high_one = from_side(high, 1, 3), from_side(high, 1, 1)
-    low_two, high_two = from_side(low_one, 1, 1), from_side(high_three, 1, 3)
+    high_one, high_three = from_side(high, 1, 1), from_side(high, 1, 3)
+    low_two, high_two = from_side(low_three, 1, 1), from_side(high_one, 1, 3)
     in_hbm = pl.BlockSpec(memory_space=pltpu.HBM)
     sources = tuple(
-        pltpu.with_memory_space_constraint(value, pltpu.HBM)
-        for value in (qkv_weight, rate_weight, base_rate[None])
+        pltpu.with_memory_space_constraint(value, pltpu.HBM) for value in (qkv_weight, rate_weight)
     )
     fetched = pl.pallas_call(
         fetch_kernel,
-        out_shape=tuple(jax.ShapeDtypeStruct(value.shape, value.dtype) for value in sources),
-        in_specs=[pl.BlockSpec(memory_space=pl.ANY)] + [in_hbm] * 3,
-        out_specs=in_vmem(3),
-        scratch_shapes=[pltpu.SemaphoreType.DMA((3,))],
+        out_shape=(
+            jax.ShapeDtypeStruct(qkv_weight.shape, BF16),
+            jax.ShapeDtypeStruct((16, width), BF16),
+        ),
+        in_specs=[pl.BlockSpec(memory_space=pl.ANY)] + [in_hbm] * 2,
+        out_specs=in_vmem(2),
+        scratch_shapes=[pltpu.VMEM((3, width), BF16), pltpu.SemaphoreType.DMA((2,))],
         compiler_params=pltpu.CompilerParams(vmem_limit_bytes=24 << 20),
         cost_estimate=pl.CostEstimate(flops=0, bytes_accessed=4 << 20, transcendentals=0),
         name="fetch",
@@ -385,8 +399,11 @@
         project_kernel,
         (jax.ShapeDtypeStruct((ROWS, 2 * MB + 16, 2 * HEAD), BF16), answer_shape),
         2 * SIDE + 3,
-        scratch=[pltpu.VMEM((2, SIDE, SIDE, 8, 256), F32)],
-    )(place, *pieces, *fetched)
+        scratch=[
+            pltpu.VMEM((2, SIDE, SIDE, 8, 3 * HEAD), F32),
+            pltpu.VMEM((2, SIDE, SIDE, 8, 16), F32),
+        ],
+    )(place, *pieces, *fetched, base_rate[None])
     pairs = exchange(pairs)
     rates = pltpu.VMEM((ROWS, 2 * MB, HEAD), F32)
     state, weights, biases = kernel_call(
@@ -417,21 +434,18 @@
     pair = jax.ShapeDtypeStruct((2, 16, width), BF16)
     single = jax.ShapeDtypeStruct((16, width), BF16)
     parts = kernel_call(
-        mix_kernel,
-        (pair,) * (2 * SIDE),
-        2,
-        scratch=[pltpu.VMEM((2, SIDE, SIDE, 8, 3 * HEAD), F32)],
+        mix_kernel, (pair,) * (2 * SIDE), 2, scratch=[pltpu.VMEM((2, SIDE, SIDE, 8, 3 * HEAD), F32)]
     )(place, exchange(answers), out_weight)
     low, high, low_one, high_one, low_two, high_two, low_three, high_three = parts
     add = kernel_call(pair_kernel, pair, 2, 0)
-    passing_one, passing_three = from_side(low_two, 1, 3), from_side(high_two, 1, 1)
-    high_one, low_three = from_side(high_one, 1, 3), from_side(low_three, 1, 1)
-    low_one = from_side(add(low_one, passing_one), 1, 3)
-    high_three = from_side(add(high_three, passing_three), 1, 1)
+    passing_three, passing_one = from_side(low_two, 1, 1), from_side(high_two, 1, 3)
+    low_one, high_three = from_side(low_one, 1, 1), from_side(high_three, 1, 3)
+    low_three = from_side(add(low_three, passing_three), 1, 3)
+    high_one = from_side(add(high_one, passing_one), 1, 1)
     line = kernel_call(line_kernel, (single,) * SIDE, 6, 0)(
         low, high, low_one, high_one, low_three, high_three
     )
-    far = [from_side(line[k], 0, SIDE - k) for k in (1, 3, 2)]
+    far = [from_side(line[k], 0, k) for k in (1, 3, 2)]
     mixed = kernel_call(last_kernel, single, SIDE, 0)(line[0], *far)
     return mixed.reshape(seqs, own_rows, width)
 

time: 109 us -> 106 us (0.972)
  the two profiles are of different devices: /device:TPU:152 before, /device:TPU:128 now
where the time goes in v2:
time: 106 us; the launch traced here: 105 us
  blocking collectives  31.8 us (30%)
  starting transfers between devices  30.7 us (29%)
  waiting for transfers between devices  22.2 us (21%)
  Pallas kernels  18.9 us (18%)
    all_to_all x2, blocking collectives, exchange(): lax.all_to_all(value, 'seq', 0, 0, axis_index_groups=GROUPS, tiled=True)  31.8 us
    ppermute x18, starting transfers between devices, from_side(): return lax.ppermute(value, ('seq', 'tensor'), pairs)  26.7 us
    ppermute x18, waiting for transfers between devices, from_side(): return lax.ppermute(value, ('seq', 'tensor'), pairs)  16.2 us
    pallas_call x1, Pallas kernels, shards(): kernel_call(second_kernel, answer_shape, 7, scratch=[rates])  10.6 us
    all_to_all x1, waiting for transfers between devices, exchange(): lax.all_to_all(value, 'seq', 0, 0, axis_index_groups=GROUPS, tiled=True)  6 us
    all_to_all x1, starting transfers between devices, exchange(): lax.all_to_all(value, 'seq', 0, 0, axis_index_groups=GROUPS, tiled=True)  3.38 us
    pallas_call x1, Pallas kernels, shards(): kernel_call(project_kernel, (jax.ShapeDtypeStruct((ROWS, 2 * MB + 16, 2 *...  3.16 us
  transfers between devices with their start and end apart: 20, of which 13 were waited for; matrix products, arithmetic and copies ran while one was open for 1% of the time, Pallas kernels for 2%

profile of v2, /device:TPU:128, one launch (start us, length us, event | category | flops | bytes accessed | tf_op | source)
XLA Modules:
  0.0 105.5 jit_solution(7513765097879838644)
XLA Ops:
  0.0 0.7 dynamic-slice_bitcast_fusion.place
  0.7 1.5 %collective-permute-start = (bf16[16,3072]{1,0:T(8,128)(2,1)}, bf16[16,3072]{1,0:T(8,128)(2,1)S(1)}, u32[]{:S(2)}, u32[]{:S(2)}) collective-permute-start(bf16[16,3072]{1,0:T(8,128)(2,1)} %bitcast.12), channel_id=1, source_target_pairs={{1,0},{0,1},{3,2},{2,3},{5,4},{4,5},{7,6},{6,7},{9,8},{8,9},{11,10... | collective-permute-start | bytes 294920 | tf_op jit(solution)/shard_map/ppermute | solution.py:80
  2.2 2.1 %collective-permute-start.2 = (bf16[16,3072]{1,0:T(8,128)(2,1)}, bf16[16,3072]{1,0:T(8,128)(2,1)S(1)}, u32[]{:S(2)}, u32[]{:S(2)}) collective-permute-start(bf16[16,3072]{1,0:T(8,128)(2,1)} %bitcast.13), channel_id=1, source_target_pairs={{3,0},{2,1},{1,2},{0,3},{7,4},{6,5},{5,6},{4,7},{11,8},{10,9},{9,1... | collective-permute-start | bytes 294920 | tf_op jit(solution)/shard_map/ppermute | solution.py:80
  4.3 0.6 collective-permute-start.1
  5.5 0.9 pad_maximum_fusion.refs_0_
  6.5 3.1 %collective-permute-start.5 = (bf16[2,16,3072]{2,1,0:T(8,128)(2,1)S(1)}, bf16[2,16,3072]{2,1,0:T(8,128)(2,1)S(1)}, u32[]{:S(2)}, u32[]{:S(2)}) collective-permute-start(bf16[2,16,3072]{2,1,0:T(8,128)(2,1)S(1)} %pad_maximum_fusion.refs_0_), channel_id=1, source_target_pairs={{12,0},{13,1},{14,2},{15,3},{8,4},{9,5},{10,6},{11,7},{4,8},{5,9},... | collective-permute-start | bytes 589832 | tf_op jit(solution)/shard_map/ppermute | solution.py:80
  9.6 1.2 %collective-permute-done.1 = bf16[16,3072]{1,0:T(8,128)(2,1)S(1)} collective-permute-done((bf16[16,3072]{1,0:T(8,128)(2,1)}, bf16[16,3072]{1,0:T(8,128)(2,1)S(1)}, u32[]{:S(2)}, u32[]{:S(2)}) %collective-permute-start.1) | collective-permute-done | bytes 98336 | tf_op jit(solution)/shard_map/ppermute | solution.py:80
  10.8 1.7 %collective-permute-start.4 = (bf16[2,16,3072]{2,1,0:T(8,128)(2,1)S(1)}, bf16[2,16,3072]{2,1,0:T(8,128)(2,1)S(1)}, u32[]{:S(2)}, u32[]{:S(2)}) collective-permute-start(bf16[2,16,3072]{2,1,0:T(8,128)(2,1)S(1)} %pad_maximum_fusion.1.after.refs_1_), channel_id=1, source_target_pairs={{4,0},{5,1},{6,2},{7,3},{0,4},{1,5},{2,6},{3,7},{12,8},{13,9},{14,... | collective-permute-start | bytes 589832 | tf_op jit(solution)/shard_map/ppermute | solution.py:80
  12.9 3.0 %collective-permute-start.8 = (bf16[2,16,3072]{2,1,0:T(8,128)(2,1)S(1)}, bf16[2,16,3072]{2,1,0:T(8,128)(2,1)S(1)}, u32[]{:S(2)}, u32[]{:S(2)}) collective-permute-start(bf16[2,16,3072]{2,1,0:T(8,128)(2,1)S(1)} %pad_maximum_fusion.1.after.refs_1_), channel_id=1, source_target_pairs={{12,0},{13,1},{14,2},{15,3},{8,4},{9,5},{10,6},{11,7},{4,8},{5,9},... | collective-permute-start | bytes 589832 | tf_op jit(solution)/shard_map/ppermute | solution.py:80
  16.5 3.0 %collective-permute-start.7 = (bf16[2,16,3072]{2,1,0:T(8,128)(2,1)S(1)}, bf16[2,16,3072]{2,1,0:T(8,128)(2,1)S(1)}, u32[]{:S(2)}, u32[]{:S(2)}) collective-permute-start(bf16[2,16,3072]{2,1,0:T(8,128)(2,1)S(1)} %collective-permute-done.4.refs_3_), channel_id=1, source_target_pairs={{12,0},{13,1},{14,2},{15,3},{8,4},{9,5},{10,6},{11,7},{4,8},{5,9},... | collective-permute-start | bytes 589832 | tf_op jit(solution)/shard_map/ppermute | solution.py:80
  19.5 2.0 %fetch.1 = (bf16[3,192,3072]{2,1,0:T(8,128)(2,1)S(1)}, bf16[16,3072]{1,0:T(8,128)(2,1)S(1)}) custom-call(bf16[2,16,3072]{2,1,0:T(8,128)(2,1)S(1)} %pad_maximum_fusion.1.after.refs_1_, bf16[3,192,3072]{2,1,0:T(8,128)(2,1)} %weight_in.1, bf16[3,3072]{1,0:T(4,128)(2,1)} %rate_weight_in.1), custom_call_target="tpu_custom_call" | custom-call | bytes 4194304 | tf_op jit(solution)/shard_map/fetch/pallas_call | solution.py:383
  21.7 1.7 %collective-permute-done.7.refs_5_ = bf16[2,16,3072]{2,1,0:T(8,128)(2,1)S(1)} collective-permute-done((bf16[2,16,3072]{2,1,0:T(8,128)(2,1)S(1)}, bf16[2,16,3072]{2,1,0:T(8,128)(2,1)S(1)}, u32[]{:S(2)}, u32[]{:S(2)}) %collective-permute-start.7) | collective-permute-done | bytes 196640 | tf_op jit(solution)/shard_map/ppermute | solution.py:80
  23.4 3.2 %shard_map.118 = (bf16[8,144,128]{2,1,0:T(8,128)(2,1)S(1)}, bf16[8,64,128]{2,1,0:T(8,128)(2,1)}) custom-call(s32[10]{0:T(128)S(1)} %dynamic-slice_bitcast_fusion.place, bf16[2,16,3072]{2,1,0:T(8,128)(2,1)S(1)} %pad_maximum_fusion.refs_0_, bf16[2,16,3072]{2,1,0:T(8,128)(2,1)S(1)} %pad_maximum_fusion.1.after.refs_1_, ...), custom_call_target="tpu_custom_call" | custom-call | tf_op jit(solution)/shard_map/pallas_call | solution.py:398
  26.6 13.4 %all_to_all.15.pairs = bf16[8,144,128]{2,1,0:T(8,128)(2,1)S(1)} all-to-all(bf16[8,144,128]{2,1,0:T(8,128)(2,1)S(1)} %get-tuple-element.32), channel_id=1, replica_groups={{0,16,32,48,64,80,96,112},{128,144,160,176,192,208,224,240},{1,17,33,49..., dimensions={0} | all-to-all | bytes 589824 | tf_op jit(solution)/shard_map/all_to_all | solution.py:354
  40.6 3.4 %all-to-all-start.1 = ((bf16[8,64,128]{2,1,0:T(8,128)(2,1)}), bf16[8,64,128]{2,1,0:T(8,128)(2,1)S(1)}, u32[]{:S(2)}, u32[]{:S(2)}) async-start(bf16[8,64,128]{2,1,0:T(8,128)(2,1)} %get-tuple-element.35), calls=%async_computation.1 | async-start | bytes 262144 | tf_op jit(solution)/shard_map/all_to_all | solution.py:354
  43.9 0.7 collective-permute-start.9
  44.6 6.0 %all-to-all-done.1.queries = bf16[8,64,128]{2,1,0:T(8,128)(2,1)S(1)} async-done(((bf16[8,64,128]{2,1,0:T(8,128)(2,1)}), bf16[8,64,128]{2,1,0:T(8,128)(2,1)S(1)}, u32[]{:S(2)}, u32[]{:S(2)}) %all-to-all-start.1) | async-done | bytes 131104 | tf_op jit(solution)/shard_map/all_to_all | solution.py:354
  50.6 10.6 %shard_map.120 = bf16[8,64,128]{2,1,0:T(8,128)(2,1)S(1)} custom-call(s32[10]{0:T(128)S(1)} %dynamic-slice_bitcast_fusion.place, bf16[8,144,128]{2,1,0:T(8,128)(2,1)S(1)} %all_to_all.15.pairs, bf16[8,64,128]{2,1,0:T(8,128)(2,1)S(1)} %all-to-all-done.1.queries, bf16[144,256]{1,0:T(8,128)(2,1)S(1)} %collective-permute-done.9.state, f32[3,64]{1,0:T(4,128)S(1)} %copy-done.3, ...), custom_call_target="tpu_custom_call" | custom-call | tf_op jit(solution)/shard_map/pallas_call | solution.py:431
  61.2 18.4 %all_to_all.16.answers = bf16[8,64,128]{2,1,0:T(8,128)(2,1)S(1)} all-to-all(bf16[8,64,128]{2,1,0:T(8,128)(2,1)S(1)} %shard_map.120), channel_id=1, replica_groups={{0,16,32,48,64,80,96,112},{128,144,160,176,192,208,224,240},{1,17,33,49..., dimensions={0} | all-to-all | bytes 262144 | tf_op jit(solution)/shard_map/all_to_all | solution.py:354
  79.6 1.6 %shard_map.121 = (bf16[2,16,3072]{2,1,0:T(8,128)(2,1)S(1)}, bf16[2,16,3072]{2,1,0:T(8,128)(2,1)S(1)}, bf16[2,16,3072]{2,1,0:T(8,128)(2,1)S(1)}, bf16[2,16,3072]{...) custom-call(s32[10]{0:T(128)S(1)} %dynamic-slice_bitcast_fusion.plac, ...), custom_call_target="tpu_custom_call" | custom-call | tf_op jit(solution)/shard_map/pallas_call | solution.py:436
  81.3 3.1 %collective-permute-start.11 = (bf16[2,16,3072]{2,1,0:T(8,128)(2,1)S(1)}, bf16[2,16,3072]{2,1,0:T(8,128)(2,1)S(1)}, u32[]{:S(2)}, u32[]{:S(2)}) collective-permute-start(bf16[2,16,3072]{2,1,0:T(8,128)(2,1)S(1)} %get-tuple-element.43), channel_id=1, source_target_pairs={{12,0},{13,1},{14,2},{15,3},{8,4},{9,5},{10,6},{11,7},{4,8},{5,9},... | collective-permute-start | bytes 589832 | tf_op jit(solution)/shard_map/ppermute | solution.py:80
  84.4 2.0 %collective-permute-start.10 = (bf16[2,16,3072]{2,1,0:T(8,128)(2,1)S(1)}, bf16[2,16,3072]{2,1,0:T(8,128)(2,1)S(1)}, u32[]{:S(2)}, u32[]{:S(2)}) collective-permute-start(bf16[2,16,3072]{2,1,0:T(8,128)(2,1)S(1)} %get-tuple-element.41), channel_id=1, source_target_pairs={{4,0},{5,1},{6,2},{7,3},{0,4},{1,5},{2,6},{3,7},{12,8},{13,9},{14,... | collective-permute-start | bytes 589832 | tf_op jit(solution)/shard_map/ppermute | solution.py:80
  86.6 1.6 %collective-permute-done.11.right = bf16[2,16,3072]{2,1,0:T(8,128)(2,1)S(1)} collective-permute-done((bf16[2,16,3072]{2,1,0:T(8,128)(2,1)S(1)}, bf16[2,16,3072]{2,1,0:T(8,128)(2,1)S(1)}, u32[]{:S(2)}, u32[]{:S(2)}) %collective-permute-start.11) | collective-permute-done | bytes 196640 | tf_op jit(solution)/shard_map/ppermute | solution.py:80
  88.4 1.7 %collective-permute-done.13.right = bf16[2,16,3072]{2,1,0:T(8,128)(2,1)S(1)} collective-permute-done((bf16[2,16,3072]{2,1,0:T(8,128)(2,1)S(1)}, bf16[2,16,3072]{2,1,0:T(8,128)(2,1)S(1)}, u32[]{:S(2)}, u32[]{:S(2)}) %collective-permute-start.13) | collective-permute-done | bytes 196640 | tf_op jit(solution)/shard_map/ppermute | solution.py:80
  90.1 1.5 %collective-permute-start.14 = (bf16[2,16,3072]{2,1,0:T(8,128)(2,1)S(1)}, bf16[2,16,3072]{2,1,0:T(8,128)(2,1)S(1)}, u32[]{:S(2)}, u32[]{:S(2)}) collective-permute-start(bf16[2,16,3072]{2,1,0:T(8,128)(2,1)S(1)} %shard_map.123), channel_id=1, source_target_pairs={{12,0},{13,1},{14,2},{15,3},{8,4},{9,5},{10,6},{11,7},{4,8},{5,9},... | collective-permute-start | bytes 589832 | tf_op jit(solution)/shard_map/ppermute | solution.py:80
  92.2 1.1 %collective-permute-done.15.refs_5_ = bf16[2,16,3072]{2,1,0:T(8,128)(2,1)S(1)} collective-permute-done((bf16[2,16,3072]{2,1,0:T(8,128)(2,1)S(1)}, bf16[2,16,3072]{2,1,0:T(8,128)(2,1)S(1)}, u32[]{:S(2)}, u32[]{:S(2)}) %collective-permute-start.15) | collective-permute-done | bytes 196640 | tf_op jit(solution)/shard_map/ppermute | solution.py:80
  93.3 1.0 collective-permute-done.12.refs_3_
  94.3 2.8 %collective-permute-done.14.refs_4_ = bf16[2,16,3072]{2,1,0:T(8,128)(2,1)S(1)} collective-permute-done((bf16[2,16,3072]{2,1,0:T(8,128)(2,1)S(1)}, bf16[2,16,3072]{2,1,0:T(8,128)(2,1)S(1)}, u32[]{:S(2)}, u32[]{:S(2)}) %collective-permute-start.14) | collective-permute-done | bytes 196640 | tf_op jit(solution)/shard_map/ppermute | solution.py:80
  97.2 0.7 collective-permute-start.16
  98.5 2.9 %collective-permute-start.18 = (bf16[16,3072]{1,0:T(8,128)(2,1)S(1)}, bf16[16,3072]{1,0:T(8,128)(2,1)S(1)}, u32[]{:S(2)}, u32[]{:S(2)}) collective-permute-start(bf16[16,3072]{1,0:T(8,128)(2,1)S(1)} %get-tuple-element.50), channel_id=1, source_target_pairs={{2,0},{3,1},{0,2},{1,3},{6,4},{7,5},{4,6},{5,7},{10,8},{11,9},{8,1... | collective-permute-start | bytes 294920 | tf_op jit(solution)/shard_map/ppermute | solution.py:80
  101.9 2.9 %collective-permute-done.17.refs_2_ = bf16[16,3072]{1,0:T(8,128)(2,1)S(1)} collective-permute-done((bf16[16,3072]{1,0:T(8,128)(2,1)S(1)}, bf16[16,3072]{1,0:T(8,128)(2,1)S(1)}, u32[]{:S(2)}, u32[]{:S(2)}) %collective-permute-start.17) | collective-permute-done | bytes 98336 | tf_op jit(solution)/shard_map/ppermute | solution.py:80
  104.8 0.7 shard_map.125
  (38 shorter events, 4.5 us)
Async XLA Ops:
  0.0 23.4 %copy-start.7 = (f32[3]{0:T(128)S(1)}, f32[3]{0:T(128)}, u32[]{:S(2)}) copy-start(f32[3]{0:T(128)} %param.15) | copy-start | bytes 40
  0.7 4.8 %collective-permute-start = (bf16[16,3072]{1,0:T(8,128)(2,1)}, bf16[16,3072]{1,0:T(8,128)(2,1)S(1)}, u32[]{:S(2)}, u32[]{:S(2)}) collective-permute-start(bf16[16,3072]{1,0:T(8,128)(2,1)} %bitcast.12), channel_id=1, source_target_pairs={{1,0},{0,1},{3,2},{2,3},{5,4},{4,5},{7,6},{6,7},{9,8},{8,9},{11,10... | collective-permute-start | bytes 294920 | tf_op jit(solution)/shard_map/ppermute | solution.py:80
  2.2 7.4 %collective-permute-start.2 = (bf16[16,3072]{1,0:T(8,128)(2,1)}, bf16[16,3072]{1,0:T(8,128)(2,1)S(1)}, u32[]{:S(2)}, u32[]{:S(2)}) collective-permute-start(bf16[16,3072]{1,0:T(8,128)(2,1)} %bitcast.13), channel_id=1, source_target_pairs={{3,0},{2,1},{1,2},{0,3},{7,4},{6,5},{5,6},{4,7},{11,8},{10,9},{9,1... | collective-permute-start | bytes 294920 | tf_op jit(solution)/shard_map/ppermute | solution.py:80
  4.3 6.4 %collective-permute-start.1 = (bf16[16,3072]{1,0:T(8,128)(2,1)}, bf16[16,3072]{1,0:T(8,128)(2,1)S(1)}, u32[]{:S(2)}, u32[]{:S(2)}) collective-permute-start(bf16[16,3072]{1,0:T(8,128)(2,1)} %bitcast.14), channel_id=1, source_target_pairs={{2,0},{3,1},{0,2},{1,3},{6,4},{7,5},{4,6},{5,7},{10,8},{11,9},{8,1... | collective-permute-start | bytes 294920 | tf_op jit(solution)/shard_map/ppermute | solution.py:80
  6.5 9.4 %collective-permute-start.5 = (bf16[2,16,3072]{2,1,0:T(8,128)(2,1)S(1)}, bf16[2,16,3072]{2,1,0:T(8,128)(2,1)S(1)}, u32[]{:S(2)}, u32[]{:S(2)}) collective-permute-start(bf16[2,16,3072]{2,1,0:T(8,128)(2,1)S(1)} %pad_maximum_fusion.refs_0_), channel_id=1, source_target_pairs={{12,0},{13,1},{14,2},{15,3},{8,4},{9,5},{10,6},{11,7},{4,8},{5,9},... | collective-permute-start | bytes 589832 | tf_op jit(solution)/shard_map/ppermute | solution.py:80
  10.8 5.8 %collective-permute-start.4 = (bf16[2,16,3072]{2,1,0:T(8,128)(2,1)S(1)}, bf16[2,16,3072]{2,1,0:T(8,128)(2,1)S(1)}, u32[]{:S(2)}, u32[]{:S(2)}) collective-permute-start(bf16[2,16,3072]{2,1,0:T(8,128)(2,1)S(1)} %pad_maximum_fusion.1.after.refs_1_), channel_id=1, source_target_pairs={{4,0},{5,1},{6,2},{7,3},{0,4},{1,5},{2,6},{3,7},{12,8},{13,9},{14,... | collective-permute-start | bytes 589832 | tf_op jit(solution)/shard_map/ppermute | solution.py:80
  12.4 9.2 %collective-permute-start.3 = (bf16[2,16,3072]{2,1,0:T(8,128)(2,1)S(1)}, bf16[2,16,3072]{2,1,0:T(8,128)(2,1)S(1)}, u32[]{:S(2)}, u32[]{:S(2)}) collective-permute-start(bf16[2,16,3072]{2,1,0:T(8,128)(2,1)S(1)} %pad_maximum_fusion.refs_0_), channel_id=1, source_target_pairs={{4,0},{5,1},{6,2},{7,3},{0,4},{1,5},{2,6},{3,7},{12,8},{13,9},{14,... | collective-permute-start | bytes 589832 | tf_op jit(solution)/shard_map/ppermute | solution.py:80
  12.9 8.8 %collective-permute-start.8 = (bf16[2,16,3072]{2,1,0:T(8,128)(2,1)S(1)}, bf16[2,16,3072]{2,1,0:T(8,128)(2,1)S(1)}, u32[]{:S(2)}, u32[]{:S(2)}) collective-permute-start(bf16[2,16,3072]{2,1,0:T(8,128)(2,1)S(1)} %pad_maximum_fusion.1.after.refs_1_), channel_id=1, source_target_pairs={{12,0},{13,1},{14,2},{15,3},{8,4},{9,5},{10,6},{11,7},{4,8},{5,9},... | collective-permute-start | bytes 589832 | tf_op jit(solution)/shard_map/ppermute | solution.py:80
  15.9 5.8 %collective-permute-start.6 = (bf16[2,16,3072]{2,1,0:T(8,128)(2,1)S(1)}, bf16[2,16,3072]{2,1,0:T(8,128)(2,1)S(1)}, u32[]{:S(2)}, u32[]{:S(2)}) collective-permute-start(bf16[2,16,3072]{2,1,0:T(8,128)(2,1)S(1)} %collective-permute-done.5.refs_6_), channel_id=1, source_target_pairs={{4,0},{5,1},{6,2},{7,3},{0,4},{1,5},{2,6},{3,7},{12,8},{13,9},{14,... | collective-permute-start | bytes 589832 | tf_op jit(solution)/shard_map/ppermute | solution.py:80
  16.5 6.9 %collective-permute-start.7 = (bf16[2,16,3072]{2,1,0:T(8,128)(2,1)S(1)}, bf16[2,16,3072]{2,1,0:T(8,128)(2,1)S(1)}, u32[]{:S(2)}, u32[]{:S(2)}) collective-permute-start(bf16[2,16,3072]{2,1,0:T(8,128)(2,1)S(1)} %collective-permute-done.4.refs_3_), channel_id=1, source_target_pairs={{12,0},{13,1},{14,2},{15,3},{8,4},{9,5},{10,6},{11,7},{4,8},{5,9},... | collective-permute-start | bytes 589832 | tf_op jit(solution)/shard_map/ppermute | solution.py:80
  21.6 18.4 %copy-start.1 = (f32[3,64,256]{2,1,0:T(8,128)S(1)}, f32[3,64,256]{2,1,0:T(8,128)}, u32[]{:S(2)}) copy-start(f32[3,64,256]{2,1,0:T(8,128)} %w1_in.1) | copy-start | bytes 589828
  21.6 18.4 %copy-start.2 = (f32[3,256,64]{1,2,0:T(8,128)S(1)}, f32[3,256,64]{1,2,0:T(8,128)}, u32[]{:S(2)}) copy-start(f32[3,256,64]{1,2,0:T(8,128)} %param.18) | copy-start | bytes 589828
  21.6 18.4 %copy-start.3 = (f32[3,64]{1,0:T(4,128)S(1)}, f32[3,64]{1,0:T(4,128)}, u32[]{:S(2)}) copy-start(f32[3,64]{1,0:T(4,128)} %gain_in.3) | copy-start | bytes 2308
  21.6 18.4 %copy-start.4 = (f32[3,64]{1,0:T(4,128)S(1)}, f32[3,64]{1,0:T(4,128)}, u32[]{:S(2)}) copy-start(f32[3,64]{1,0:T(4,128)} %shift_in.3) | copy-start | bytes 2308
  21.6 18.4 %copy-start.5 = (f32[3,256]{1,0:T(4,128)S(1)}, f32[3,256]{1,0:T(4,128)}, u32[]{:S(2)}) copy-start(f32[3,256]{1,0:T(4,128)} %c1_in.1) | copy-start | bytes 9220
  21.6 18.4 %copy-start.6 = (f32[3,64]{1,0:T(4,128)S(1)}, f32[3,64]{1,0:T(4,128)}, u32[]{:S(2)}) copy-start(f32[3,64]{1,0:T(4,128)} %c2_in.1) | copy-start | bytes 2308
  23.4 56.3 %copy-start = (bf16[192,3072]{1,0:T(8,128)(2,1)S(1)}, bf16[192,3072]{1,0:T(8,128)(2,1)}, u32[]{:S(2)}) copy-start(bf16[192,3072]{1,0:T(8,128)(2,1)} %weight.1) | copy-start | bytes 3538948
  40.6 10.1 %all-to-all-start.1 = ((bf16[8,64,128]{2,1,0:T(8,128)(2,1)}), bf16[8,64,128]{2,1,0:T(8,128)(2,1)S(1)}, u32[]{:S(2)}, u32[]{:S(2)}) async-start(bf16[8,64,128]{2,1,0:T(8,128)(2,1)} %get-tuple-element.35), calls=%async_computation.1 | async-start | bytes 262144 | tf_op jit(solution)/shard_map/all_to_all | solution.py:354
  43.9 0.7 collective-permute-start.9
  81.3 7.0 %collective-permute-start.11 = (bf16[2,16,3072]{2,1,0:T(8,128)(2,1)S(1)}, bf16[2,16,3072]{2,1,0:T(8,128)(2,1)S(1)}, u32[]{:S(2)}, u32[]{:S(2)}) collective-permute-start(bf16[2,16,3072]{2,1,0:T(8,128)(2,1)S(1)} %get-tuple-element.43), channel_id=1, source_target_pairs={{12,0},{13,1},{14,2},{15,3},{8,4},{9,5},{10,6},{11,7},{4,8},{5,9},... | collective-permute-start | bytes 589832 | tf_op jit(solution)/shard_map/ppermute | solution.py:80
  84.4 5.7 %collective-permute-start.13 = (bf16[2,16,3072]{2,1,0:T(8,128)(2,1)S(1)}, bf16[2,16,3072]{2,1,0:T(8,128)(2,1)S(1)}, u32[]{:S(2)}, u32[]{:S(2)}) collective-permute-start(bf16[2,16,3072]{2,1,0:T(8,128)(2,1)S(1)} %get-tuple-element.45), channel_id=1, source_target_pairs={{4,0},{5,1},{6,2},{7,3},{0,4},{1,5},{2,6},{3,7},{12,8},{13,9},{14,... | collective-permute-start | bytes 589832 | tf_op jit(solution)/shard_map/ppermute | solution.py:80
  84.4 7.8 %collective-permute-start.10 = (bf16[2,16,3072]{2,1,0:T(8,128)(2,1)S(1)}, bf16[2,16,3072]{2,1,0:T(8,128)(2,1)S(1)}, u32[]{:S(2)}, u32[]{:S(2)}) collective-permute-start(bf16[2,16,3072]{2,1,0:T(8,128)(2,1)S(1)} %get-tuple-element.41), channel_id=1, source_target_pairs={{4,0},{5,1},{6,2},{7,3},{0,4},{1,5},{2,6},{3,7},{12,8},{13,9},{14,... | collective-permute-start | bytes 589832 | tf_op jit(solution)/shard_map/ppermute | solution.py:80
  86.4 6.9 %collective-permute-start.15 = (bf16[2,16,3072]{2,1,0:T(8,128)(2,1)S(1)}, bf16[2,16,3072]{2,1,0:T(8,128)(2,1)S(1)}, u32[]{:S(2)}, u32[]{:S(2)}) collective-permute-start(bf16[2,16,3072]{2,1,0:T(8,128)(2,1)S(1)} %get-tuple-element.46), channel_id=1, source_target_pairs={{12,0},{13,1},{14,2},{15,3},{8,4},{9,5},{10,6},{11,7},{4,8},{5,9},... | collective-permute-start | bytes 589832 | tf_op jit(solution)/shard_map/ppermute | solution.py:80
  88.3 6.0 %collective-permute-start.12 = (bf16[2,16,3072]{2,1,0:T(8,128)(2,1)S(1)}, bf16[2,16,3072]{2,1,0:T(8,128)(2,1)S(1)}, u32[]{:S(2)}, u32[]{:S(2)}) collective-permute-start(bf16[2,16,3072]{2,1,0:T(8,128)(2,1)S(1)} %shard_map.122), channel_id=1, source_target_pairs={{4,0},{5,1},{6,2},{7,3},{0,4},{1,5},{2,6},{3,7},{12,8},{13,9},{14,... | collective-permute-start | bytes 589832 | tf_op jit(solution)/shard_map/ppermute | solution.py:80
  90.1 7.0 %collective-permute-start.14 = (bf16[2,16,3072]{2,1,0:T(8,128)(2,1)S(1)}, bf16[2,16,3072]{2,1,0:T(8,128)(2,1)S(1)}, u32[]{:S(2)}, u32[]{:S(2)}) collective-permute-start(bf16[2,16,3072]{2,1,0:T(8,128)(2,1)S(1)} %shard_map.123), channel_id=1, source_target_pairs={{12,0},{13,1},{14,2},{15,3},{8,4},{9,5},{10,6},{11,7},{4,8},{5,9},... | collective-permute-start | bytes 589832 | tf_op jit(solution)/shard_map/ppermute | solution.py:80
  97.2 4.7 %collective-permute-start.16 = (bf16[16,3072]{1,0:T(8,128)(2,1)S(1)}, bf16[16,3072]{1,0:T(8,128)(2,1)S(1)}, u32[]{:S(2)}, u32[]{:S(2)}) collective-permute-start(bf16[16,3072]{1,0:T(8,128)(2,1)S(1)} %get-tuple-element.48), channel_id=1, source_target_pairs={{1,0},{0,1},{3,2},{2,3},{5,4},{4,5},{7,6},{6,7},{9,8},{8,9},{11,10... | collective-permute-start | bytes 294920 | tf_op jit(solution)/shard_map/ppermute | solution.py:80
  97.9 6.9 %collective-permute-start.17 = (bf16[16,3072]{1,0:T(8,128)(2,1)S(1)}, bf16[16,3072]{1,0:T(8,128)(2,1)S(1)}, u32[]{:S(2)}, u32[]{:S(2)}) collective-permute-start(bf16[16,3072]{1,0:T(8,128)(2,1)S(1)} %get-tuple-element.49), channel_id=1, source_target_pairs={{3,0},{2,1},{1,2},{0,3},{7,4},{6,5},{5,6},{4,7},{11,8},{10,9},{9,1... | collective-permute-start | bytes 294920 | tf_op jit(solution)/shard_map/ppermute | solution.py:80
  98.5 6.3 %collective-permute-start.18 = (bf16[16,3072]{1,0:T(8,128)(2,1)S(1)}, bf16[16,3072]{1,0:T(8,128)(2,1)S(1)}, u32[]{:S(2)}, u32[]{:S(2)}) collective-permute-start(bf16[16,3072]{1,0:T(8,128)(2,1)S(1)} %get-tuple-element.50), channel_id=1, source_target_pairs={{2,0},{3,1},{0,2},{1,3},{6,4},{7,5},{4,6},{5,7},{10,8},{11,9},{8,1... | collective-permute-start | bytes 294920 | tf_op jit(solution)/shard_map/ppermute | solution.py:80

commit v3 on v2

--- a/solution.py
+++ b/solution.py
@@ -133,13 +133,17 @@
     base = jnp.zeros((1, 16), F32)
     for head in range(3):
         base = jnp.where(lane // 2 == head, base_rate[:, head : head + 1], base)
-    rate = base * jax.nn.sigmoid(mm_nt(rows, rate_weight[...]))
-    high = rate.astype(BF16).astype(F32)
-    settle(jnp.where(lane % 2 == 0, high, rate - high), rate_place)
-    rates = [rate_place[seq].reshape(2 * MB, 16).T.astype(BF16) for seq in range(2)]
     for head in range(3):
         parts = [weight[head, spot * HEAD : (spot + 1) * HEAD, :] for spot in (1, 2, 0)]
-        settle(mm_nt(rows, jnp.concatenate(parts, axis=0)), by_place)
+        if head == 0:
+            value = mm_nt(rows, jnp.concatenate(parts + [rate_weight[...]], axis=0))
+            rate = base * jax.nn.sigmoid(value[:, 3 * HEAD :])
+            high = rate.astype(BF16).astype(F32)
+            settle(jnp.where(lane % 2 == 0, high, rate - high), rate_place)
+            rates = [rate_place[seq].reshape(2 * MB, 16).T.astype(BF16) for seq in range(2)]
+            settle(value[:, 0 : 3 * HEAD], by_place)
+        else:
+            settle(mm_nt(rows, jnp.concatenate(parts, axis=0)), by_place)
         for seq in range(2):
             target = place[SEAT + 3 * seq + head]
             block = by_place[seq].reshape(2 * MB, 3 * HEAD)
@@ -181,9 +185,11 @@
         target = gain * (shift - (v.astype(F32) - k.astype(F32)))
         t_mean = mean_last(target)
 
-        square, t, half = gelu_parts(pre)
-        hidden = (half + half * t).astype(BF16)
-        slope = 0.5 + 0.5 * t + half * (1.0 - t * t) * (C0 + (3.0 * C0 * C1) * square)
+        square, t, _ = gelu_parts(pre)
+        share = 0.5 + 0.5 * t
+        gated = pre * share
+        hidden = gated.astype(BF16)
+        slope = share + gated * ((1.0 - t) * (C0 + (3.0 * C0 * C1) * square))
         outer = mm_nt(hidden, w2tb) + c2
         sq = outer * outer
         m = mean_last(outer)
@@ -369,9 +375,8 @@
 ):
     seqs, own_rows, width = tokens.shape
     place = jnp.asarray(routes())[lax.axis_index(("seq", "tensor"))]
-    tokens, place = lax.optimization_barrier((tokens, place))
     own = tokens.reshape(seqs * own_rows, width)
-    one, three, two = (from_side(own, 0, ahead) for ahead in (1, 3, 2))
+    two, one, three = (from_side(own, 0, step) for step in (2, 1, 3))
     low, high = jnp.stack([own, one]), jnp.stack([two, three])
     low_one, low_three = from_side(low, 1, 1), from_side(low, 1, 3)
     high_one, high_three = from_side(high, 1, 1), from_side(high, 1, 3)

time: 106 us -> 105 us (level)
  waiting for transfers between devices: 22.2 us -> 21.1 us
  transfers between devices with their start and end apart: 20 -> 20, of which waited for: 13 -> 13; matrix products, arithmetic and copies ran while one was open for 1% -> 2% of each run, Pallas kernels for 2% -> 2%
where the time goes in v3:
time: 105 us; the launch traced here: 104 us
  blocking collectives  31.8 us (30%)
  starting transfers between devices  31.1 us (30%)
  waiting for transfers between devices  21.1 us (20%)
  Pallas kernels  18.5 us (18%)
    all_to_all x2, blocking collectives, exchange(): lax.all_to_all(value, 'seq', 0, 0, axis_index_groups=GROUPS, tiled=True)  31.8 us
    ppermute x18, starting transfers between devices, from_side(): return lax.ppermute(value, ('seq', 'tensor'), pairs)  27.1 us
    ppermute x18, waiting for transfers between devices, from_side(): return lax.ppermute(value, ('seq', 'tensor'), pairs)  15.1 us
    pallas_call x1, Pallas kernels, shards(): kernel_call(second_kernel, answer_shape, 7, scratch=[rates])  10.5 us
    all_to_all x1, waiting for transfers between devices, exchange(): lax.all_to_all(value, 'seq', 0, 0, axis_index_groups=GROUPS, tiled=True)  6 us
    all_to_all x1, starting transfers between devices, exchange(): lax.all_to_all(value, 'seq', 0, 0, axis_index_groups=GROUPS, tiled=True)  3.38 us
    pallas_call x1, Pallas kernels, shards(): kernel_call(project_kernel, (jax.ShapeDtypeStruct((ROWS, 2 * MB + 16, 2 *...  2.88 us
  transfers between devices with their start and end apart: 20, of which 13 were waited for; matrix products, arithmetic and copies ran while one was open for 2% of the time, Pallas kernels for 2%

profile of v3, /device:TPU:128, one launch (start us, length us, event | category | flops | bytes accessed | tf_op | source)
XLA Modules:
  0.0 104.4 jit_solution(11728061902820102501)
XLA Ops:
  0.0 1.5 %collective-permute-start = (bf16[16,3072]{1,0:T(8,128)(2,1)}, bf16[16,3072]{1,0:T(8,128)(2,1)S(1)}, u32[]{:S(2)}, u32[]{:S(2)}) collective-permute-start(bf16[16,3072]{1,0:T(8,128)(2,1)} %bitcast.12), channel_id=1, source_target_pairs={{1,0},{0,1},{3,2},{2,3},{5,4},{4,5},{7,6},{6,7},{9,8},{8,9},{11,10... | collective-permute-start | bytes 294920 | tf_op jit(solution)/shard_map/ppermute | solution.py:80
  1.5 2.1 %collective-permute-start.2 = (bf16[16,3072]{1,0:T(8,128)(2,1)}, bf16[16,3072]{1,0:T(8,128)(2,1)S(1)}, u32[]{:S(2)}, u32[]{:S(2)}) collective-permute-start(bf16[16,3072]{1,0:T(8,128)(2,1)} %bitcast.13), channel_id=1, source_target_pairs={{3,0},{2,1},{1,2},{0,3},{7,4},{6,5},{5,6},{4,7},{11,8},{10,9},{9,1... | collective-permute-start | bytes 294920 | tf_op jit(solution)/shard_map/ppermute | solution.py:80
  3.6 0.6 collective-permute-start.1
  4.8 0.9 pad_maximum_fusion.refs_0_
  5.7 3.1 %collective-permute-start.5 = (bf16[2,16,3072]{2,1,0:T(8,128)(2,1)S(1)}, bf16[2,16,3072]{2,1,0:T(8,128)(2,1)S(1)}, u32[]{:S(2)}, u32[]{:S(2)}) collective-permute-start(bf16[2,16,3072]{2,1,0:T(8,128)(2,1)S(1)} %pad_maximum_fusion.refs_0_), channel_id=1, source_target_pairs={{12,0},{13,1},{14,2},{15,3},{8,4},{9,5},{10,6},{11,7},{4,8},{5,9},... | collective-permute-start | bytes 589832 | tf_op jit(solution)/shard_map/ppermute | solution.py:80
  8.9 1.2 %collective-permute-done.1 = bf16[16,3072]{1,0:T(8,128)(2,1)S(1)} collective-permute-done((bf16[16,3072]{1,0:T(8,128)(2,1)}, bf16[16,3072]{1,0:T(8,128)(2,1)S(1)}, u32[]{:S(2)}, u32[]{:S(2)}) %collective-permute-start.1) | collective-permute-done | bytes 98336 | tf_op jit(solution)/shard_map/ppermute | solution.py:80
  10.0 1.7 %collective-permute-start.4 = (bf16[2,16,3072]{2,1,0:T(8,128)(2,1)S(1)}, bf16[2,16,3072]{2,1,0:T(8,128)(2,1)S(1)}, u32[]{:S(2)}, u32[]{:S(2)}) collective-permute-start(bf16[2,16,3072]{2,1,0:T(8,128)(2,1)S(1)} %pad_maximum_fusion.1.after.refs_1_), channel_id=1, source_target_pairs={{4,0},{5,1},{6,2},{7,3},{0,4},{1,5},{2,6},{3,7},{12,8},{13,9},{14,... | collective-permute-start | bytes 589832 | tf_op jit(solution)/shard_map/ppermute | solution.py:80
  12.2 3.0 %collective-permute-start.8 = (bf16[2,16,3072]{2,1,0:T(8,128)(2,1)S(1)}, bf16[2,16,3072]{2,1,0:T(8,128)(2,1)S(1)}, u32[]{:S(2)}, u32[]{:S(2)}) collective-permute-start(bf16[2,16,3072]{2,1,0:T(8,128)(2,1)S(1)} %pad_maximum_fusion.1.after.refs_1_), channel_id=1, source_target_pairs={{12,0},{13,1},{14,2},{15,3},{8,4},{9,5},{10,6},{11,7},{4,8},{5,9},... | collective-permute-start | bytes 589832 | tf_op jit(solution)/shard_map/ppermute | solution.py:80
  15.8 3.0 %collective-permute-start.7 = (bf16[2,16,3072]{2,1,0:T(8,128)(2,1)S(1)}, bf16[2,16,3072]{2,1,0:T(8,128)(2,1)S(1)}, u32[]{:S(2)}, u32[]{:S(2)}) collective-permute-start(bf16[2,16,3072]{2,1,0:T(8,128)(2,1)S(1)} %collective-permute-done.4.refs_3_), channel_id=1, source_target_pairs={{12,0},{13,1},{14,2},{15,3},{8,4},{9,5},{10,6},{11,7},{4,8},{5,9},... | collective-permute-start | bytes 589832 | tf_op jit(solution)/shard_map/ppermute | solution.py:80
  18.8 0.7 dynamic-slice_bitcast_fusion.place
  19.5 2.0 %fetch.1 = (bf16[3,192,3072]{2,1,0:T(8,128)(2,1)S(1)}, bf16[16,3072]{1,0:T(8,128)(2,1)S(1)}) custom-call(bf16[2,16,3072]{2,1,0:T(8,128)(2,1)S(1)} %pad_maximum_fusion.1.after.refs_1_, bf16[3,192,3072]{2,1,0:T(8,128)(2,1)} %weight_in.1, bf16[3,3072]{1,0:T(4,128)(2,1)} %rate_weight_in.1), custom_call_target="tpu_custom_call" | custom-call | bytes 4194304 | tf_op jit(solution)/shard_map/fetch/pallas_call | solution.py:388
  21.6 1.0 %collective-permute-done.7.refs_5_ = bf16[2,16,3072]{2,1,0:T(8,128)(2,1)S(1)} collective-permute-done((bf16[2,16,3072]{2,1,0:T(8,128)(2,1)S(1)}, bf16[2,16,3072]{2,1,0:T(8,128)(2,1)S(1)}, u32[]{:S(2)}, u32[]{:S(2)}) %collective-permute-start.7) | collective-permute-done | bytes 196640 | tf_op jit(solution)/shard_map/ppermute | solution.py:80
  22.7 2.9 %shard_map.118 = (bf16[8,144,128]{2,1,0:T(8,128)(2,1)S(1)}, bf16[8,64,128]{2,1,0:T(8,128)(2,1)}) custom-call(s32[10]{0:T(128)S(1)} %dynamic-slice_bitcast_fusion.place, bf16[2,16,3072]{2,1,0:T(8,128)(2,1)S(1)} %pad_maximum_fusion.refs_0_, bf16[2,16,3072]{2,1,0:T(8,128)(2,1)S(1)} %pad_maximum_fusion.1.after.refs_1_, ...), custom_call_target="tpu_custom_call" | custom-call | tf_op jit(solution)/shard_map/pallas_call | solution.py:403
  25.6 13.4 %all_to_all.15.pairs = bf16[8,144,128]{2,1,0:T(8,128)(2,1)S(1)} all-to-all(bf16[8,144,128]{2,1,0:T(8,128)(2,1)S(1)} %get-tuple-element.28), channel_id=1, replica_groups={{0,16,32,48,64,80,96,112},{128,144,160,176,192,208,224,240},{1,17,33,49..., dimensions={0} | all-to-all | bytes 589824 | tf_op jit(solution)/shard_map/all_to_all | solution.py:360
  39.6 3.4 %all-to-all-start.1 = ((bf16[8,64,128]{2,1,0:T(8,128)(2,1)}), bf16[8,64,128]{2,1,0:T(8,128)(2,1)S(1)}, u32[]{:S(2)}, u32[]{:S(2)}) async-start(bf16[8,64,128]{2,1,0:T(8,128)(2,1)} %get-tuple-element.31), calls=%async_computation.1 | async-start | bytes 262144 | tf_op jit(solution)/shard_map/all_to_all | solution.py:360
  42.9 0.7 collective-permute-start.9
  43.6 6.0 %all-to-all-done.1.queries = bf16[8,64,128]{2,1,0:T(8,128)(2,1)S(1)} async-done(((bf16[8,64,128]{2,1,0:T(8,128)(2,1)}), bf16[8,64,128]{2,1,0:T(8,128)(2,1)S(1)}, u32[]{:S(2)}, u32[]{:S(2)}) %all-to-all-start.1) | async-done | bytes 131104 | tf_op jit(solution)/shard_map/all_to_all | solution.py:360
  49.6 10.5 %shard_map.120 = bf16[8,64,128]{2,1,0:T(8,128)(2,1)S(1)} custom-call(s32[10]{0:T(128)S(1)} %dynamic-slice_bitcast_fusion.place, bf16[8,144,128]{2,1,0:T(8,128)(2,1)S(1)} %all_to_all.15.pairs, bf16[8,64,128]{2,1,0:T(8,128)(2,1)S(1)} %all-to-all-done.1.queries, bf16[144,256]{1,0:T(8,128)(2,1)S(1)} %collective-permute-done.9.state, f32[3,64]{1,0:T(4,128)S(1)} %copy-done.3, ...), custom_call_target="tpu_custom_call" | custom-call | tf_op jit(solution)/shard_map/pallas_call | solution.py:436
  60.1 18.5 %all_to_all.16.answers = bf16[8,64,128]{2,1,0:T(8,128)(2,1)S(1)} all-to-all(bf16[8,64,128]{2,1,0:T(8,128)(2,1)S(1)} %shard_map.120), channel_id=1, replica_groups={{0,16,32,48,64,80,96,112},{128,144,160,176,192,208,224,240},{1,17,33,49..., dimensions={0} | all-to-all | bytes 262144 | tf_op jit(solution)/shard_map/all_to_all | solution.py:360
  78.6 1.6 %shard_map.121 = (bf16[2,16,3072]{2,1,0:T(8,128)(2,1)S(1)}, bf16[2,16,3072]{2,1,0:T(8,128)(2,1)S(1)}, bf16[2,16,3072]{2,1,0:T(8,128)(2,1)S(1)}, bf16[2,16,3072]{...) custom-call(s32[10]{0:T(128)S(1)} %dynamic-slice_bitcast_fusion.plac, ...), custom_call_target="tpu_custom_call" | custom-call | tf_op jit(solution)/shard_map/pallas_call | solution.py:441
  80.2 3.1 %collective-permute-start.11 = (bf16[2,16,3072]{2,1,0:T(8,128)(2,1)S(1)}, bf16[2,16,3072]{2,1,0:T(8,128)(2,1)S(1)}, u32[]{:S(2)}, u32[]{:S(2)}) collective-permute-start(bf16[2,16,3072]{2,1,0:T(8,128)(2,1)S(1)} %get-tuple-element.39), channel_id=1, source_target_pairs={{12,0},{13,1},{14,2},{15,3},{8,4},{9,5},{10,6},{11,7},{4,8},{5,9},... | collective-permute-start | bytes 589832 | tf_op jit(solution)/shard_map/ppermute | solution.py:80
  83.3 2.0 %collective-permute-start.10 = (bf16[2,16,3072]{2,1,0:T(8,128)(2,1)S(1)}, bf16[2,16,3072]{2,1,0:T(8,128)(2,1)S(1)}, u32[]{:S(2)}, u32[]{:S(2)}) collective-permute-start(bf16[2,16,3072]{2,1,0:T(8,128)(2,1)S(1)} %get-tuple-element.37), channel_id=1, source_target_pairs={{4,0},{5,1},{6,2},{7,3},{0,4},{1,5},{2,6},{3,7},{12,8},{13,9},{14,... | collective-permute-start | bytes 589832 | tf_op jit(solution)/shard_map/ppermute | solution.py:80
  85.6 1.6 %collective-permute-done.11.right = bf16[2,16,3072]{2,1,0:T(8,128)(2,1)S(1)} collective-permute-done((bf16[2,16,3072]{2,1,0:T(8,128)(2,1)S(1)}, bf16[2,16,3072]{2,1,0:T(8,128)(2,1)S(1)}, u32[]{:S(2)}, u32[]{:S(2)}) %collective-permute-start.11) | collective-permute-done | bytes 196640 | tf_op jit(solution)/shard_map/ppermute | solution.py:80
  87.5 1.5 %collective-permute-done.13.right = bf16[2,16,3072]{2,1,0:T(8,128)(2,1)S(1)} collective-permute-done((bf16[2,16,3072]{2,1,0:T(8,128)(2,1)S(1)}, bf16[2,16,3072]{2,1,0:T(8,128)(2,1)S(1)}, u32[]{:S(2)}, u32[]{:S(2)}) %collective-permute-start.13) | collective-permute-done | bytes 196640 | tf_op jit(solution)/shard_map/ppermute | solution.py:80
  89.1 1.6 %collective-permute-start.14 = (bf16[2,16,3072]{2,1,0:T(8,128)(2,1)S(1)}, bf16[2,16,3072]{2,1,0:T(8,128)(2,1)S(1)}, u32[]{:S(2)}, u32[]{:S(2)}) collective-permute-start(bf16[2,16,3072]{2,1,0:T(8,128)(2,1)S(1)} %shard_map.123), channel_id=1, source_target_pairs={{12,0},{13,1},{14,2},{15,3},{8,4},{9,5},{10,6},{11,7},{4,8},{5,9},... | collective-permute-start | bytes 589832 | tf_op jit(solution)/shard_map/ppermute | solution.py:80
  91.1 1.1 %collective-permute-done.15.refs_5_ = bf16[2,16,3072]{2,1,0:T(8,128)(2,1)S(1)} collective-permute-done((bf16[2,16,3072]{2,1,0:T(8,128)(2,1)S(1)}, bf16[2,16,3072]{2,1,0:T(8,128)(2,1)S(1)}, u32[]{:S(2)}, u32[]{:S(2)}) %collective-permute-start.15) | collective-permute-done | bytes 196640 | tf_op jit(solution)/shard_map/ppermute | solution.py:80
  92.2 1.0 collective-permute-done.12.refs_3_
  93.2 2.8 %collective-permute-done.14.refs_4_ = bf16[2,16,3072]{2,1,0:T(8,128)(2,1)S(1)} collective-permute-done((bf16[2,16,3072]{2,1,0:T(8,128)(2,1)S(1)}, bf16[2,16,3072]{2,1,0:T(8,128)(2,1)S(1)}, u32[]{:S(2)}, u32[]{:S(2)}) %collective-permute-start.14) | collective-permute-done | bytes 196640 | tf_op jit(solution)/shard_map/ppermute | solution.py:80
  96.2 0.7 collective-permute-start.16
  97.4 3.0 %collective-permute-start.18 = (bf16[16,3072]{1,0:T(8,128)(2,1)S(1)}, bf16[16,3072]{1,0:T(8,128)(2,1)S(1)}, u32[]{:S(2)}, u32[]{:S(2)}) collective-permute-start(bf16[16,3072]{1,0:T(8,128)(2,1)S(1)} %get-tuple-element.46), channel_id=1, source_target_pairs={{2,0},{3,1},{0,2},{1,3},{6,4},{7,5},{4,6},{5,7},{10,8},{11,9},{8,1... | collective-permute-start | bytes 294920 | tf_op jit(solution)/shard_map/ppermute | solution.py:80
  100.9 2.9 %collective-permute-done.17.refs_2_ = bf16[16,3072]{1,0:T(8,128)(2,1)S(1)} collective-permute-done((bf16[16,3072]{1,0:T(8,128)(2,1)S(1)}, bf16[16,3072]{1,0:T(8,128)(2,1)S(1)}, u32[]{:S(2)}, u32[]{:S(2)}) %collective-permute-start.17) | collective-permute-done | bytes 98336 | tf_op jit(solution)/shard_map/ppermute | solution.py:80
  103.7 0.7 shard_map.125
  (38 shorter events, 4.5 us)
Async XLA Ops:
  0.0 22.7 %copy-start.7 = (f32[3]{0:T(128)S(1)}, f32[3]{0:T(128)}, u32[]{:S(2)}) copy-start(f32[3]{0:T(128)} %param.15) | copy-start | bytes 40
  0.0 4.8 %collective-permute-start = (bf16[16,3072]{1,0:T(8,128)(2,1)}, bf16[16,3072]{1,0:T(8,128)(2,1)S(1)}, u32[]{:S(2)}, u32[]{:S(2)}) collective-permute-start(bf16[16,3072]{1,0:T(8,128)(2,1)} %bitcast.12), channel_id=1, source_target_pairs={{1,0},{0,1},{3,2},{2,3},{5,4},{4,5},{7,6},{6,7},{9,8},{8,9},{11,10... | collective-permute-start | bytes 294920 | tf_op jit(solution)/shard_map/ppermute | solution.py:80
  1.5 7.4 %collective-permute-start.2 = (bf16[16,3072]{1,0:T(8,128)(2,1)}, bf16[16,3072]{1,0:T(8,128)(2,1)S(1)}, u32[]{:S(2)}, u32[]{:S(2)}) collective-permute-start(bf16[16,3072]{1,0:T(8,128)(2,1)} %bitcast.13), channel_id=1, source_target_pairs={{3,0},{2,1},{1,2},{0,3},{7,4},{6,5},{5,6},{4,7},{11,8},{10,9},{9,1... | collective-permute-start | bytes 294920 | tf_op jit(solution)/shard_map/ppermute | solution.py:80
  3.6 6.4 %collective-permute-start.1 = (bf16[16,3072]{1,0:T(8,128)(2,1)}, bf16[16,3072]{1,0:T(8,128)(2,1)S(1)}, u32[]{:S(2)}, u32[]{:S(2)}) collective-permute-start(bf16[16,3072]{1,0:T(8,128)(2,1)} %bitcast.14), channel_id=1, source_target_pairs={{2,0},{3,1},{0,2},{1,3},{6,4},{7,5},{4,6},{5,7},{10,8},{11,9},{8,1... | collective-permute-start | bytes 294920 | tf_op jit(solution)/shard_map/ppermute | solution.py:80
  5.7 9.4 %collective-permute-start.5 = (bf16[2,16,3072]{2,1,0:T(8,128)(2,1)S(1)}, bf16[2,16,3072]{2,1,0:T(8,128)(2,1)S(1)}, u32[]{:S(2)}, u32[]{:S(2)}) collective-permute-start(bf16[2,16,3072]{2,1,0:T(8,128)(2,1)S(1)} %pad_maximum_fusion.refs_0_), channel_id=1, source_target_pairs={{12,0},{13,1},{14,2},{15,3},{8,4},{9,5},{10,6},{11,7},{4,8},{5,9},... | collective-permute-start | bytes 589832 | tf_op jit(solution)/shard_map/ppermute | solution.py:80
  10.0 5.8 %collective-permute-start.4 = (bf16[2,16,3072]{2,1,0:T(8,128)(2,1)S(1)}, bf16[2,16,3072]{2,1,0:T(8,128)(2,1)S(1)}, u32[]{:S(2)}, u32[]{:S(2)}) collective-permute-start(bf16[2,16,3072]{2,1,0:T(8,128)(2,1)S(1)} %pad_maximum_fusion.1.after.refs_1_), channel_id=1, source_target_pairs={{4,0},{5,1},{6,2},{7,3},{0,4},{1,5},{2,6},{3,7},{12,8},{13,9},{14,... | collective-permute-start | bytes 589832 | tf_op jit(solution)/shard_map/ppermute | solution.py:80
  11.7 9.9 %collective-permute-start.3 = (bf16[2,16,3072]{2,1,0:T(8,128)(2,1)S(1)}, bf16[2,16,3072]{2,1,0:T(8,128)(2,1)S(1)}, u32[]{:S(2)}, u32[]{:S(2)}) collective-permute-start(bf16[2,16,3072]{2,1,0:T(8,128)(2,1)S(1)} %pad_maximum_fusion.refs_0_), channel_id=1, source_target_pairs={{4,0},{5,1},{6,2},{7,3},{0,4},{1,5},{2,6},{3,7},{12,8},{13,9},{14,... | collective-permute-start | bytes 589832 | tf_op jit(solution)/shard_map/ppermute | solution.py:80
  12.2 9.5 %collective-permute-start.8 = (bf16[2,16,3072]{2,1,0:T(8,128)(2,1)S(1)}, bf16[2,16,3072]{2,1,0:T(8,128)(2,1)S(1)}, u32[]{:S(2)}, u32[]{:S(2)}) collective-permute-start(bf16[2,16,3072]{2,1,0:T(8,128)(2,1)S(1)} %pad_maximum_fusion.1.after.refs_1_), channel_id=1, source_target_pairs={{12,0},{13,1},{14,2},{15,3},{8,4},{9,5},{10,6},{11,7},{4,8},{5,9},... | collective-permute-start | bytes 589832 | tf_op jit(solution)/shard_map/ppermute | solution.py:80
  15.2 6.5 %collective-permute-start.6 = (bf16[2,16,3072]{2,1,0:T(8,128)(2,1)S(1)}, bf16[2,16,3072]{2,1,0:T(8,128)(2,1)S(1)}, u32[]{:S(2)}, u32[]{:S(2)}) collective-permute-start(bf16[2,16,3072]{2,1,0:T(8,128)(2,1)S(1)} %collective-permute-done.5.refs_6_), channel_id=1, source_target_pairs={{4,0},{5,1},{6,2},{7,3},{0,4},{1,5},{2,6},{3,7},{12,8},{13,9},{14,... | collective-permute-start | bytes 589832 | tf_op jit(solution)/shard_map/ppermute | solution.py:80
  15.8 6.9 %collective-permute-start.7 = (bf16[2,16,3072]{2,1,0:T(8,128)(2,1)S(1)}, bf16[2,16,3072]{2,1,0:T(8,128)(2,1)S(1)}, u32[]{:S(2)}, u32[]{:S(2)}) collective-permute-start(bf16[2,16,3072]{2,1,0:T(8,128)(2,1)S(1)} %collective-permute-done.4.refs_3_), channel_id=1, source_target_pairs={{12,0},{13,1},{14,2},{15,3},{8,4},{9,5},{10,6},{11,7},{4,8},{5,9},... | collective-permute-start | bytes 589832 | tf_op jit(solution)/shard_map/ppermute | solution.py:80
  21.5 17.4 %copy-start.1 = (f32[3,64,256]{2,1,0:T(8,128)S(1)}, f32[3,64,256]{2,1,0:T(8,128)}, u32[]{:S(2)}) copy-start(f32[3,64,256]{2,1,0:T(8,128)} %w1_in.1) | copy-start | bytes 589828
  21.5 17.4 %copy-start.2 = (f32[3,256,64]{1,2,0:T(8,128)S(1)}, f32[3,256,64]{1,2,0:T(8,128)}, u32[]{:S(2)}) copy-start(f32[3,256,64]{1,2,0:T(8,128)} %param.18) | copy-start | bytes 589828
  21.6 17.4 %copy-start.3 = (f32[3,64]{1,0:T(4,128)S(1)}, f32[3,64]{1,0:T(4,128)}, u32[]{:S(2)}) copy-start(f32[3,64]{1,0:T(4,128)} %gain_in.3) | copy-start | bytes 2308
  21.6 17.4 %copy-start.4 = (f32[3,64]{1,0:T(4,128)S(1)}, f32[3,64]{1,0:T(4,128)}, u32[]{:S(2)}) copy-start(f32[3,64]{1,0:T(4,128)} %shift_in.3) | copy-start | bytes 2308
  21.6 17.4 %copy-start.5 = (f32[3,256]{1,0:T(4,128)S(1)}, f32[3,256]{1,0:T(4,128)}, u32[]{:S(2)}) copy-start(f32[3,256]{1,0:T(4,128)} %c1_in.1) | copy-start | bytes 9220
  21.6 17.4 %copy-start.6 = (f32[3,64]{1,0:T(4,128)S(1)}, f32[3,64]{1,0:T(4,128)}, u32[]{:S(2)}) copy-start(f32[3,64]{1,0:T(4,128)} %c2_in.1) | copy-start | bytes 2308
  22.7 55.9 %copy-start = (bf16[192,3072]{1,0:T(8,128)(2,1)S(1)}, bf16[192,3072]{1,0:T(8,128)(2,1)}, u32[]{:S(2)}) copy-start(bf16[192,3072]{1,0:T(8,128)(2,1)} %weight.1) | copy-start | bytes 3538948
  39.6 10.1 %all-to-all-start.1 = ((bf16[8,64,128]{2,1,0:T(8,128)(2,1)}), bf16[8,64,128]{2,1,0:T(8,128)(2,1)S(1)}, u32[]{:S(2)}, u32[]{:S(2)}) async-start(bf16[8,64,128]{2,1,0:T(8,128)(2,1)} %get-tuple-element.31), calls=%async_computation.1 | async-start | bytes 262144 | tf_op jit(solution)/shard_map/all_to_all | solution.py:360
  42.9 0.7 collective-permute-start.9
  80.2 7.0 %collective-permute-start.11 = (bf16[2,16,3072]{2,1,0:T(8,128)(2,1)S(1)}, bf16[2,16,3072]{2,1,0:T(8,128)(2,1)S(1)}, u32[]{:S(2)}, u32[]{:S(2)}) collective-permute-start(bf16[2,16,3072]{2,1,0:T(8,128)(2,1)S(1)} %get-tuple-element.39), channel_id=1, source_target_pairs={{12,0},{13,1},{14,2},{15,3},{8,4},{9,5},{10,6},{11,7},{4,8},{5,9},... | collective-permute-start | bytes 589832 | tf_op jit(solution)/shard_map/ppermute | solution.py:80
  83.3 5.7 %collective-permute-start.13 = (bf16[2,16,3072]{2,1,0:T(8,128)(2,1)S(1)}, bf16[2,16,3072]{2,1,0:T(8,128)(2,1)S(1)}, u32[]{:S(2)}, u32[]{:S(2)}) collective-permute-start(bf16[2,16,3072]{2,1,0:T(8,128)(2,1)S(1)} %get-tuple-element.41), channel_id=1, source_target_pairs={{4,0},{5,1},{6,2},{7,3},{0,4},{1,5},{2,6},{3,7},{12,8},{13,9},{14,... | collective-permute-start | bytes 589832 | tf_op jit(solution)/shard_map/ppermute | solution.py:80
  83.3 7.8 %collective-permute-start.10 = (bf16[2,16,3072]{2,1,0:T(8,128)(2,1)S(1)}, bf16[2,16,3072]{2,1,0:T(8,128)(2,1)S(1)}, u32[]{:S(2)}, u32[]{:S(2)}) collective-permute-start(bf16[2,16,3072]{2,1,0:T(8,128)(2,1)S(1)} %get-tuple-element.37), channel_id=1, source_target_pairs={{4,0},{5,1},{6,2},{7,3},{0,4},{1,5},{2,6},{3,7},{12,8},{13,9},{14,... | collective-permute-start | bytes 589832 | tf_op jit(solution)/shard_map/ppermute | solution.py:80
  85.4 6.9 %collective-permute-start.15 = (bf16[2,16,3072]{2,1,0:T(8,128)(2,1)S(1)}, bf16[2,16,3072]{2,1,0:T(8,128)(2,1)S(1)}, u32[]{:S(2)}, u32[]{:S(2)}) collective-permute-start(bf16[2,16,3072]{2,1,0:T(8,128)(2,1)S(1)} %get-tuple-element.42), channel_id=1, source_target_pairs={{12,0},{13,1},{14,2},{15,3},{8,4},{9,5},{10,6},{11,7},{4,8},{5,9},... | collective-permute-start | bytes 589832 | tf_op jit(solution)/shard_map/ppermute | solution.py:80
  87.2 6.0 %collective-permute-start.12 = (bf16[2,16,3072]{2,1,0:T(8,128)(2,1)S(1)}, bf16[2,16,3072]{2,1,0:T(8,128)(2,1)S(1)}, u32[]{:S(2)}, u32[]{:S(2)}) collective-permute-start(bf16[2,16,3072]{2,1,0:T(8,128)(2,1)S(1)} %shard_map.122), channel_id=1, source_target_pairs={{4,0},{5,1},{6,2},{7,3},{0,4},{1,5},{2,6},{3,7},{12,8},{13,9},{14,... | collective-permute-start | bytes 589832 | tf_op jit(solution)/shard_map/ppermute | solution.py:80
  89.1 7.0 %collective-permute-start.14 = (bf16[2,16,3072]{2,1,0:T(8,128)(2,1)S(1)}, bf16[2,16,3072]{2,1,0:T(8,128)(2,1)S(1)}, u32[]{:S(2)}, u32[]{:S(2)}) collective-permute-start(bf16[2,16,3072]{2,1,0:T(8,128)(2,1)S(1)} %shard_map.123), channel_id=1, source_target_pairs={{12,0},{13,1},{14,2},{15,3},{8,4},{9,5},{10,6},{11,7},{4,8},{5,9},... | collective-permute-start | bytes 589832 | tf_op jit(solution)/shard_map/ppermute | solution.py:80
  96.2 4.7 %collective-permute-start.16 = (bf16[16,3072]{1,0:T(8,128)(2,1)S(1)}, bf16[16,3072]{1,0:T(8,128)(2,1)S(1)}, u32[]{:S(2)}, u32[]{:S(2)}) collective-permute-start(bf16[16,3072]{1,0:T(8,128)(2,1)S(1)} %get-tuple-element.44), channel_id=1, source_target_pairs={{1,0},{0,1},{3,2},{2,3},{5,4},{4,5},{7,6},{6,7},{9,8},{8,9},{11,10... | collective-permute-start | bytes 294920 | tf_op jit(solution)/shard_map/ppermute | solution.py:80
  96.8 6.9 %collective-permute-start.17 = (bf16[16,3072]{1,0:T(8,128)(2,1)S(1)}, bf16[16,3072]{1,0:T(8,128)(2,1)S(1)}, u32[]{:S(2)}, u32[]{:S(2)}) collective-permute-start(bf16[16,3072]{1,0:T(8,128)(2,1)S(1)} %get-tuple-element.45), channel_id=1, source_target_pairs={{3,0},{2,1},{1,2},{0,3},{7,4},{6,5},{5,6},{4,7},{11,8},{10,9},{9,1... | collective-permute-start | bytes 294920 | tf_op jit(solution)/shard_map/ppermute | solution.py:80
  97.4 6.3 %collective-permute-start.18 = (bf16[16,3072]{1,0:T(8,128)(2,1)S(1)}, bf16[16,3072]{1,0:T(8,128)(2,1)S(1)}, u32[]{:S(2)}, u32[]{:S(2)}) collective-permute-start(bf16[16,3072]{1,0:T(8,128)(2,1)S(1)} %get-tuple-element.46), channel_id=1, source_target_pairs={{2,0},{3,1},{0,2},{1,3},{6,4},{7,5},{4,6},{5,7},{10,8},{11,9},{8,1... | collective-permute-start | bytes 294920 | tf_op jit(solution)/shard_map/ppermute | solution.py:80

commit v4 on v3

--- a/solution.py
+++ b/solution.py
@@ -305,8 +305,7 @@
 
 
 def mix_kernel(place, answers, weight, *refs):
-    outs, by_place = refs[: 2 * SIDE], refs[2 * SIDE]
-    width = weight.shape[1]
+    outs, by_place = refs[: SIDE * SIDE], refs[SIDE * SIDE]
     for seq in range(2):
         heads = [answers[place[SEAT + 3 * seq + head]].astype(F32) for head in range(3)]
         for half in range(2):
@@ -323,25 +322,13 @@
         )
         rows = jnp.where(place[CORE] == 0, first, second).reshape(64, 3 * HEAD)
         total = mm(rows.astype(BF16), weight[...]).astype(BF16)
-        outs[2 * k][...] = total[0:32].reshape(2, 16, width)
-        outs[2 * k + 1][...] = total[32:64].reshape(2, 16, width)
-
-
-def pair_kernel(left, right, out):
-    out[...] = (left[...].astype(F32) + right[...].astype(F32)).astype(BF16)
-
-
-def line_kernel(*refs):
-    for half in range(2):
-        parts = refs[half : 6 : 2]
-        total = sum(part[...].astype(F32) for part in parts).astype(BF16)
-        refs[6 + 2 * half][...] = total[0]
-        refs[7 + 2 * half][...] = total[1]
-
-
-def last_kernel(*refs):
-    total = sum(part[...].astype(F32) for part in refs[:SIDE])
-    refs[SIDE][...] = total.astype(BF16)
+        for place_in_line in range(SIDE):
+            outs[SIDE * k + place_in_line][...] = total[16 * place_in_line :][0:16]
+
+
+def add_kernel(*refs):
+    total = sum(part[...].astype(F32) for part in refs[:-1])
+    refs[-1][...] = total.astype(BF16)
 
 
 def kernel_call(kernel, out_shape, count, scalars=1, scratch=()):
@@ -436,22 +423,26 @@
     answers = kernel_call(second_kernel, answer_shape, 7, scratch=[rates])(
         place, pairs, queries, state, norm_gain, norm_shift, weights, biases
     )
-    pair = jax.ShapeDtypeStruct((2, 16, width), BF16)
     single = jax.ShapeDtypeStruct((16, width), BF16)
     parts = kernel_call(
-        mix_kernel, (pair,) * (2 * SIDE), 2, scratch=[pltpu.VMEM((2, SIDE, SIDE, 8, 3 * HEAD), F32)]
+        mix_kernel,
+        (single,) * (SIDE * SIDE),
+        2,
+        scratch=[pltpu.VMEM((2, SIDE, SIDE, 8, 3 * HEAD), F32)],
     )(place, exchange(answers), out_weight)
-    low, high, low_one, high_one, low_two, high_two, low_three, high_three = parts
-    add = kernel_call(pair_kernel, pair, 2, 0)
-    passing_three, passing_one = from_side(low_two, 1, 1), from_side(high_two, 1, 3)
-    low_one, high_three = from_side(low_one, 1, 1), from_side(high_three, 1, 3)
-    low_three = from_side(add(low_three, passing_three), 1, 3)
-    high_one = from_side(add(high_one, passing_one), 1, 1)
-    line = kernel_call(line_kernel, (single,) * SIDE, 6, 0)(
-        low, high, low_one, high_one, low_three, high_three
-    )
-    far = [from_side(line[k], 0, k) for k in (1, 3, 2)]
-    mixed = kernel_call(last_kernel, single, SIDE, 0)(line[0], *far)
+    near, far = {0: 1, 1: 1, 2: 3, 3: 3}, {0: 3, 1: 3, 2: 1, 3: 1}
+    order = (2, 1, 3, 0)
+    passing = {k: from_side(parts[2 * SIDE + k], 1, near[k]) for k in order}
+    direct = {k: from_side(parts[near[k] * SIDE + k], 1, near[k]) for k in order}
+    line = {}
+    for k in order:
+        joint = kernel_call(add_kernel, single, 2, 0)(parts[far[k] * SIDE + k], passing[k])
+        line[k] = kernel_call(add_kernel, single, 3, 0)(
+            parts[k], direct[k], from_side(joint, 1, far[k])
+        )
+    mixed = kernel_call(add_kernel, single, SIDE, 0)(
+        line[0], *(from_side(line[k], 0, k) for k in (1, 3, 2))
+    )
     return mixed.reshape(seqs, own_rows, width)
 
 

time: 105 us -> 105 us (level)
  waiting for transfers between devices: 21.1 us -> 13 us
  starting transfers between devices: 31.1 us -> 39.1 us
    ppermute x18 -> x24, waiting for transfers between devices: 15.1 us -> 7.03 us  [from_side(): return lax.ppermute(value, ('seq', 'tensor'), pairs)]
    ppermute x18 -> x24, starting transfers between devices: 27.1 us -> 35 us  [from_side(): return lax.ppermute(value, ('seq', 'tensor'), pairs)]
    pallas_call x5 -> x10, Pallas kernels: 2.56 us -> 2.58 us  [the longest x1 1.63 us: shards(): kernel_call(mix_kernel, (single,) * (SIDE * SIDE), 2, scratch=[pltpu.VMEM...]
  transfers between devices with their start and end apart: 20 -> 26, of which waited for: 13 -> 9; matrix products, arithmetic and copies ran while one was open for 2% -> 2% of each run, Pallas kernels for 2% -> 2%
where the time goes in v4:
time: 105 us; the launch traced here: 104 us
  starting transfers between devices  39.1 us (37%)
  blocking collectives  31.9 us (30%)
  Pallas kernels  18.5 us (18%)
  waiting for transfers between devices  13 us (12%)
    ppermute x24, starting transfers between devices, from_side(): return lax.ppermute(value, ('seq', 'tensor'), pairs)  35 us
    all_to_all x2, blocking collectives, exchange(): lax.all_to_all(value, 'seq', 0, 0, axis_index_groups=GROUPS, tiled=True)  31.9 us
    pallas_call x1, Pallas kernels, shards(): kernel_call(second_kernel, answer_shape, 7, scratch=[rates])  10.5 us
    ppermute x24, waiting for transfers between devices, from_side(): return lax.ppermute(value, ('seq', 'tensor'), pairs)  7.03 us
    all_to_all x1, waiting for transfers between devices, exchange(): lax.all_to_all(value, 'seq', 0, 0, axis_index_groups=GROUPS, tiled=True)  6 us
    all_to_all x1, starting transfers between devices, exchange(): lax.all_to_all(value, 'seq', 0, 0, axis_index_groups=GROUPS, tiled=True)  3.38 us
    pallas_call x1, Pallas kernels, shards(): kernel_call(project_kernel, (jax.ShapeDtypeStruct((ROWS, 2 * MB + 16, 2 *...  2.87 us
  transfers between devices with their start and end apart: 26, of which 9 were waited for; matrix products, arithmetic and copies ran while one was open for 2% of the time, Pallas kernels for 2%

profile of v4, /device:TPU:128, one launch (start us, length us, event | category | flops | bytes accessed | tf_op | source)
XLA Modules:
  0.0 104.4 jit_solution(18372413832046247101)
XLA Ops:
  0.0 1.5 %collective-permute-start = (bf16[16,3072]{1,0:T(8,128)(2,1)}, bf16[16,3072]{1,0:T(8,128)(2,1)S(1)}, u32[]{:S(2)}, u32[]{:S(2)}) collective-permute-start(bf16[16,3072]{1,0:T(8,128)(2,1)} %bitcast.12), channel_id=1, source_target_pairs={{1,0},{0,1},{3,2},{2,3},{5,4},{4,5},{7,6},{6,7},{9,8},{8,9},{11,10... | collective-permute-start | bytes 294920 | tf_op jit(solution)/shard_map/ppermute | solution.py:80
  1.5 2.1 %collective-permute-start.2 = (bf16[16,3072]{1,0:T(8,128)(2,1)}, bf16[16,3072]{1,0:T(8,128)(2,1)S(1)}, u32[]{:S(2)}, u32[]{:S(2)}) collective-permute-start(bf16[16,3072]{1,0:T(8,128)(2,1)} %bitcast.13), channel_id=1, source_target_pairs={{3,0},{2,1},{1,2},{0,3},{7,4},{6,5},{5,6},{4,7},{11,8},{10,9},{9,1... | collective-permute-start | bytes 294920 | tf_op jit(solution)/shard_map/ppermute | solution.py:80
  4.8 0.9 pad_maximum_fusion.refs_0_
  5.7 3.1 %collective-permute-start.5 = (bf16[2,16,3072]{2,1,0:T(8,128)(2,1)S(1)}, bf16[2,16,3072]{2,1,0:T(8,128)(2,1)S(1)}, u32[]{:S(2)}, u32[]{:S(2)}) collective-permute-start(bf16[2,16,3072]{2,1,0:T(8,128)(2,1)S(1)} %pad_maximum_fusion.refs_0_), channel_id=1, source_target_pairs={{12,0},{13,1},{14,2},{15,3},{8,4},{9,5},{10,6},{11,7},{4,8},{5,9},... | collective-permute-start | bytes 589832 | tf_op jit(solution)/shard_map/ppermute | solution.py:80
  8.9 1.2 %collective-permute-done.1 = bf16[16,3072]{1,0:T(8,128)(2,1)S(1)} collective-permute-done((bf16[16,3072]{1,0:T(8,128)(2,1)}, bf16[16,3072]{1,0:T(8,128)(2,1)S(1)}, u32[]{:S(2)}, u32[]{:S(2)}) %collective-permute-start.1) | collective-permute-done | bytes 98336 | tf_op jit(solution)/shard_map/ppermute | solution.py:80
  10.0 1.7 %collective-permute-start.4 = (bf16[2,16,3072]{2,1,0:T(8,128)(2,1)S(1)}, bf16[2,16,3072]{2,1,0:T(8,128)(2,1)S(1)}, u32[]{:S(2)}, u32[]{:S(2)}) collective-permute-start(bf16[2,16,3072]{2,1,0:T(8,128)(2,1)S(1)} %pad_maximum_fusion.1.after.refs_1_), channel_id=1, source_target_pairs={{4,0},{5,1},{6,2},{7,3},{0,4},{1,5},{2,6},{3,7},{12,8},{13,9},{14,... | collective-permute-start | bytes 589832 | tf_op jit(solution)/shard_map/ppermute | solution.py:80
  12.2 3.0 %collective-permute-start.8 = (bf16[2,16,3072]{2,1,0:T(8,128)(2,1)S(1)}, bf16[2,16,3072]{2,1,0:T(8,128)(2,1)S(1)}, u32[]{:S(2)}, u32[]{:S(2)}) collective-permute-start(bf16[2,16,3072]{2,1,0:T(8,128)(2,1)S(1)} %pad_maximum_fusion.1.after.refs_1_), channel_id=1, source_target_pairs={{12,0},{13,1},{14,2},{15,3},{8,4},{9,5},{10,6},{11,7},{4,8},{5,9},... | collective-permute-start | bytes 589832 | tf_op jit(solution)/shard_map/ppermute | solution.py:80
  15.8 3.0 %collective-permute-start.7 = (bf16[2,16,3072]{2,1,0:T(8,128)(2,1)S(1)}, bf16[2,16,3072]{2,1,0:T(8,128)(2,1)S(1)}, u32[]{:S(2)}, u32[]{:S(2)}) collective-permute-start(bf16[2,16,3072]{2,1,0:T(8,128)(2,1)S(1)} %collective-permute-done.4.refs_3_), channel_id=1, source_target_pairs={{12,0},{13,1},{14,2},{15,3},{8,4},{9,5},{10,6},{11,7},{4,8},{5,9},... | collective-permute-start | bytes 589832 | tf_op jit(solution)/shard_map/ppermute | solution.py:80
  18.8 0.7 dynamic-slice_bitcast_fusion.place
  19.5 2.0 %fetch.1 = (bf16[3,192,3072]{2,1,0:T(8,128)(2,1)S(1)}, bf16[16,3072]{1,0:T(8,128)(2,1)S(1)}) custom-call(bf16[2,16,3072]{2,1,0:T(8,128)(2,1)S(1)} %pad_maximum_fusion.1.after.refs_1_, bf16[3,192,3072]{2,1,0:T(8,128)(2,1)} %weight_in.1, bf16[3,3072]{1,0:T(4,128)(2,1)} %rate_weight_in.1), custom_call_target="tpu_custom_call" | custom-call | bytes 4194304 | tf_op jit(solution)/shard_map/fetch/pallas_call | solution.py:375
  21.6 1.0 %collective-permute-done.7.refs_5_ = bf16[2,16,3072]{2,1,0:T(8,128)(2,1)S(1)} collective-permute-done((bf16[2,16,3072]{2,1,0:T(8,128)(2,1)S(1)}, bf16[2,16,3072]{2,1,0:T(8,128)(2,1)S(1)}, u32[]{:S(2)}, u32[]{:S(2)}) %collective-permute-start.7) | collective-permute-done | bytes 196640 | tf_op jit(solution)/shard_map/ppermute | solution.py:80
  22.7 2.9 %shard_map.118 = (bf16[8,144,128]{2,1,0:T(8,128)(2,1)S(1)}, bf16[8,64,128]{2,1,0:T(8,128)(2,1)}) custom-call(s32[10]{0:T(128)S(1)} %dynamic-slice_bitcast_fusion.place, bf16[2,16,3072]{2,1,0:T(8,128)(2,1)S(1)} %pad_maximum_fusion.refs_0_, bf16[2,16,3072]{2,1,0:T(8,128)(2,1)S(1)} %pad_maximum_fusion.1.after.refs_1_, ...), custom_call_target="tpu_custom_call" | custom-call | tf_op jit(solution)/shard_map/pallas_call | solution.py:390
  25.6 13.4 %all_to_all.15.pairs = bf16[8,144,128]{2,1,0:T(8,128)(2,1)S(1)} all-to-all(bf16[8,144,128]{2,1,0:T(8,128)(2,1)S(1)} %get-tuple-element.32), channel_id=1, replica_groups={{0,16,32,48,64,80,96,112},{128,144,160,176,192,208,224,240},{1,17,33,49..., dimensions={0} | all-to-all | bytes 589824 | tf_op jit(solution)/shard_map/all_to_all | solution.py:347
  39.6 3.4 %all-to-all-start.1 = ((bf16[8,64,128]{2,1,0:T(8,128)(2,1)}), bf16[8,64,128]{2,1,0:T(8,128)(2,1)S(1)}, u32[]{:S(2)}, u32[]{:S(2)}) async-start(bf16[8,64,128]{2,1,0:T(8,128)(2,1)} %get-tuple-element.35), calls=%async_computation.1 | async-start | bytes 262144 | tf_op jit(solution)/shard_map/all_to_all | solution.py:347
  43.6 6.0 %all-to-all-done.1.queries = bf16[8,64,128]{2,1,0:T(8,128)(2,1)S(1)} async-done(((bf16[8,64,128]{2,1,0:T(8,128)(2,1)}), bf16[8,64,128]{2,1,0:T(8,128)(2,1)S(1)}, u32[]{:S(2)}, u32[]{:S(2)}) %all-to-all-start.1) | async-done | bytes 131104 | tf_op jit(solution)/shard_map/all_to_all | solution.py:347
  49.6 10.5 %shard_map.120 = bf16[8,64,128]{2,1,0:T(8,128)(2,1)S(1)} custom-call(s32[10]{0:T(128)S(1)} %dynamic-slice_bitcast_fusion.place, bf16[8,144,128]{2,1,0:T(8,128)(2,1)S(1)} %all_to_all.15.pairs, bf16[8,64,128]{2,1,0:T(8,128)(2,1)S(1)} %all-to-all-done.1.queries, bf16[144,256]{1,0:T(8,128)(2,1)S(1)} %collective-permute-done.9.state, f32[3,64]{1,0:T(4,128)S(1)} %copy-done.3, ...), custom_call_target="tpu_custom_call" | custom-call | tf_op jit(solution)/shard_map/pallas_call | solution.py:423
  60.1 18.5 %all_to_all.16.answers = bf16[8,64,128]{2,1,0:T(8,128)(2,1)S(1)} all-to-all(bf16[8,64,128]{2,1,0:T(8,128)(2,1)S(1)} %shard_map.120), channel_id=1, replica_groups={{0,16,32,48,64,80,96,112},{128,144,160,176,192,208,224,240},{1,17,33,49..., dimensions={0} | all-to-all | bytes 262144 | tf_op jit(solution)/shard_map/all_to_all | solution.py:347
  78.6 1.6 %shard_map.121 = (bf16[16,3072]{1,0:T(8,128)(2,1)S(1)}, bf16[16,3072]{1,0:T(8,128)(2,1)S(1)}, bf16[16,3072]{1,0:T(8,128)(2,1)S(1)}, bf16[16,3072]{1,0:T(8,128)(2...) custom-call(s32[10]{0:T(128)S(1)} %dynamic-slice_bitcast_fusion.plac, ...), custom_call_target="tpu_custom_call" | custom-call | tf_op jit(solution)/shard_map/pallas_call | solution.py:427
  80.7 2.8 %collective-permute-start.18 = (bf16[16,3072]{1,0:T(8,128)(2,1)S(1)}, bf16[16,3072]{1,0:T(8,128)(2,1)S(1)}, u32[]{:S(2)}, u32[]{:S(2)}) collective-permute-start(bf16[16,3072]{1,0:T(8,128)(2,1)S(1)} %get-tuple-element.50), channel_id=1, source_target_pairs={{12,0},{13,1},{14,2},{15,3},{8,4},{9,5},{10,6},{11,7},{4,8},{5,9},... | collective-permute-start | bytes 294920 | tf_op jit(solution)/shard_map/ppermute | solution.py:80
  83.9 0.9 collective-permute-start.11
  84.8 1.2 %collective-permute-start.13 = (bf16[16,3072]{1,0:T(8,128)(2,1)S(1)}, bf16[16,3072]{1,0:T(8,128)(2,1)S(1)}, u32[]{:S(2)}, u32[]{:S(2)}) collective-permute-start(bf16[16,3072]{1,0:T(8,128)(2,1)S(1)} %get-tuple-element.44), channel_id=1, source_target_pairs={{4,0},{5,1},{6,2},{7,3},{0,4},{1,5},{2,6},{3,7},{12,8},{13,9},{14,... | collective-permute-start | bytes 294920 | tf_op jit(solution)/shard_map/ppermute | solution.py:80
  86.0 2.8 %collective-permute-start.15 = (bf16[16,3072]{1,0:T(8,128)(2,1)S(1)}, bf16[16,3072]{1,0:T(8,128)(2,1)S(1)}, u32[]{:S(2)}, u32[]{:S(2)}) collective-permute-start(bf16[16,3072]{1,0:T(8,128)(2,1)S(1)} %shard_map.124), channel_id=1, source_target_pairs={{12,0},{13,1},{14,2},{15,3},{8,4},{9,5},{10,6},{11,7},{4,8},{5,9},... | collective-permute-start | bytes 294920 | tf_op jit(solution)/shard_map/ppermute | solution.py:80
  89.5 2.8 %collective-permute-start.21 = (bf16[16,3072]{1,0:T(8,128)(2,1)S(1)}, bf16[16,3072]{1,0:T(8,128)(2,1)S(1)}, u32[]{:S(2)}, u32[]{:S(2)}) collective-permute-start(bf16[16,3072]{1,0:T(8,128)(2,1)S(1)} %get-tuple-element.52), channel_id=1, source_target_pairs={{12,0},{13,1},{14,2},{15,3},{8,4},{9,5},{10,6},{11,7},{4,8},{5,9},... | collective-permute-start | bytes 294920 | tf_op jit(solution)/shard_map/ppermute | solution.py:80
  92.3 1.4 %collective-permute-start.23 = (bf16[16,3072]{1,0:T(8,128)(2,1)S(1)}, bf16[16,3072]{1,0:T(8,128)(2,1)S(1)}, u32[]{:S(2)}, u32[]{:S(2)}) collective-permute-start(bf16[16,3072]{1,0:T(8,128)(2,1)S(1)} %shard_map.128), channel_id=1, source_target_pairs={{4,0},{5,1},{6,2},{7,3},{0,4},{1,5},{2,6},{3,7},{12,8},{13,9},{14,... | collective-permute-start | bytes 294920 | tf_op jit(solution)/shard_map/ppermute | solution.py:80
  93.8 0.7 collective-permute-start.10
  94.6 1.0 %collective-permute-start.12 = (bf16[16,3072]{1,0:T(8,128)(2,1)S(1)}, bf16[16,3072]{1,0:T(8,128)(2,1)S(1)}, u32[]{:S(2)}, u32[]{:S(2)}) collective-permute-start(bf16[16,3072]{1,0:T(8,128)(2,1)S(1)} %shard_map.122), channel_id=1, source_target_pairs={{12,0},{13,1},{14,2},{15,3},{8,4},{9,5},{10,6},{11,7},{4,8},{5,9},... | collective-permute-start | bytes 294920 | tf_op jit(solution)/shard_map/ppermute | solution.py:80
  96.3 1.1 %collective-permute-start.20 = (bf16[16,3072]{1,0:T(8,128)(2,1)S(1)}, bf16[16,3072]{1,0:T(8,128)(2,1)S(1)}, u32[]{:S(2)}, u32[]{:S(2)}) collective-permute-start(bf16[16,3072]{1,0:T(8,128)(2,1)S(1)} %shard_map.127), channel_id=1, source_target_pairs={{3,0},{2,1},{1,2},{0,3},{7,4},{6,5},{5,6},{4,7},{11,8},{10,9},{9,1... | collective-permute-start | bytes 294920 | tf_op jit(solution)/shard_map/ppermute | solution.py:80
  97.5 2.6 %collective-permute-start.24 = (bf16[16,3072]{1,0:T(8,128)(2,1)S(1)}, bf16[16,3072]{1,0:T(8,128)(2,1)S(1)}, u32[]{:S(2)}, u32[]{:S(2)}) collective-permute-start(bf16[16,3072]{1,0:T(8,128)(2,1)S(1)} %shard_map.129), channel_id=1, source_target_pairs={{2,0},{3,1},{0,2},{1,3},{6,4},{7,5},{4,6},{5,7},{10,8},{11,9},{8,1... | collective-permute-start | bytes 294920 | tf_op jit(solution)/shard_map/ppermute | solution.py:80
  100.1 1.4 %collective-permute-done.12.refs_2_ = bf16[16,3072]{1,0:T(8,128)(2,1)S(1)} collective-permute-done((bf16[16,3072]{1,0:T(8,128)(2,1)S(1)}, bf16[16,3072]{1,0:T(8,128)(2,1)S(1)}, u32[]{:S(2)}, u32[]{:S(2)}) %collective-permute-start.12) | collective-permute-done | bytes 98336 | tf_op jit(solution)/shard_map/ppermute | solution.py:80
  101.5 0.7 collective-permute-done.20.refs_2_
  102.3 1.4 %collective-permute-done.24.refs_3_ = bf16[16,3072]{1,0:T(8,128)(2,1)S(1)} collective-permute-done((bf16[16,3072]{1,0:T(8,128)(2,1)S(1)}, bf16[16,3072]{1,0:T(8,128)(2,1)S(1)}, u32[]{:S(2)}, u32[]{:S(2)}) %collective-permute-start.24) | collective-permute-done | bytes 98336 | tf_op jit(solution)/shard_map/ppermute | solution.py:80
  103.7 0.7 shard_map.130
  (55 shorter events, 6.2 us)
Async XLA Ops:
  0.0 22.7 %copy-start.7 = (f32[3]{0:T(128)S(1)}, f32[3]{0:T(128)}, u32[]{:S(2)}) copy-start(f32[3]{0:T(128)} %param.15) | copy-start | bytes 40
  0.0 4.8 %collective-permute-start = (bf16[16,3072]{1,0:T(8,128)(2,1)}, bf16[16,3072]{1,0:T(8,128)(2,1)S(1)}, u32[]{:S(2)}, u32[]{:S(2)}) collective-permute-start(bf16[16,3072]{1,0:T(8,128)(2,1)} %bitcast.12), channel_id=1, source_target_pairs={{1,0},{0,1},{3,2},{2,3},{5,4},{4,5},{7,6},{6,7},{9,8},{8,9},{11,10... | collective-permute-start | bytes 294920 | tf_op jit(solution)/shard_map/ppermute | solution.py:80
  1.5 7.4 %collective-permute-start.2 = (bf16[16,3072]{1,0:T(8,128)(2,1)}, bf16[16,3072]{1,0:T(8,128)(2,1)S(1)}, u32[]{:S(2)}, u32[]{:S(2)}) collective-permute-start(bf16[16,3072]{1,0:T(8,128)(2,1)} %bitcast.13), channel_id=1, source_target_pairs={{3,0},{2,1},{1,2},{0,3},{7,4},{6,5},{5,6},{4,7},{11,8},{10,9},{9,1... | collective-permute-start | bytes 294920 | tf_op jit(solution)/shard_map/ppermute | solution.py:80
  3.6 6.4 %collective-permute-start.1 = (bf16[16,3072]{1,0:T(8,128)(2,1)}, bf16[16,3072]{1,0:T(8,128)(2,1)S(1)}, u32[]{:S(2)}, u32[]{:S(2)}) collective-permute-start(bf16[16,3072]{1,0:T(8,128)(2,1)} %bitcast.14), channel_id=1, source_target_pairs={{2,0},{3,1},{0,2},{1,3},{6,4},{7,5},{4,6},{5,7},{10,8},{11,9},{8,1... | collective-permute-start | bytes 294920 | tf_op jit(solution)/shard_map/ppermute | solution.py:80
  5.7 9.4 %collective-permute-start.5 = (bf16[2,16,3072]{2,1,0:T(8,128)(2,1)S(1)}, bf16[2,16,3072]{2,1,0:T(8,128)(2,1)S(1)}, u32[]{:S(2)}, u32[]{:S(2)}) collective-permute-start(bf16[2,16,3072]{2,1,0:T(8,128)(2,1)S(1)} %pad_maximum_fusion.refs_0_), channel_id=1, source_target_pairs={{12,0},{13,1},{14,2},{15,3},{8,4},{9,5},{10,6},{11,7},{4,8},{5,9},... | collective-permute-start | bytes 589832 | tf_op jit(solution)/shard_map/ppermute | solution.py:80
  10.0 5.8 %collective-permute-start.4 = (bf16[2,16,3072]{2,1,0:T(8,128)(2,1)S(1)}, bf16[2,16,3072]{2,1,0:T(8,128)(2,1)S(1)}, u32[]{:S(2)}, u32[]{:S(2)}) collective-permute-start(bf16[2,16,3072]{2,1,0:T(8,128)(2,1)S(1)} %pad_maximum_fusion.1.after.refs_1_), channel_id=1, source_target_pairs={{4,0},{5,1},{6,2},{7,3},{0,4},{1,5},{2,6},{3,7},{12,8},{13,9},{14,... | collective-permute-start | bytes 589832 | tf_op jit(solution)/shard_map/ppermute | solution.py:80
  11.7 9.9 %collective-permute-start.3 = (bf16[2,16,3072]{2,1,0:T(8,128)(2,1)S(1)}, bf16[2,16,3072]{2,1,0:T(8,128)(2,1)S(1)}, u32[]{:S(2)}, u32[]{:S(2)}) collective-permute-start(bf16[2,16,3072]{2,1,0:T(8,128)(2,1)S(1)} %pad_maximum_fusion.refs_0_), channel_id=1, source_target_pairs={{4,0},{5,1},{6,2},{7,3},{0,4},{1,5},{2,6},{3,7},{12,8},{13,9},{14,... | collective-permute-start | bytes 589832 | tf_op jit(solution)/shard_map/ppermute | solution.py:80
  12.2 9.5 %collective-permute-start.8 = (bf16[2,16,3072]{2,1,0:T(8,128)(2,1)S(1)}, bf16[2,16,3072]{2,1,0:T(8,128)(2,1)S(1)}, u32[]{:S(2)}, u32[]{:S(2)}) collective-permute-start(bf16[2,16,3072]{2,1,0:T(8,128)(2,1)S(1)} %pad_maximum_fusion.1.after.refs_1_), channel_id=1, source_target_pairs={{12,0},{13,1},{14,2},{15,3},{8,4},{9,5},{10,6},{11,7},{4,8},{5,9},... | collective-permute-start | bytes 589832 | tf_op jit(solution)/shard_map/ppermute | solution.py:80
  15.2 6.5 %collective-permute-start.6 = (bf16[2,16,3072]{2,1,0:T(8,128)(2,1)S(1)}, bf16[2,16,3072]{2,1,0:T(8,128)(2,1)S(1)}, u32[]{:S(2)}, u32[]{:S(2)}) collective-permute-start(bf16[2,16,3072]{2,1,0:T(8,128)(2,1)S(1)} %collective-permute-done.5.refs_6_), channel_id=1, source_target_pairs={{4,0},{5,1},{6,2},{7,3},{0,4},{1,5},{2,6},{3,7},{12,8},{13,9},{14,... | collective-permute-start | bytes 589832 | tf_op jit(solution)/shard_map/ppermute | solution.py:80
  15.8 6.9 %collective-permute-start.7 = (bf16[2,16,3072]{2,1,0:T(8,128)(2,1)S(1)}, bf16[2,16,3072]{2,1,0:T(8,128)(2,1)S(1)}, u32[]{:S(2)}, u32[]{:S(2)}) collective-permute-start(bf16[2,16,3072]{2,1,0:T(8,128)(2,1)S(1)} %collective-permute-done.4.refs_3_), channel_id=1, source_target_pairs={{12,0},{13,1},{14,2},{15,3},{8,4},{9,5},{10,6},{11,7},{4,8},{5,9},... | collective-permute-start | bytes 589832 | tf_op jit(solution)/shard_map/ppermute | solution.py:80
  21.5 17.4 %copy-start.1 = (f32[3,64,256]{2,1,0:T(8,128)S(1)}, f32[3,64,256]{2,1,0:T(8,128)}, u32[]{:S(2)}) copy-start(f32[3,64,256]{2,1,0:T(8,128)} %w1_in.1) | copy-start | bytes 589828
  21.5 17.4 %copy-start.2 = (f32[3,256,64]{1,2,0:T(8,128)S(1)}, f32[3,256,64]{1,2,0:T(8,128)}, u32[]{:S(2)}) copy-start(f32[3,256,64]{1,2,0:T(8,128)} %param.18) | copy-start | bytes 589828
  21.6 17.4 %copy-start.3 = (f32[3,64]{1,0:T(4,128)S(1)}, f32[3,64]{1,0:T(4,128)}, u32[]{:S(2)}) copy-start(f32[3,64]{1,0:T(4,128)} %gain_in.3) | copy-start | bytes 2308
  21.6 17.4 %copy-start.4 = (f32[3,64]{1,0:T(4,128)S(1)}, f32[3,64]{1,0:T(4,128)}, u32[]{:S(2)}) copy-start(f32[3,64]{1,0:T(4,128)} %shift_in.3) | copy-start | bytes 2308
  22.7 55.9 %copy-start = (bf16[192,3072]{1,0:T(8,128)(2,1)S(1)}, bf16[192,3072]{1,0:T(8,128)(2,1)}, u32[]{:S(2)}) copy-start(bf16[192,3072]{1,0:T(8,128)(2,1)} %weight.1) | copy-start | bytes 3538948
  39.6 10.1 %all-to-all-start.1 = ((bf16[8,64,128]{2,1,0:T(8,128)(2,1)}), bf16[8,64,128]{2,1,0:T(8,128)(2,1)S(1)}, u32[]{:S(2)}, u32[]{:S(2)}) async-start(bf16[8,64,128]{2,1,0:T(8,128)(2,1)} %get-tuple-element.35), calls=%async_computation.1 | async-start | bytes 262144 | tf_op jit(solution)/shard_map/all_to_all | solution.py:347
  42.9 0.7 collective-permute-start.9
  80.2 5.7 %collective-permute-start.14 = (bf16[16,3072]{1,0:T(8,128)(2,1)S(1)}, bf16[16,3072]{1,0:T(8,128)(2,1)S(1)}, u32[]{:S(2)}, u32[]{:S(2)}) collective-permute-start(bf16[16,3072]{1,0:T(8,128)(2,1)S(1)} %get-tuple-element.46), channel_id=1, source_target_pairs={{4,0},{5,1},{6,2},{7,3},{0,4},{1,5},{2,6},{3,7},{12,8},{13,9},{14,... | collective-permute-start | bytes 294920 | tf_op jit(solution)/shard_map/ppermute | solution.py:80
  80.7 8.1 %collective-permute-start.18 = (bf16[16,3072]{1,0:T(8,128)(2,1)S(1)}, bf16[16,3072]{1,0:T(8,128)(2,1)S(1)}, u32[]{:S(2)}, u32[]{:S(2)}) collective-permute-start(bf16[16,3072]{1,0:T(8,128)(2,1)S(1)} %get-tuple-element.50), channel_id=1, source_target_pairs={{12,0},{13,1},{14,2},{15,3},{8,4},{9,5},{10,6},{11,7},{4,8},{5,9},... | collective-permute-start | bytes 294920 | tf_op jit(solution)/shard_map/ppermute | solution.py:80
  83.4 5.9 %collective-permute-start.22 = (bf16[16,3072]{1,0:T(8,128)(2,1)S(1)}, bf16[16,3072]{1,0:T(8,128)(2,1)S(1)}, u32[]{:S(2)}, u32[]{:S(2)}) collective-permute-start(bf16[16,3072]{1,0:T(8,128)(2,1)S(1)} %get-tuple-element.54), channel_id=1, source_target_pairs={{12,0},{13,1},{14,2},{15,3},{8,4},{9,5},{10,6},{11,7},{4,8},{5,9},... | collective-permute-start | bytes 294920 | tf_op jit(solution)/shard_map/ppermute | solution.py:80
  83.9 5.6 %collective-permute-start.11 = (bf16[16,3072]{1,0:T(8,128)(2,1)S(1)}, bf16[16,3072]{1,0:T(8,128)(2,1)S(1)}, u32[]{:S(2)}, u32[]{:S(2)}) collective-permute-start(bf16[16,3072]{1,0:T(8,128)(2,1)S(1)} %get-tuple-element.42), channel_id=1, source_target_pairs={{4,0},{5,1},{6,2},{7,3},{0,4},{1,5},{2,6},{3,7},{12,8},{13,9},{14,... | collective-permute-start | bytes 294920 | tf_op jit(solution)/shard_map/ppermute | solution.py:80
  84.8 7.6 %collective-permute-start.13 = (bf16[16,3072]{1,0:T(8,128)(2,1)S(1)}, bf16[16,3072]{1,0:T(8,128)(2,1)S(1)}, u32[]{:S(2)}, u32[]{:S(2)}) collective-permute-start(bf16[16,3072]{1,0:T(8,128)(2,1)S(1)} %get-tuple-element.44), channel_id=1, source_target_pairs={{4,0},{5,1},{6,2},{7,3},{0,4},{1,5},{2,6},{3,7},{12,8},{13,9},{14,... | collective-permute-start | bytes 294920 | tf_op jit(solution)/shard_map/ppermute | solution.py:80
  86.0 7.8 %collective-permute-start.15 = (bf16[16,3072]{1,0:T(8,128)(2,1)S(1)}, bf16[16,3072]{1,0:T(8,128)(2,1)S(1)}, u32[]{:S(2)}, u32[]{:S(2)}) collective-permute-start(bf16[16,3072]{1,0:T(8,128)(2,1)S(1)} %shard_map.124), channel_id=1, source_target_pairs={{12,0},{13,1},{14,2},{15,3},{8,4},{9,5},{10,6},{11,7},{4,8},{5,9},... | collective-permute-start | bytes 294920 | tf_op jit(solution)/shard_map/ppermute | solution.py:80
  88.8 5.8 %collective-permute-start.17 = (bf16[16,3072]{1,0:T(8,128)(2,1)S(1)}, bf16[16,3072]{1,0:T(8,128)(2,1)S(1)}, u32[]{:S(2)}, u32[]{:S(2)}) collective-permute-start(bf16[16,3072]{1,0:T(8,128)(2,1)S(1)} %get-tuple-element.48), channel_id=1, source_target_pairs={{12,0},{13,1},{14,2},{15,3},{8,4},{9,5},{10,6},{11,7},{4,8},{5,9},... | collective-permute-start | bytes 294920 | tf_op jit(solution)/shard_map/ppermute | solution.py:80
  89.3 6.4 %collective-permute-start.19 = (bf16[16,3072]{1,0:T(8,128)(2,1)S(1)}, bf16[16,3072]{1,0:T(8,128)(2,1)S(1)}, u32[]{:S(2)}, u32[]{:S(2)}) collective-permute-start(bf16[16,3072]{1,0:T(8,128)(2,1)S(1)} %shard_map.126), channel_id=1, source_target_pairs={{4,0},{5,1},{6,2},{7,3},{0,4},{1,5},{2,6},{3,7},{12,8},{13,9},{14,... | collective-permute-start | bytes 294920 | tf_op jit(solution)/shard_map/ppermute | solution.py:80
  89.5 6.8 %collective-permute-start.21 = (bf16[16,3072]{1,0:T(8,128)(2,1)S(1)}, bf16[16,3072]{1,0:T(8,128)(2,1)S(1)}, u32[]{:S(2)}, u32[]{:S(2)}) collective-permute-start(bf16[16,3072]{1,0:T(8,128)(2,1)S(1)} %get-tuple-element.52), channel_id=1, source_target_pairs={{12,0},{13,1},{14,2},{15,3},{8,4},{9,5},{10,6},{11,7},{4,8},{5,9},... | collective-permute-start | bytes 294920 | tf_op jit(solution)/shard_map/ppermute | solution.py:80
  92.3 5.1 %collective-permute-start.23 = (bf16[16,3072]{1,0:T(8,128)(2,1)S(1)}, bf16[16,3072]{1,0:T(8,128)(2,1)S(1)}, u32[]{:S(2)}, u32[]{:S(2)}) collective-permute-start(bf16[16,3072]{1,0:T(8,128)(2,1)S(1)} %shard_map.128), channel_id=1, source_target_pairs={{4,0},{5,1},{6,2},{7,3},{0,4},{1,5},{2,6},{3,7},{12,8},{13,9},{14,... | collective-permute-start | bytes 294920 | tf_op jit(solution)/shard_map/ppermute | solution.py:80
  93.8 6.3 %collective-permute-start.10 = (bf16[16,3072]{1,0:T(8,128)(2,1)S(1)}, bf16[16,3072]{1,0:T(8,128)(2,1)S(1)}, u32[]{:S(2)}, u32[]{:S(2)}) collective-permute-start(bf16[16,3072]{1,0:T(8,128)(2,1)S(1)} %get-tuple-element.40), channel_id=1, source_target_pairs={{4,0},{5,1},{6,2},{7,3},{0,4},{1,5},{2,6},{3,7},{12,8},{13,9},{14,... | collective-permute-start | bytes 294920 | tf_op jit(solution)/shard_map/ppermute | solution.py:80
  94.6 6.8 %collective-permute-start.12 = (bf16[16,3072]{1,0:T(8,128)(2,1)S(1)}, bf16[16,3072]{1,0:T(8,128)(2,1)S(1)}, u32[]{:S(2)}, u32[]{:S(2)}) collective-permute-start(bf16[16,3072]{1,0:T(8,128)(2,1)S(1)} %shard_map.122), channel_id=1, source_target_pairs={{12,0},{13,1},{14,2},{15,3},{8,4},{9,5},{10,6},{11,7},{4,8},{5,9},... | collective-permute-start | bytes 294920 | tf_op jit(solution)/shard_map/ppermute | solution.py:80
  95.7 5.8 %collective-permute-start.16 = (bf16[16,3072]{1,0:T(8,128)(2,1)S(1)}, bf16[16,3072]{1,0:T(8,128)(2,1)S(1)}, u32[]{:S(2)}, u32[]{:S(2)}) collective-permute-start(bf16[16,3072]{1,0:T(8,128)(2,1)S(1)} %shard_map.125), channel_id=1, source_target_pairs={{1,0},{0,1},{3,2},{2,3},{5,4},{4,5},{7,6},{6,7},{9,8},{8,9},{11,10... | collective-permute-start | bytes 294920 | tf_op jit(solution)/shard_map/ppermute | solution.py:80
  96.3 5.9 %collective-permute-start.20 = (bf16[16,3072]{1,0:T(8,128)(2,1)S(1)}, bf16[16,3072]{1,0:T(8,128)(2,1)S(1)}, u32[]{:S(2)}, u32[]{:S(2)}) collective-permute-start(bf16[16,3072]{1,0:T(8,128)(2,1)S(1)} %shard_map.127), channel_id=1, source_target_pairs={{3,0},{2,1},{1,2},{0,3},{7,4},{6,5},{5,6},{4,7},{11,8},{10,9},{9,1... | collective-permute-start | bytes 294920 | tf_op jit(solution)/shard_map/ppermute | solution.py:80
  97.5 6.2 %collective-permute-start.24 = (bf16[16,3072]{1,0:T(8,128)(2,1)S(1)}, bf16[16,3072]{1,0:T(8,128)(2,1)S(1)}, u32[]{:S(2)}, u32[]{:S(2)}) collective-permute-start(bf16[16,3072]{1,0:T(8,128)(2,1)S(1)} %shard_map.129), channel_id=1, source_target_pairs={{2,0},{3,1},{0,2},{1,3},{6,4},{7,5},{4,6},{5,7},{10,8},{11,9},{8,1... | collective-permute-start | bytes 294920 | tf_op jit(solution)/shard_map/ppermute | solution.py:80
  (2 other events, 34.8 us)
